TPU v7x, 128 devices: a whole 4x4x4 slice. The times are simulated.
128 devices in a mesh: cube: 4 (over y), grid: 32 (over z, x, core).
Axes of the slice: x: 4, y: 4, z: 4, core: 2. Of those that a mesh axis runs over, the one named last changes fastest.
Arguments:
- parent_front: float32 [8192, 4, 4096], P('grid', 'cube'), as said below
- child_block: bfloat16 [4, 6144, 6144], P('cube', 'grid'), as said below
- child_panel: bfloat16 [4, 6144, 512], P('cube', 'grid'), may hold values from -0.15625 to 0.15625
- row_map: int32 [4, 6144], replicated, may hold values from 0 to 8191, as said below
Outputs:
- schur_block: float32 [8192, 4, 4096], P('grid', 'cube')
- panel_factor: float32 [8192, 4, 256], P('grid', 'cube')
Inputs may be any that keep to these rules, and one draw needn't show every extreme that they name: Each row of row_map lists 6144 distinct parent rows. Cut the 6144 entries of a row into 192 entries for each grid index, and the parent rows into blocks of 256: from one grid index at most 12 entries fall into one block, a number reached in every draw. `parent_front`: symmetric with a dominant positive diagonal. `child_block`: symmetric with a dominant positive diagonal.
All inputs are finite; a program needn't handle non-finite values.
Results may differ from a plain program's by a relative error of at most 0.0015.
Values may be sent and summed in bfloat16 or wider, within the bound.
No kernel may reach another device: no remote copies, remote signals or barrier semaphores. Data moves between devices by JAX's collectives and lax.ppermute only.
A program may use at most 128 MiB of HBM per device.

v0:
```python
import jax
import jax.numpy as jnp
from jax import lax
from jax.sharding import PartitionSpec as P

PW = 512


def swapped(block, axis, distance):
    count = lax.axis_size(axis)
    route = []
    for low in range(count):
        high = low | 1 << distance
        if high != low and high < count:
            route += [(low, high), (high, low)]
    return lax.ppermute(block, axis, route)


def spread_columns(contrib_rows, column_map, front_order):
    block_width = min(512, front_order)

    def place_block(block_number, buffer_cols):
        targets = block_number * block_width + lax.iota(jnp.int32, block_width)
        one_hot = (column_map[:, None] == targets[None, :]).astype(jnp.bfloat16)
        placed_part = jnp.dot(contrib_rows, one_hot, preferred_element_type=jnp.float32).astype(
            jnp.bfloat16
        )
        return lax.dynamic_update_slice_in_dim(
            buffer_cols, placed_part, block_number * block_width, 1
        )

    initial = jnp.zeros((contrib_rows.shape[0], front_order), jnp.bfloat16)
    return lax.fori_loop(0, front_order // block_width, place_block, initial)


def parity_columns(matrix, parity):
    paired = matrix.reshape(matrix.shape[0], matrix.shape[1] // 2, 2)
    return lax.dynamic_index_in_dim(paired, parity, 2, keepdims=False)


def pack_rows(slab_rows, local_map, owned_rows, owners, capacity):
    owner_of = local_map // owned_rows
    owner_hot = (owner_of[:, None] == lax.iota(jnp.int32, owners)[None, :]).astype(jnp.int32)
    rank_of = jnp.sum((jnp.cumsum(owner_hot, axis=0) - 1) * owner_hot, axis=1)
    slot_of = owner_of * capacity + rank_of
    selector = (lax.iota(jnp.int32, owners * capacity)[:, None] == slot_of[None, :]).astype(
        jnp.bfloat16
    )
    packed = jnp.dot(selector, slab_rows, preferred_element_type=jnp.float32).astype(jnp.bfloat16)
    return packed.reshape(owners, capacity, slab_rows.shape[1])


def placement_matrix(full_map, grid_pos, owned_rows, owners, capacity):
    mine_mask = full_map // owned_rows == grid_pos
    by_source = mine_mask.reshape(owners, -1).astype(jnp.int32)
    rank_of = jnp.cumsum(by_source, axis=1) - 1
    column_of = (lax.iota(jnp.int32, owners)[:, None] * capacity + rank_of).reshape(-1)
    local_row = full_map - grid_pos * owned_rows
    row_hot = (
        (local_row[:, None] == lax.iota(jnp.int32, owned_rows)[None, :]) & mine_mask[:, None]
    ).astype(jnp.bfloat16)
    column_hot = (column_of[:, None] == lax.iota(jnp.int32, owners * capacity)[None, :]).astype(
        jnp.bfloat16
    )
    return jnp.einsum("ir,iq->rq", row_hot, column_hot, preferred_element_type=jnp.float32).astype(
        jnp.bfloat16
    )


def place_rows(received, matrix):
    flat_rows = received.reshape(-1, received.shape[2])
    return jnp.dot(matrix, flat_rows, preferred_element_type=jnp.float32)


def shards(parent_front, child_block, child_panel, row_map):
    owners = lax.axis_size("grid")
    cube_pos = lax.axis_index("cube")
    grid_pos = lax.axis_index("grid")
    half_index = cube_pos % 2
    other_index = 1 - half_index
    partner_pos = jnp.bitwise_xor(cube_pos, 1)
    child_rows = child_block.shape[1]
    owned_rows = parent_front.shape[0]
    half_cols = parent_front.shape[2]
    front_order = 2 * half_cols
    capacity = 2 * child_rows // owners
    own_panel = child_panel[0]
    products = jnp.einsum(
        "ik,jk->ij",
        own_panel,
        lax.all_gather(child_panel, "grid", axis=1, tiled=True)[0],
        preferred_element_type=jnp.float32,
    )
    contrib_rows = (child_block[0].astype(jnp.float32) - products).astype(jnp.bfloat16)
    own_map = lax.dynamic_index_in_dim(row_map, cube_pos, 0, keepdims=False)
    partner_map = lax.dynamic_index_in_dim(row_map, partner_pos, 0, keepdims=False)
    own_local = lax.dynamic_slice_in_dim(own_map, grid_pos * child_rows, child_rows)
    partner_local = lax.dynamic_slice_in_dim(partner_map, grid_pos * child_rows, child_rows)
    spread = spread_columns(contrib_rows, own_map, front_order)
    own_half = parity_columns(spread, half_index)
    other_half = parity_columns(spread, other_index)
    partner_half = swapped(other_half, "cube", 0)
    sent_own = pack_rows(own_half, own_local, owned_rows, owners, capacity)
    sent_partner = pack_rows(partner_half, partner_local, owned_rows, owners, capacity)
    recv_own, recv_partner = (
        lax.all_to_all(sent_own, "grid", split_axis=0, concat_axis=0, tiled=True),
        lax.all_to_all(sent_partner, "grid", split_axis=0, concat_axis=0, tiled=True),
    )
    placed = place_rows(recv_own, placement_matrix(own_map, grid_pos, owned_rows, owners, capacity))
    placed = placed + place_rows(
        recv_partner, placement_matrix(partner_map, grid_pos, owned_rows, owners, capacity)
    )
    front_rows_mine = parent_front[:, 0, :] + placed
    own_panel_cols = front_rows_mine[:, : PW // 2]
    traded = swapped(own_panel_cols.astype(jnp.bfloat16), "cube", 0).astype(own_panel_cols.dtype)
    even_cols = jnp.where(half_index == 0, own_panel_cols, traded)
    odd_cols = jnp.where(half_index == 0, traded, own_panel_cols)
    panel_cols = jnp.stack([even_cols, odd_cols], axis=2).reshape(owned_rows, PW)
    global_rows = grid_pos * owned_rows + lax.iota(jnp.int32, owned_rows)
    picker = (global_rows[:, None] == lax.iota(jnp.int32, PW)[None, :]).astype(jnp.float32)
    top_rows = jnp.einsum(
        "rk,rc->kc",
        picker,
        panel_cols,
        precision=lax.Precision.HIGHEST,
        preferred_element_type=jnp.float32,
    )
    pivot_block = lax.psum(top_rows, "grid")
    lower_factor = jnp.linalg.cholesky(pivot_block)
    factor_mine = lax.linalg.triangular_solve(
        lower_factor, panel_cols, left_side=False, lower=True, transpose_a=True
    )
    update = jnp.einsum(
        "ik,jk->ij",
        factor_mine,
        lax.all_gather(factor_mine, "grid", axis=0, tiled=True),
        precision=lax.Precision.HIGHEST,
        preferred_element_type=jnp.float32,
    )
    my_update = parity_columns(update, half_index)
    schur_rows = front_rows_mine - my_update
    panel_rows = parity_columns(factor_mine, half_index)
    return (schur_rows[:, None, :], panel_rows[:, None, :])


def solution(mesh):
    in_specs = (P("grid", "cube", None), P("cube", "grid", None), P("cube", "grid", None), P())
    out_specs = (P("grid", "cube", None), P("grid", "cube", None))
    return jax.shard_map(shards, mesh=mesh, in_specs=in_specs, out_specs=out_specs, check_vma=False)
```

profile of v0, /device:TPU:1, one launch (start us, length us, event | category | flops | bytes accessed | tf_op | source)
XLA Modules:
  0.0 708.4 jit_solution(5996073163895084289)
XLA Ops:
  10.2 1.8 fusion.97
  12.1 51.1 %all-gather.3.cloned.1.call-done = bf16[1,6144,512]{2,1,0:T(8,128)(2,1)} async-done(((bf16[1,192,512]{2,1,0:T(8,128)(2,1)}), bf16[1,6144,512]{2,1,0:T(8,128)(2,1)}) %all-gather.3.cloned.1.call-update) | async-done | bytes 6291472 | tf_op jit(solution)/shard_map/all_gather | solution.py:91
  63.2 7.1 %fusion.15 = bf16[192,6144]{1,0:T(8,128)(2,1)} fusion(bf16[1,6144,512]{2,1,0:T(8,128)(2,1)} %all-gather.3.cloned.1.call-done, bf16[1,192,6144]{2,1,0:T(8,128)(2,1)} %param.7, bf16[1,192,512]{2,1,0:T(8,128)(2,1)} %param.8), kind=kOutput, calls=%fused_computation.15 | convolution fusion | flops 1211498496 | bytes 11206656 | tf_op jit(solution)/shard_map/ik,jk->ij/dot_general | solution.py:88
  70.6 62.6 %while.14 = (s32[]{:T(128)}, bf16[192,8192]{1,0:T(8,128)(2,1)S(1)}, s32[6144]{0:T(1024)S(1)}, bf16[192,6144]{1,0:T(8,128)(2,1)}, s32[]{:T(128)}, /*index=5*/s32[]{:T(128)}, s32[]{:T(128)}, s32[]{:T(128)}) while((s32[]{:T(128)}, bf16[192,8192]{1,0:T(8,128)(2,1)S(1)}, s32[6144]{0:T(1024)S(1)}, bf16[192,6144]{1,0:T(8,128)(2,1)}, s32[]{:T(128)}, ...), condition=%wide.region_6.7_spmd, body=%wide.region_5.6_spmd.sunk | while | flops 1211204096 | bytes 2584715 | solution.py:33
  70.7 3.9 fusion.128
  74.6 3.9 fusion.128
  78.5 3.9 fusion.128
  82.4 3.9 fusion.128
  86.3 3.9 fusion.128
  90.2 3.9 fusion.128
  94.2 3.9 fusion.128
  98.1 3.9 fusion.128
  102.0 3.9 fusion.128
  105.9 3.9 fusion.128
  109.8 3.9 fusion.128
  113.7 3.9 fusion.128
  117.6 3.9 fusion.128
  121.6 3.9 fusion.128
  125.5 3.9 fusion.128
  129.4 3.9 fusion.128
  133.3 3.9 copy.15
  137.1 7.5 %reshape.263 = bf16[192,4096,2]{0,2,1:T(2,128)(2,1)} reshape(bf16[192,8192]{0,1:T(8,128)(2,1)} %copy.15) | data formatting | bytes 6291456 | tf_op jit(solution)/shard_map/reshape | solution.py:37
  144.6 11.3 %constant_dynamic-slice_fusion.3 = (bf16[192,4096,1]{0,2,1:T(2,128)(2,1)}, bf16[192,4096,1]{0,2,1:T(2,128)(2,1)}) fusion(bf16[192,4096,2]{0,2,1:T(2,128)(2,1)} %reshape.263, s32[]{:T(128)S(6)} %select_n.118, s32[]{:T(128)S(6)} %select_n.111), kind=kLoop, calls=%fused_computation.189 | loop fusion | bytes 6291464 | tf_op jit(solution)/shard_map/jit(dynamic_index_in_dim)/dynamic_slice | solution.py:38
  155.9 9.6 %copy.16 = bf16[192,4096,1]{1,0,2:T(8,128)(2,1)} copy(bf16[192,4096,1]{0,2,1:T(2,128)(2,1)} %get-tuple-element.119) | data formatting | bytes 3145728 | tf_op jit(solution)/shard_map/jit(dynamic_index_in_dim)/dynamic_slice | solution.py:38
  165.5 2.4 convolution_convert_fusion.1
  167.9 2.7 reshape.264
  170.7 4.9 all-to-all-start
  175.6 9.9 %copy.21 = bf16[192,4096,1]{1,0,2:T(8,128)(2,1)S(1)} copy(bf16[192,4096,1]{0,2,1:T(2,128)(2,1)} %get-tuple-element.118) | data formatting | bytes 3145728 | tf_op jit(solution)/shard_map/jit(dynamic_index_in_dim)/dynamic_slice | solution.py:38
  187.9 33.4 %collective-permute-done = bf16[192,4096]{1,0:T(8,128)(2,1)S(1)} collective-permute-done((bf16[192,4096]{1,0:T(8,128)(2,1)S(1)}, bf16[192,4096]{1,0:T(8,128)(2,1)S(1)}, u32[]{:S(2)}, u32[]{:S(2)}) %collective-permute-start) | collective-permute-done | bytes 1572896 | tf_op jit(solution)/shard_map/ppermute | solution.py:16
  222.5 2.4 convolution_convert_fusion
  224.9 2.7 reshape.270
  227.6 8.1 %all-to-all-start.1 = ((bf16[32,12,4096]{2,1,0:T(8,128)(2,1)}), bf16[32,12,4096]{2,1,0:T(8,128)(2,1)}, u32[]{:S(2)}, u32[]{:S(2)}) async-start(bf16[32,12,4096]{2,1,0:T(8,128)(2,1)} %reshape.270), calls=%async_computation.1 | async-start | bytes 8388608 | tf_op jit(solution)/shard_map/all_to_all | solution.py:107
  238.1 4.9 fusion.33.clone.4
  243.1 4.9 fusion.30.clone.4
  248.0 4.0 reshape.265
  252.0 3.3 fusion.37
  255.2 30.7 %all-to-all-done.1 = bf16[32,12,4096]{2,1,0:T(8,128)(2,1)} async-done(((bf16[32,12,4096]{2,1,0:T(8,128)(2,1)}), bf16[32,12,4096]{2,1,0:T(8,128)(2,1)}, u32[]{:S(2)}, u32[]{:S(2)}) %all-to-all-start.1) | async-done | bytes 3145760 | tf_op jit(solution)/shard_map/all_to_all | solution.py:107
  286.0 4.0 reshape.271
  289.9 6.7 fusion.21
  296.7 2.0 copy-done
  300.0 2.6 collective-permute-done.1
  304.2 1.7 fusion.42
  306.5 105.6 %all-reduce.7.cloned.1.call-done = f32[512,512]{0,1:T(8,128)} async-done(((f32[512,512]{0,1:T(8,128)}), f32[512,512]{0,1:T(8,128)}) %all-reduce.7.cloned.1.call-update) | async-done | bytes 1048592 | tf_op jit(solution)/shard_map/psum | solution.py:128
  412.1 1.6 copy.24
  413.6 1.4 fusion.39
  415.1 11.7 %cholesky.104 = f32[128,128]{1,0:T(8,128)S(1)} custom-call(f32[128,128]{1,0:T(8,128)S(1)} %cholesky.266), custom_call_target="Cholesky" | custom-call | tf_op jit(solution)/shard_map/jit(cholesky)/cholesky | solution.py:129
  427.6 9.8 %custom-call.30 = f32[1,128,128]{1,2,0:T(8,128)S(1)} custom-call(f32[1,128,128]{2,1,0:T(8,128)S(1)} %get-tuple-element.133), custom_call_target="InvertDiagBlocksLowerTriangular" | custom-call | tf_op jit(solution)/shard_map/jit(cholesky)/cholesky | solution.py:129
  438.2 11.7 %cholesky.217 = f32[128,128]{1,0:T(8,128)S(1)} custom-call(f32[128,128]{1,0:T(8,128)S(1)} %cholesky.270), custom_call_target="Cholesky" | custom-call | tf_op jit(solution)/shard_map/jit(cholesky)/cholesky | solution.py:129
  450.6 10.0 %custom-call.31 = f32[1,128,128]{1,2,0:T(8,128)S(1)} custom-call(f32[1,128,128]{2,1,0:T(8,128)S(1)} %get-tuple-element.130), custom_call_target="InvertDiagBlocksLowerTriangular" | custom-call | tf_op jit(solution)/shard_map/jit(cholesky)/cholesky | solution.py:129
  461.2 11.7 %cholesky.238 = f32[128,128]{1,0:T(8,128)S(1)} custom-call(f32[128,128]{1,0:T(8,128)S(1)} %cholesky.275), custom_call_target="Cholesky" | custom-call | tf_op jit(solution)/shard_map/jit(cholesky)/cholesky | solution.py:129
  473.6 9.8 %custom-call.32 = f32[1,128,128]{1,2,0:T(8,128)S(1)} custom-call(f32[1,128,128]{2,1,0:T(8,128)S(1)} %get-tuple-element.127), custom_call_target="InvertDiagBlocksLowerTriangular" | custom-call | tf_op jit(solution)/shard_map/jit(cholesky)/cholesky | solution.py:129
  484.0 11.7 %cholesky.255 = f32[128,128]{1,0:T(8,128)S(1)} custom-call(f32[128,128]{1,0:T(8,128)S(1)} %convolution_subtract_fusion.6), custom_call_target="Cholesky" | custom-call | tf_op jit(solution)/shard_map/jit(cholesky)/cholesky | solution.py:129
  499.4 8.1 %while.15 = (s32[]{:T(128)}, f32[512,512]{1,0:T(8,128)S(1)}, s32[4,2]{0,1:T(2,128)S(1)}, f32[4,128,128]{2,1,0:T(8,128)S(1)}, s32[]{:T(128)}) while((s32[]{:T(128)}, f32[512,512]{1,0:T(8,128)S(1)}, s32[4,2]{0,1:T(2,128)S(1)}, f32[4,128,128]{2,1,0:T(8,128)S(1)}, s32[]{:T(128)}) %tuple.70), condition=%wide.while_cond, body=%wide.while_body.sunk | while | flops 2 | bytes 131189 | solution.py:130
  500.0 1.3 bitcast_dynamic-update-slice_fusion.2
  502.1 1.3 bitcast_dynamic-update-slice_fusion.2
  507.5 39.3 %custom-call.33 = f32[4,128,128]{1,2,0:T(8,128)S(1)} custom-call(f32[4,128,128]{2,1,0:T(8,128)S(1)} %get-tuple-element.89), custom_call_target="InvertDiagBlocksLowerTriangular" | custom-call | tf_op jit(solution)/shard_map/triangular_solve | solution.py:130
  550.0 1.3 reshape.274
  552.6 78.9 %all-gather.5.cloned.1.call-done = f32[8192,512]{0,1:T(8,128)} async-done(((f32[256,512]{0,1:T(8,128)}), f32[8192,512]{0,1:T(8,128)}) %all-gather.5.cloned.1.call-update) | async-done | bytes 16777232 | tf_op jit(solution)/shard_map/all_gather | solution.py:136
  631.5 31.6 %fusion.96 = f32[256,8192]{0,1:T(8,128)} fusion(f32[8192,512]{0,1:T(8,128)} %all-gather.5.cloned.1.call-done, f32[256,128]{0,1:T(8,128)S(1)} %fusion.67, f32[256,128]{0,1:T(8,128)S(1)} %fusion.68, f32[256,128]{0,1:T(8,128)S(1)} %fusion.69, f32[256,128]{0,1:T(8,128)S(1)} %fusion.65), kind=kOutput, calls=%fused_computation.209 | convolution fusion | flops 12885295104 | bytes 25690112 | tf_op jit(solution)/shard_map/ik,jk->ij/dot_general | solution.py:133
  663.1 10.6 %reshape.273 = f32[256,4096,2]{0,2,1:T(2,128)} reshape(f32[256,8192]{0,1:T(8,128)} %fusion.96) | data formatting | bytes 16777216 | tf_op jit(solution)/shard_map/reshape | solution.py:37
  673.7 7.1 %constant_dynamic-slice_fusion.2 = f32[256,4096,1]{0,2,1:T(1,128)} fusion(f32[256,4096,2]{0,2,1:T(2,128)} %reshape.273, s32[]{:T(128)S(6)} %select_n.111), kind=kLoop, calls=%fused_computation.187 | loop fusion | bytes 8388612 | tf_op jit(solution)/shard_map/jit(dynamic_index_in_dim)/dynamic_slice | solution.py:38
  680.8 10.4 %copy.26 = f32[256,4096,1]{1,0,2:T(8,128)} copy(f32[256,4096,1]{0,2,1:T(1,128)} %constant_dynamic-slice_fusion.2) | data formatting | bytes 8388608 | tf_op jit(solution)/shard_map/jit(dynamic_index_in_dim)/dynamic_slice | solution.py:38
  691.2 3.9 fusion.24
  695.1 6.3 copy.28
  (119 shorter events, 27.7 us)
Async XLA Ops:
  7.2 56.0 %all-gather.3.cloned.1.call-start = ((), (), s32[]{:S(2)}) async-start(), calls=%async_computation.2 | async-start | bytes 6488064 | tf_op jit(solution)/shard_map/all_gather | solution.py:91
  170.7 56.9 %all-to-all-start = ((bf16[32,12,4096]{2,1,0:T(8,128)(2,1)}), bf16[32,12,4096]{2,1,0:T(8,128)(2,1)}, u32[]{:S(2)}, u32[]{:S(2)}) async-start(bf16[32,12,4096]{2,1,0:T(8,128)(2,1)} %reshape.264), calls=%async_computation | async-start | bytes 8388608 | tf_op jit(solution)/shard_map/all_to_all | solution.py:106
  185.5 35.9 %collective-permute-start = (bf16[192,4096]{1,0:T(8,128)(2,1)S(1)}, bf16[192,4096]{1,0:T(8,128)(2,1)S(1)}, u32[]{:S(2)}, u32[]{:S(2)}) collective-permute-start(bf16[192,4096]{1,0:T(8,128)(2,1)S(1)} %bitcast.153), channel_id=1, source_target_pairs={{0,32},{32,0},{64,96},{96,64},{1,33},{33,1},{65,97},{97,65},{2,34}... | collective-permute-start | bytes 4718600 | tf_op jit(solution)/shard_map/ppermute | solution.py:16
  221.4 1.1 copy-start.1
  227.6 58.4 %all-to-all-start.1 = ((bf16[32,12,4096]{2,1,0:T(8,128)(2,1)}), bf16[32,12,4096]{2,1,0:T(8,128)(2,1)}, u32[]{:S(2)}, u32[]{:S(2)}) async-start(bf16[32,12,4096]{2,1,0:T(8,128)(2,1)} %reshape.270), calls=%async_computation.1 | async-start | bytes 8388608 | tf_op jit(solution)/shard_map/all_to_all | solution.py:107
  235.7 176.4 %all-reduce.7.cloned.1.call-start = ((), (), s32[]{:S(2)}) async-start(), calls=%async_computation.3 | async-start | bytes 2097152 | tf_op jit(solution)/shard_map/psum | solution.py:128
  296.6 2.0 copy-start
  298.7 3.9 collective-permute-start.1
  306.0 325.5 %all-gather.5.cloned.1.call-start = ((), (), s32[]{:S(2)}) async-start(), calls=%async_computation.4 | async-start | bytes 17301504 | tf_op jit(solution)/shard_map/all_gather | solution.py:136
Sparse Core Ops, SparseCore 0:
  10.3 52.8 all-gather.2
  306.1 105.9 all-reduce.6
  550.1 81.3 all-gather.4
where the time goes:
time: 719 us; the launch traced here: 708 us
  waiting for transfers between devices  303 us (42%)
  matrix products  131 us (18%)
  other arithmetic  130 us (18%)
  local copies, waits for them, and re-layouts  111 us (15%)
  between operations  17.2 us (2%)
  starting transfers between devices  16.1 us (2%)
    psum x1, waiting for transfers between devices, shards(): pivot_block = lax.psum(top_rows, 'grid')  106 us
    another operation x15, other arithmetic, shards(): lower_factor = jnp.linalg.cholesky(pivot_block)  79.3 us
    all_gather x1, waiting for transfers between devices, shards(): lax.all_gather(factor_mine, 'grid', axis=0, tiled=True)  78.9 us
    dot_general x16, matrix products, place_block(): jnp.dot(contrib_rows, one_hot, preferred_element_type=jnp.float32)  62 us
    all_gather x1, waiting for transfers between devices, shards(): lax.all_gather(child_panel, 'grid', axis=1, tiled=True)[0]  51.1 us
    dynamic_slice x7, local copies, waits for them, and re-layouts, parity_columns(): return lax.dynamic_index_in_dim(paired, parity, 2, keepdims=False)  49.6 us
    another operation x4, other arithmetic, shards(): lax.linalg.triangular_solve(lower_factor, panel_cols, left_side=False, lo...  40.5 us
    ppermute x2, waiting for transfers between devices, swapped(): return lax.ppermute(block, axis, route)  36.1 us
  transfers between devices with their start and end apart: 7, of which 6 were waited for; matrix products, arithmetic and copies ran while one was open for 6% of the time, Pallas kernels for 0%

commit v1 on v0

v1 whole, which is shorter than its diff:
```python
import functools

import jax
import jax.numpy as jnp
from jax import lax
from jax.experimental import pallas as pl
from jax.experimental.pallas import tpu as pltpu
from jax.sharding import PartitionSpec as P

PW = 512
BF = jnp.bfloat16
F32 = jnp.float32
NN = (((1,), (0,)), ((), ()))
NT = (((1,), (1,)), ((), ()))
VMEM_LIMIT = 60 << 20


def dot(a, b, dims=NN, precision=None):
    return lax.dot_general(a, b, dims, precision=precision, preferred_element_type=F32)


def hot(rows, row_vector):
    n = row_vector.shape[-1]
    rows_iota = lax.broadcasted_iota(jnp.int32, (rows, n), 0)
    return jnp.where(rows_iota == row_vector, 1.0, 0.0).astype(BF)


def eye(n, dtype=F32):
    r = lax.broadcasted_iota(jnp.int32, (n, n), 0)
    c = lax.broadcasted_iota(jnp.int32, (n, n), 1)
    return jnp.where(r == c, 1.0, 0.0).astype(dtype)


def call(kernel, out_shape, scratch=(), **kw):
    return pl.pallas_call(
        kernel,
        out_shape=out_shape,
        scratch_shapes=list(scratch),
        compiler_params=pltpu.CompilerParams(vmem_limit_bytes=VMEM_LIMIT),
        **kw,
    )


def source_kernel(owners, slots, owned, block_ref, slot_ref, target_ref, out_ref, y_ref):
    width = block_ref.shape[0]
    total = owners * slots

    def first(pair, carry):
        pick = hot(2 * total, slot_ref[pl.ds(pair, 1), :])
        cols = block_ref[:, pl.ds(pl.multiple_of(pair * 2 * width, 128), 2 * width)]
        y = dot(pick, cols, NT).astype(BF).reshape(2, owners, slots, width)
        base = pl.multiple_of(pair * 2 * slots, 16)
        y_ref[:, pl.ds(base, slots), :] = y[0]
        y_ref[:, pl.ds(base + slots, slots), :] = y[1]
        return carry

    lax.fori_loop(0, owners // 2, first, 0, unroll=2)
    unit = eye(width, BF)

    def second(owner, carry):
        pick = hot(owned, target_ref[pl.ds(owner, 1), :])
        turned = dot(pick, y_ref[owner]).astype(BF)
        out_ref[owner] = dot(unit, turned, NT).astype(BF)
        return carry

    lax.fori_loop(0, owners, second, 0, unroll=2)


def owner_kernel(owners, slots, owned, recv_ref, panel_ref, local_ref, slot_ref, target_ref, own_ref, other_ref, q_ref, y_ref):
    total = owners * slots
    q_ref[...] = jnp.zeros_like(q_ref)

    def gather(s, carry):
        q_ref[...] += dot(hot(owned, local_ref[pl.ds(s, 1), :]), panel_ref[s])
        return carry

    lax.fori_loop(0, owners, gather, 0, unroll=2)
    q = q_ref[...].astype(BF)

    def first(s, carry):
        product = dot(panel_ref[s], q, NT)
        contrib = (recv_ref[s].astype(F32) - product).astype(BF)
        y = dot(hot(total, slot_ref[pl.ds(s, 1), :]), contrib).astype(BF)
        y_ref[:, pl.ds(pl.multiple_of(s * slots, 16), slots), :] = y.reshape(owners, slots, owned)
        return carry

    lax.fori_loop(0, owners, first, 0, unroll=2)
    half = owned // 2

    def second(owner, carry):
        z = dot(hot(owned, target_ref[pl.ds(owner, 1), :]), y_ref[owner]).astype(BF)
        own_ref[owner] = z[:half]
        other_ref[owner] = z[half:]
        return carry

    lax.fori_loop(0, owners, second, 0, unroll=2)


def split(x):
    hi = x.astype(BF)
    return hi, (x - hi.astype(F32)).astype(BF)


def dot3(a, b, dims=NN):
    return dot(a[0], b[0], dims) + (dot(a[0], b[1], dims) + dot(a[1], b[0], dims))


def natural(position, parity, half):
    return jnp.where(position < half, 2 * position + parity, 2 * (position - half) + 1 - parity)


def inverse_kernel(parity_ref, a_ref, w_ref, s_ref, t_ref):
    n = a_ref.shape[0]
    half = n // 2
    parity = parity_ref[0]
    row_at = lax.broadcasted_iota(jnp.int32, (n, n), 0)
    col_at = lax.broadcasted_iota(jnp.int32, (n, n), 1)
    row_nat = natural(row_at, parity, half)
    col_nat = natural(col_at, parity, half)
    on = row_at == col_at
    phi = jnp.where(on, 0.5, jnp.where(row_nat > col_nat, 1.0, 0.0))
    unit = jnp.where(on, 1.0, 0.0)
    a = a_ref[...]
    diagonal = jnp.where(on, a, 0.0)
    scale_row = lax.rsqrt(jnp.sum(diagonal, axis=0, keepdims=True))
    scale_col = lax.rsqrt(jnp.sum(diagonal, axis=1, keepdims=True))
    scaled = a * scale_row * scale_col
    s_ref[...] = scaled
    w_ref[...] = unit - phi * (scaled - unit)
    s_parts = split(scaled)

    def step(state):
        count, _ = state
        w = w_ref[...]
        w_parts = split(w)
        m_parts = split(dot3(w_parts, s_parts))
        e = dot3(m_parts, w_parts, NT) - unit
        w_ref[...] = w - dot3(split(phi * e), w_parts)
        return count + 1, jnp.sum(e * e)

    def more(state):
        count, size = state
        return jnp.logical_and(count < 16, jnp.logical_not(size < 1e-6))

    _, size = lax.while_loop(more, step, (jnp.int32(0), jnp.float32(1.0)))

    @pl.when(jnp.logical_not(size < 1e-6))
    def _():
        lane = lax.broadcasted_iota(jnp.int32, (1, n), 1)
        lane_nat = natural(lane, parity, half)

        def place(j):
            return jnp.where((j & 1) == parity, j >> 1, half + (j >> 1))

        def column(j, carry):
            p = place(j)
            row = jnp.where(lane_nat >= j, s_ref[pl.ds(p, 1), :], 0.0)
            pivot = jnp.sum(jnp.where(lane == p, row, 0.0))
            row = row * lax.rsqrt(jnp.full((1, n), pivot))
            t_ref[pl.ds(p, 1), :] = row
            col = jnp.sum(jnp.where(on, row, 0.0), axis=1, keepdims=True)
            s_ref[...] = s_ref[...] - col * row
            return carry

        lax.fori_loop(0, n, column, 0)
        w_ref[...] = jnp.zeros_like(w_ref)

        def solve(j, carry):
            p = place(j)
            col = jnp.sum(jnp.where(col_at == p, t_ref[...], 0.0), axis=1, keepdims=True)
            known = jnp.sum(col * w_ref[...], axis=0, keepdims=True)
            pivot = jnp.sum(jnp.where(lane == p, t_ref[pl.ds(p, 1), :], 0.0))
            w_ref[pl.ds(p, 1), :] = (jnp.where(lane == p, 1.0, 0.0) - known) / pivot
            return carry

        lax.fori_loop(0, n, solve, 0)

    w_ref[...] = w_ref[...] * scale_row


def final_kernel(parent_ref, cols_ref, own_ref, recv_ref, w_ref, rows_ref, pivot_ref, schur_ref, panel_ref):
    owned = rows_ref.shape[0]
    strips = parent_ref.shape[0] // owned
    high = lax.Precision.HIGHEST
    factor = dot(rows_ref[...], w_ref[...], NT, high)
    panel_ref[...] = factor[:, : panel_ref.shape[1]]
    g = dot(factor, w_ref[...], NN, high)
    g_hi, g_lo = split(g)
    unit = eye(owned, BF)
    for chunk in range(strips // 2):
        at = pl.ds(chunk * 256, 256)
        if chunk == 0:
            update = dot(g, pivot_ref[...], NT, high)
        else:
            update = dot(g_hi, cols_ref[at, :], NT) + dot(g_lo, cols_ref[at, :], NT)
        placed = dot(unit, own_ref[at, :], NT) + dot(unit, recv_ref[at, :], NT)
        change = placed - update
        for side in range(2):
            lanes = pl.ds(2 * chunk + side, owned, stride=strips)
            schur_ref[lanes, :] = parent_ref[lanes, :] + change[:, side * 128 : side * 128 + 128]


def swap_halves(x, axis):
    a, b = jnp.split(x, 2, axis=axis)
    return jnp.concatenate([b, a], axis=axis)


def swapped(block):
    count = lax.axis_size("cube")
    return lax.ppermute(block, "cube", [(i, i ^ 1) for i in range(count)])


def shards(parent_front, child_block, child_panel, row_map):
    owners = lax.axis_size("grid")
    cube_pos = lax.axis_index("cube")
    grid_pos = lax.axis_index("grid")
    parity = cube_pos % 2
    width = child_block.shape[1]
    owned = parent_front.shape[0]
    half_cols = parent_front.shape[2]
    capacity = 2 * width // owners
    slots = -(-capacity // 16) * 16
    total = owners * slots
    half = owned // 2
    block = child_block[0]
    own_panel = child_panel[0]
    panel_all = lax.all_gather(own_panel, "grid")

    parent_pan = parent_front[:, 0, : PW // 2]
    hi = parent_pan.astype(BF)
    lo = (parent_pan - hi.astype(F32)).astype(BF)
    per = owned // owners
    scatter = jnp.concatenate([hi, lo], axis=1).reshape(owners, per, PW)
    pieces = lax.all_to_all(scatter, "grid", 0, 0, tiled=True)[:2].reshape(per, 2 * PW)

    row_of = lax.dynamic_index_in_dim(row_map, cube_pos, 0, keepdims=False).reshape(owners, width)
    owner_of = row_of // owned
    local_of = row_of % owned
    earlier = lax.iota(jnp.int32, width)[:, None] < lax.iota(jnp.int32, width)[None, :]
    same = (owner_of[:, :, None] == owner_of[:, None, :]) & earlier[None]
    rank_of = jnp.sum(same.astype(jnp.int32), axis=1)
    slot_of = owner_of * slots + rank_of
    hits = slot_of[:, :, None] == lax.iota(jnp.int32, total)[None, None, :]
    target = jnp.sum(jnp.where(hits, local_of[:, :, None] + 1, 0), axis=1) - 1
    target = target.reshape(owners, owners, slots).transpose(1, 0, 2)
    target_nat = target.reshape(owners, total)
    target_own = jnp.where(
        target_nat >= 0, ((target_nat & 1) ^ parity) * half + (target_nat >> 1), -1
    )
    pair_slot = (slot_of.reshape(owners // 2, 2, width) + jnp.array([0, total])[None, :, None]).reshape(
        owners // 2, 2 * width
    )
    my_slot = lax.dynamic_index_in_dim(slot_of, grid_pos, 0, keepdims=False)
    my_owner = lax.dynamic_index_in_dim(owner_of, grid_pos, 0, keepdims=False)
    my_rank = lax.dynamic_index_in_dim(rank_of, grid_pos, 0, keepdims=False)

    spread = call(
        functools.partial(source_kernel, owners, slots, owned),
        jax.ShapeDtypeStruct((owners, width, owned), BF),
        [pltpu.VMEM((owners, total, width), BF)],
    )(block, pair_slot, target_nat)

    pan_nat = lax.iota(jnp.int32, PW)
    pan_pos = ((pan_nat & 1) ^ parity) * (PW // 2) + (pan_nat >> 1)
    turn = (pan_pos[:, None] == lax.iota(jnp.int32, PW)[None, :]).astype(BF)
    block_pan = jnp.concatenate([spread[0], spread[1]], axis=1)
    block_pan = dot(block_pan, turn).astype(BF)
    pivot_slot = jnp.where(my_owner < 2, my_owner * capacity + my_rank, -1)
    pivot_pick = (lax.iota(jnp.int32, 2 * capacity)[:, None] == pivot_slot[None, :]).astype(BF)
    pivot_rows = dot(pivot_pick, jnp.concatenate([block_pan, own_panel], axis=1)).astype(BF)
    message = jnp.concatenate([pivot_rows, pieces], axis=0)
    message = lax.all_to_all(
        jnp.broadcast_to(message[None], (owners,) + message.shape), "grid", 0, 0, tiled=True
    )
    bulk = lax.all_to_all(spread, "grid", 0, 0, tiled=True)

    pivot_target = target[:2, :, :capacity]
    pivot_pos = jnp.where(
        pivot_target >= 0,
        ((pivot_target & 1) ^ parity) * (PW // 2)
        + lax.iota(jnp.int32, 2)[:, None, None] * half
        + (pivot_target >> 1),
        -1,
    )
    pivot_pos = pivot_pos.transpose(1, 0, 2).reshape(-1)
    pivot_hot = (lax.iota(jnp.int32, PW)[:, None] == pivot_pos[None, :]).astype(BF)
    child_part = dot(pivot_hot, message[:, : 2 * capacity].reshape(-1, 2 * PW)).astype(BF)
    panel_pan = child_part[:, PW:]
    pivot_child = (child_part[:, :PW].astype(F32) - dot(panel_pan, panel_pan, NT)).astype(BF)
    parts = message[:, 2 * capacity :].reshape(owners, 2, per, PW).transpose(1, 0, 2, 3).reshape(PW, PW)
    parts = dot(turn, parts, (((0,), (0,)), ((), ())))
    pivot_parent = parts[:, : PW // 2] + parts[:, PW // 2 :]
    pivot_mine = pivot_child.astype(F32) + jnp.pad(pivot_parent, ((0, 0), (0, PW // 2)))
    pivot_theirs = swapped(pivot_mine.astype(BF))

    contrib_pan = (block_pan.astype(F32) - dot(own_panel, panel_pan, NT)).astype(BF)
    pack = (lax.iota(jnp.int32, total)[:, None] == my_slot[None, :]).astype(BF)
    packed = dot(pack, contrib_pan).astype(BF).reshape(owners, slots, PW)
    packed = lax.all_to_all(packed, "grid", 0, 0, tiled=True).reshape(total, PW)
    my_target = lax.dynamic_index_in_dim(target_nat, grid_pos, 0, keepdims=False)
    unpack = (lax.iota(jnp.int32, owned)[:, None] == my_target[None, :]).astype(BF)
    rows_mine = dot(unpack, packed) + jnp.pad(parent_pan, ((0, 0), (0, PW // 2)))
    rows_theirs = swapped(rows_mine.astype(BF))
    rows = rows_mine + swap_halves(rows_theirs, 1).astype(F32)
    choose = (2 * lax.iota(jnp.int32, half)[:, None] + parity == lax.iota(jnp.int32, owned)[None, :]).astype(BF)
    parity_rows = dot(choose, rows.astype(BF)).astype(BF)
    front_cols = lax.all_gather(parity_rows, "grid", tiled=True)

    pivot = pivot_mine + swap_halves(swap_halves(pivot_theirs, 0), 1).astype(F32)
    pos_nat = natural(lax.iota(jnp.int32, PW), parity, PW // 2)
    pivot = jnp.where(pos_nat[:, None] >= pos_nat[None, :], pivot, pivot.T)
    vmem = pl.BlockSpec(memory_space=pltpu.VMEM)
    inverse = call(
        inverse_kernel,
        jax.ShapeDtypeStruct((PW, PW), F32),
        [pltpu.VMEM((PW, PW), F32), pltpu.VMEM((PW, PW), F32)],
        in_specs=[pl.BlockSpec(memory_space=pltpu.SMEM), vmem],
    )(parity.reshape(1).astype(jnp.int32), pivot)

    local_here = jnp.where(owner_of == grid_pos, local_of, -1)
    own_t, other_t = call(
        functools.partial(owner_kernel, owners, slots, owned),
        [jax.ShapeDtypeStruct((owners, half, owned), BF)] * 2,
        [pltpu.VMEM((owned, PW), F32), pltpu.VMEM((owners, total, owned), BF)],
    )(bulk, panel_all, local_here, slot_of, target_own)
    recv_t = swapped(other_t)

    strips = half_cols // 128
    schur, panel = call(
        final_kernel,
        [
            jax.ShapeDtypeStruct((owned * strips, 128), F32),
            jax.ShapeDtypeStruct((owned, PW // 2), F32),
        ],
    )(
        parent_front.reshape(owned * strips, 128),
        front_cols,
        own_t.reshape(half_cols, owned),
        recv_t.reshape(half_cols, owned),
        inverse,
        rows,
        pivot[: PW // 2],
    )
    return (schur.reshape(owned, 1, half_cols), panel[:, None, :])


def solution(mesh):
    in_specs = (P("grid", "cube", None), P("cube", "grid", None), P("cube", "grid", None), P())
    out_specs = (P("grid", "cube", None), P("grid", "cube", None))
    return jax.shard_map(shards, mesh=mesh, in_specs=in_specs, out_specs=out_specs, check_vma=False)
```

time: 719 us -> 294 us (0.41); the launches traced: 708 us -> 291 us
  waiting for transfers between devices: 303 us -> 132 us
  matrix products: 131 us -> 7.32 us
  other arithmetic: 130 us -> 7.04 us
  local copies, waits for them, and re-layouts: 111 us -> 19.6 us
  Pallas kernels: 0 us -> 78.7 us
  starting transfers between devices: 16.1 us -> 31.4 us
    all_gather x2, waiting for transfers between devices: 130 us -> 0.01 us  [the longest x1 0.01 us: shards(): panel_all = lax.all_gather(own_panel, 'grid')]
    another operation x37 -> x1, other arithmetic: 124 us -> 0.01 us  [the longest x15 79.3 us: shards(): lower_factor = jnp.linalg.cholesky(pivot_block)]
    dot_general x25 -> x8, matrix products: 127 us -> 7.32 us  [dot(): lax.dot_general(a, b, dims, precision=precision, preferred_element_type=F32)]
    psum x1 -> x0, waiting for transfers between devices: 106 us -> none  [shards(): pivot_block = lax.psum(top_rows, 'grid')]
    pallas_call x0 -> x4, Pallas kernels: none -> 78.7 us  [the longest x1 30.1 us: shards(): call(functools.partial(owner_kernel, owners, slots, owned), [jax.ShapeDty...]
    dynamic_slice x10 -> x4, local copies, waits for them, and re-layouts: 52.7 us -> 2.37 us  [the longest x2 2.12 us: shards(): lax.dynamic_index_in_dim(row_map, cube_pos, 0, keepdims=False)]
    all_to_all x2 -> x4, waiting for transfers between devices: 30.7 us -> 73.4 us  [the longest x1 34.5 us: shards(): bulk = lax.all_to_all(spread, 'grid', 0, 0, tiled=True)]
    reshape x8 -> x5, local copies, waits for them, and re-layouts: 33.1 us -> 2.84 us  [the longest x1 2.02 us: shards(): message[:, 2 * capacity:].reshape(owners, 2, per, PW).transpose(1, 0, 2, 3)]
  transfers between devices with their start and end apart: 7 -> 9, of which waited for: 6 -> 5; matrix products, arithmetic and copies ran while one was open for 6% -> 10% of each run, Pallas kernels for 0% -> 22%
where the time goes in v1:
time: 294 us; the launch traced here: 291 us
  waiting for transfers between devices  132 us (45%)
  Pallas kernels  78.7 us (27%)
  starting transfers between devices  31.4 us (11%)
  local copies, waits for them, and re-layouts  19.6 us (7%)
  between operations  14.4 us (5%)
  matrix products  7.32 us (2%)
  other arithmetic  7.04 us (2%)
    ppermute x3, waiting for transfers between devices, swapped(): return lax.ppermute(block, 'cube', [(i, i ^ 1) for i in range(count)])  58.3 us
    all_to_all x1, waiting for transfers between devices, shards(): bulk = lax.all_to_all(spread, 'grid', 0, 0, tiled=True)  34.5 us
    pallas_call x1, Pallas kernels, shards(): call(functools.partial(owner_kernel, owners, slots, owned), [jax.ShapeDty...  30.1 us
    all_to_all x1, waiting for transfers between devices, shards(): lax.all_to_all(jnp.broadcast_to(message[None], (owners,) + message.shape)...  27.5 us
    pallas_call x1, Pallas kernels, shards(): call(functools.partial(source_kernel, owners, slots, owned), jax.ShapeDty...  21.8 us
    pallas_call x1, Pallas kernels, shards(): call(final_kernel, [jax.ShapeDtypeStruct((owned * strips, 128), F32), jax...  15.9 us
    all_to_all x1, waiting for transfers between devices, shards(): packed = lax.all_to_all(packed, 'grid', 0, 0, tiled=True).reshape(total, PW)  11.3 us
    pallas_call x1, Pallas kernels, shards(): call(inverse_kernel, jax.ShapeDtypeStruct((PW, PW), F32), [pltpu.VMEM((PW...  10.8 us
  transfers between devices with their start and end apart: 9, of which 5 were waited for; matrix products, arithmetic and copies ran while one was open for 10% of the time, Pallas kernels for 22%

profile of v1, /device:TPU:1, one launch (start us, length us, event | category | flops | bytes accessed | tf_op | source)
XLA Modules:
  0.0 290.8 jit_solution(3402007176772203377)
XLA Ops:
  7.2 0.0 all-gather.5.cloned.1.call-start
  7.2 0.7 all-gather.5.cloned.1.call-update
  7.9 1.1 slice.39
  9.1 0.7 pad_maximum_fusion.1
  9.8 9.4 %all-to-all-start = ((bf16[32,8,512]{2,1,0:T(8,128)(2,1)}), bf16[32,8,512]{2,1,0:T(8,128)(2,1)S(1)}, u32[]{:S(2)}, u32[]{:S(2)}) async-start(bf16[32,8,512]{2,1,0:T(8,128)(2,1)} %pad_maximum_fusion.1), calls=%async_computation | async-start | bytes 524288 | tf_op jit(solution)/shard_map/all_to_all | solution.py:234
  19.3 0.5 broadcast.311
  19.8 1.6 fusion.41
  21.4 0.1 reshape.217
  21.5 1.4 convert_reduce_fusion
  22.9 0.1 reduce_sum.22
  23.0 0.6 compare_select_fusion
  23.6 2.3 select_reduce_fusion
  26.0 0.1 copy.63
  26.1 0.2 copy.64
  26.3 0.7 copy.65.target_ref
  27.1 0.1 add.166
  27.1 0.1 add.167
  27.2 0.6 fusion.32.slot_ref
  27.8 21.8 %shard_map.68 = bf16[32,192,256]{2,1,0:T(8,128)(2,1)} custom-call(bf16[192,6144]{1,0:T(8,128)(2,1)} %bitcast.56, s32[16,384]{1,0:T(8,128)} %fusion.32.slot_ref, s32[32,512]{1,0:T(8,128)} %copy.65.target_ref), custom_call_target="tpu_custom_call" | custom-call | tf_op jit(solution)/shard_map/pallas_call | solution.py:257
  49.7 1.0 slice_bitcast_fusion.1
  50.6 0.4 convolution_convert_fusion.1
  51.1 0.2 convolution_convert_fusion.3
  51.3 1.6 broadcast_in_dim.30
  53.0 7.4 %all-to-all-start.1 = ((bf16[32,32,1024]{2,1,0:T(8,128)(2,1)}), bf16[32,32,1024]{2,1,0:T(8,128)(2,1)S(1)}, u32[]{:S(2)}, u32[]{:S(2)}) async-start(bf16[32,32,1024]{2,1,0:T(8,128)(2,1)} %broadcast_in_dim.30), calls=%async_computation.1 | async-start | bytes 4194304 | tf_op jit(solution)/shard_map/all_to_all | solution.py:272
  60.4 0.1 select_bitcast_fusion
  60.4 0.1 copy.66
  60.5 0.1 eq.143
  60.7 27.5 %all-to-all-done.1 = bf16[32,32,1024]{2,1,0:T(8,128)(2,1)S(1)} async-done(((bf16[32,32,1024]{2,1,0:T(8,128)(2,1)}), bf16[32,32,1024]{2,1,0:T(8,128)(2,1)S(1)}, u32[]{:S(2)}, u32[]{:S(2)}) %all-to-all-start.1) | async-done | bytes 2097184 | tf_op jit(solution)/shard_map/all_to_all | solution.py:272
  88.2 0.1 slice.52
  88.4 2.1 fusion.1
  90.4 2.5 convolution_convert_fusion
  92.9 5.9 %all-to-all-start.2 = ((bf16[32,16,512]{2,1,0:T(8,128)(2,1)}), bf16[32,16,512]{2,1,0:T(8,128)(2,1)S(1)}, u32[]{:S(2)}, u32[]{:S(2)}) async-start(bf16[32,16,512]{2,1,0:T(8,128)(2,1)} %bitcast.15), calls=%async_computation.2 | async-start | bytes 1048576 | tf_op jit(solution)/shard_map/all_to_all | solution.py:299
  98.8 0.0 all-gather.3.cloned.1.call-start
  98.9 0.2 dynamic-slice_reduce_fusion
  99.1 11.3 %all-to-all-done.2 = bf16[32,16,512]{2,1,0:T(8,128)(2,1)S(1)} async-done(((bf16[32,16,512]{2,1,0:T(8,128)(2,1)}), bf16[32,16,512]{2,1,0:T(8,128)(2,1)S(1)}, u32[]{:S(2)}, u32[]{:S(2)}) %all-to-all-start.2) | async-done | bytes 524320 | tf_op jit(solution)/shard_map/all_to_all | solution.py:299
  110.5 0.3 fusion.44
  110.8 1.4 collective-permute-start
  112.2 6.1 %collective-permute-done = bf16[256,512]{1,0:T(8,128)(2,1)S(1)} collective-permute-done((bf16[256,512]{1,0:T(8,128)(2,1)S(1)}, bf16[256,512]{1,0:T(8,128)(2,1)S(1)}, u32[]{:S(2)}, u32[]{:S(2)}) %collective-permute-start) | collective-permute-done | bytes 262176 | tf_op jit(solution)/shard_map/ppermute | solution.py:210
  118.3 0.1 convert_add_fusion.1.rows_ref
  118.4 0.8 copy-done.3
  119.2 0.9 convolution_convert_fusion.2
  120.1 0.0 all-gather.3.cloned.1.call-update
  120.1 5.2 %all-to-all-start.3 = ((bf16[32,192,256]{2,1,0:T(8,128)(2,1)}), bf16[32,192,256]{2,1,0:T(8,128)(2,1)S(1)}, u32[]{:S(2)}, u32[]{:S(2)}) async-start(bf16[32,192,256]{2,1,0:T(8,128)(2,1)} %shard_map.68), calls=%async_computation.3 | async-start | bytes 6291456 | tf_op jit(solution)/shard_map/all_to_all | solution.py:275
  125.3 0.6 add_select_fusion.target_ref
  125.9 1.9 slice.55
  127.9 2.0 reshape.227
  129.9 1.9 copy.73
  131.8 34.5 %all-to-all-done.3.recv_ref = bf16[32,192,256]{2,1,0:T(8,128)(2,1)S(1)} async-done(((bf16[32,192,256]{2,1,0:T(8,128)(2,1)}), bf16[32,192,256]{2,1,0:T(8,128)(2,1)S(1)}, u32[]{:S(2)}, u32[]{:S(2)}) %all-to-all-start.3) | async-done | bytes 3145760 | tf_op jit(solution)/shard_map/all_to_all | solution.py:275
  166.3 1.7 copy-done
  167.9 30.1 %shard_map.69 = (bf16[32,128,256]{2,1,0:T(8,128)(2,1)}, bf16[32,128,256]{2,1,0:T(8,128)(2,1)}) custom-call(bf16[32,192,256]{2,1,0:T(8,128)(2,1)} %copy-done, bf16[32,192,512]{2,1,0:T(8,128)(2,1)} %all-gather.5.cloned.1.call-done.panel_ref, s32[32,192]{1,0:T(8,128)} %get-tuple-element.28.local_ref, s32[32,192]{1,0:T(8,128)} %copy-done.6, ...), custom_call_target="tpu_custom_call" | custom-call | tf_op jit(solution)/shard_map/pallas_call | solution.py:321
  198.1 1.3 collective-permute-start.1
  199.3 0.5 fusion.7
  199.9 0.1 slice_add_fusion
  200.0 0.5 fusion.45
  200.5 0.8 collective-permute-start.2
  201.3 52.1 %collective-permute-done.2 = bf16[512,512]{0,1:T(8,128)(2,1)S(1)} collective-permute-done((bf16[512,512]{0,1:T(8,128)(2,1)S(1)}, bf16[512,512]{0,1:T(8,128)(2,1)S(1)}, u32[]{:S(2)}, u32[]{:S(2)}) %collective-permute-start.2) | collective-permute-done | bytes 524320 | tf_op jit(solution)/shard_map/ppermute | solution.py:210
  253.5 0.2 convert_add_fusion
  253.7 0.3 copy.76
  254.0 0.2 bitcast_select_fusion.a_ref
  254.2 0.9 slice.58.pivot_ref
  255.1 0.3 copy-done.2
  255.3 10.8 %shard_map.70.w_ref = f32[512,512]{1,0:T(8,128)} custom-call(s32[1]{0:T(128)} %bitcast.20.parity_ref, f32[512,512]{1,0:T(8,128)} %copy-done.2), custom_call_target="tpu_custom_call" | custom-call | tf_op jit(solution)/shard_map/pallas_call | solution.py:313
  266.1 15.9 %shard_map.71 = (f32[8192,128]{1,0:T(8,128)}, f32[256,256]{1,0:T(8,128)}) custom-call(f32[8192,128]{1,0:T(8,128)} %bitcast.53, bf16[4096,512]{1,0:T(8,128)(2,1)} %all-gather.3.cloned.1.call-done.cols_ref, bf16[4096,256]{1,0:T(8,128)(2,1)} %bitcast.57, bf16[4096,256]{1,0:T(8,128)(2,1)} %bitcast.19.recv_ref, f32[512,512]{1,0:T(8,128)} %shard_map.70.w_ref, ...), custom_call_target="tpu_custom_call" | custom-call | tf_op jit(solution)/shard_map/pallas_call | solution.py:329
  282.1 1.9 copy.78
  (43 shorter events, 0.3 us)
Async XLA Ops:
  7.2 159.1 %all-gather.5.cloned.1.call-start = ((), (), s32[]{:S(2)}) async-start(), calls=%async_computation.5 | async-start | bytes 6488064 | tf_op jit(solution)/shard_map/all_gather | solution.py:227
  9.8 41.5 %all-to-all-start = ((bf16[32,8,512]{2,1,0:T(8,128)(2,1)}), bf16[32,8,512]{2,1,0:T(8,128)(2,1)S(1)}, u32[]{:S(2)}, u32[]{:S(2)}) async-start(bf16[32,8,512]{2,1,0:T(8,128)(2,1)} %pad_maximum_fusion.1), calls=%async_computation | async-start | bytes 524288 | tf_op jit(solution)/shard_map/all_to_all | solution.py:234
  23.6 37.0 %copy-start.6 = (s32[32,192]{1,0:T(8,128)}, s32[32,192]{1,0:T(8,128)S(1)}, u32[]{:S(2)}) copy-start(s32[32,192]{1,0:T(8,128)S(1)} %get-tuple-element.29.slot_ref) | copy-start | bytes 73732
  27.8 23.3 %copy-start.8 = (bf16[1,192,512]{2,1,0:T(8,128)(2,1)S(1)}, bf16[1,192,512]{2,1,0:T(8,128)(2,1)}, u32[]{:S(2)}) copy-start(bf16[1,192,512]{2,1,0:T(8,128)(2,1)} %param.7) | copy-start | bytes 589828
  51.1 1.9 copy-start.9
  53.0 35.2 %all-to-all-start.1 = ((bf16[32,32,1024]{2,1,0:T(8,128)(2,1)}), bf16[32,32,1024]{2,1,0:T(8,128)(2,1)S(1)}, u32[]{:S(2)}, u32[]{:S(2)}) async-start(bf16[32,32,1024]{2,1,0:T(8,128)(2,1)} %broadcast_in_dim.30), calls=%async_computation.1 | async-start | bytes 4194304 | tf_op jit(solution)/shard_map/all_to_all | solution.py:272
  88.2 2.2 copy-start.1
  88.3 2.1 copy-start.10
  92.9 17.6 %all-to-all-start.2 = ((bf16[32,16,512]{2,1,0:T(8,128)(2,1)}), bf16[32,16,512]{2,1,0:T(8,128)(2,1)S(1)}, u32[]{:S(2)}, u32[]{:S(2)}) async-start(bf16[32,16,512]{2,1,0:T(8,128)(2,1)} %bitcast.15), calls=%async_computation.2 | async-start | bytes 1048576 | tf_op jit(solution)/shard_map/all_to_all | solution.py:299
  98.8 167.3 %all-gather.3.cloned.1.call-start = ((), (), s32[]{:S(2)}) async-start(), calls=%async_computation.4 | async-start | bytes 4325376 | tf_op jit(solution)/shard_map/all_gather | solution.py:307
  110.8 7.5 %collective-permute-start = (bf16[256,512]{1,0:T(8,128)(2,1)S(1)}, bf16[256,512]{1,0:T(8,128)(2,1)S(1)}, u32[]{:S(2)}, u32[]{:S(2)}) collective-permute-start(bf16[256,512]{1,0:T(8,128)(2,1)S(1)} %get-tuple-element.31), channel_id=1, source_target_pairs={{0,32},{32,0},{64,96},{96,64},{1,33},{33,1},{65,97},{97,65},{2,34}... | collective-permute-start | bytes 786440 | tf_op jit(solution)/shard_map/ppermute | solution.py:210
  118.4 0.8 copy-start.3
  120.1 5.2 %copy-start.5 = (s32[32,512]{1,0:T(8,128)S(1)}, s32[32,512]{1,0:T(8,128)}, u32[]{:S(2)}) copy-start(s32[32,512]{1,0:T(8,128)} %copy.65.target_ref) | copy-start | bytes 196612
  120.1 46.1 %all-to-all-start.3 = ((bf16[32,192,256]{2,1,0:T(8,128)(2,1)}), bf16[32,192,256]{2,1,0:T(8,128)(2,1)S(1)}, u32[]{:S(2)}, u32[]{:S(2)}) async-start(bf16[32,192,256]{2,1,0:T(8,128)(2,1)} %shard_map.68), calls=%async_computation.3 | async-start | bytes 6291456 | tf_op jit(solution)/shard_map/all_to_all | solution.py:275
  166.3 1.7 copy-start
  167.9 31.4 %copy-start.4 = (bf16[2,32,8,512]{3,2,1,0:T(8,128)(2,1)S(1)}, bf16[2,32,8,512]{3,2,1,0:T(8,128)(2,1)}, u32[]{:S(2)}) copy-start(bf16[2,32,8,512]{3,2,1,0:T(8,128)(2,1)} %copy.73) | copy-start | bytes 1572868
  198.1 1.9 copy-start.7
  198.1 68.1 %collective-permute-start.1 = (bf16[32,128,256]{2,1,0:T(8,128)(2,1)}, bf16[32,128,256]{2,1,0:T(8,128)(2,1)}, u32[]{:S(2)}, u32[]{:S(2)}) collective-permute-start(bf16[32,128,256]{2,1,0:T(8,128)(2,1)} %get-tuple-element.7), channel_id=1, source_target_pairs={{0,32},{32,0},{64,96},{96,64},{1,33},{33,1},{65,97},{97,65},{2,34}... | collective-permute-start | bytes 6291464 | tf_op jit(solution)/shard_map/ppermute | solution.py:210
  200.5 53.0 %collective-permute-start.2 = (bf16[512,512]{0,1:T(8,128)(2,1)S(1)}, bf16[512,512]{0,1:T(8,128)(2,1)S(1)}, u32[]{:S(2)}, u32[]{:S(2)}) collective-permute-start(bf16[512,512]{0,1:T(8,128)(2,1)S(1)} %get-tuple-element.33), channel_id=1, source_target_pairs={{0,32},{32,0},{64,96},{96,64},{1,33},{33,1},{65,97},{97,65},{2,34}... | collective-permute-start | bytes 1572872 | tf_op jit(solution)/shard_map/ppermute | solution.py:210
  254.2 1.1 copy-start.2
Sparse Core Ops, SparseCore 0:
  10.2 52.8 all-gather.4
  120.2 69.0 all-gather.2

commit v2 on v1

v2 whole, which is shorter than its diff:
```python
import functools

import jax
import jax.numpy as jnp
from jax import lax
from jax.experimental import pallas as pl
from jax.experimental.pallas import tpu as pltpu
from jax.sharding import PartitionSpec as P

PW = 512
CHUNKS = 2
LOW_ROWS = 16
BF = jnp.bfloat16
F32 = jnp.float32
NN = (((1,), (0,)), ((), ()))
NT = (((1,), (1,)), ((), ()))
VMEM_LIMIT = 60 << 20


def dot(a, b, dims=NN, precision=None):
    return lax.dot_general(a, b, dims, precision=precision, preferred_element_type=F32)


def row_numbers(rows, n):
    return lax.broadcasted_iota(jnp.int32, (rows, n), 0).astype(F32).astype(BF)


def hot(numbers, row_vector):
    one, zero = jnp.ones((), BF), jnp.zeros((), BF)
    return jnp.where(numbers == row_vector.astype(BF), one, zero)


def eye(n, dtype=F32):
    r = lax.broadcasted_iota(jnp.int32, (n, n), 0)
    c = lax.broadcasted_iota(jnp.int32, (n, n), 1)
    return jnp.where(r == c, 1.0, 0.0).astype(dtype)


def call(kernel, out_shape, scratch=(), **kw):
    return pl.pallas_call(
        kernel,
        out_shape=out_shape,
        scratch_shapes=list(scratch),
        compiler_params=pltpu.CompilerParams(vmem_limit_bytes=VMEM_LIMIT),
        **kw,
    )


def source_kernel(owners, slots, owned, block_ref, slot_ref, target_ref, pan_target_ref, *refs):
    outs, pan_ref, y_ref = refs[:CHUNKS], refs[CHUNKS], refs[CHUNKS + 1]
    width = block_ref.shape[0]
    part = owners * slots // 2
    numbers = row_numbers(part, width)

    def first(pair, carry):
        cols = block_ref[:, pl.ds(pl.multiple_of(pair * 2 * width, 128), 2 * width)]
        for side in range(2):
            s = pair * 2 + side
            mine = cols[:, side * width : (side + 1) * width]
            for b in range(2):
                pick = hot(numbers, slot_ref[b, pl.ds(s, 1), :])
                y = dot(pick, mine, NT).astype(BF).reshape(owners // 2, slots, width)
                y_ref[pl.ds(b * (owners // 2), owners // 2), pl.ds(pl.multiple_of(s * slots, 16), slots), :] = y
        return carry

    lax.fori_loop(0, owners // 2, first, 0, unroll=2)
    unit = eye(width, BF)
    spots = row_numbers(owned, owners * slots)
    lanes = owned // CHUNKS

    def place(targets, owner):
        turned = dot(hot(spots, targets), y_ref[owner]).astype(BF)
        return dot(unit, turned, NT).astype(BF)

    half = owned // 2
    for b in range(2):
        z = place(pan_target_ref[pl.ds(b, 1), :], b)
        pan_ref[:, b * half : (b + 1) * half] = z[:, :half]
        pan_ref[:, owned + b * half : owned + (b + 1) * half] = z[:, half:]

    def second(owner, carry):
        z = place(target_ref[pl.ds(owner, 1), :], owner)
        for c in range(CHUNKS):
            outs[c][owner] = z[:, c * lanes : (c + 1) * lanes]
        return carry

    lax.fori_loop(0, owners, second, 0, unroll=2)


def owner_kernel(owners, slots, owned, recv_ref, panel_ref, local_ref, slot_ref, target_ref, own_ref, other_ref, q_ref, y_ref):
    width, lanes = panel_ref.shape[1], recv_ref.shape[2]
    part = owners * slots // 2
    q_ref[...] = jnp.zeros_like(q_ref)
    here = row_numbers(lanes, width)

    def gather(s, carry):
        q_ref[...] += dot(hot(here, local_ref[pl.ds(s, 1), :]), panel_ref[s])
        return carry

    lax.fori_loop(0, owners, gather, 0, unroll=4)
    q = q_ref[...].astype(BF)
    numbers = row_numbers(part, width)

    def first(s, carry):
        product = dot(panel_ref[s], q, NT)
        contrib = (recv_ref[s, :width].astype(F32) - product).astype(BF)
        for b in range(2):
            y = dot(hot(numbers, slot_ref[b, pl.ds(s, 1), :]), contrib).astype(BF)
            y_ref[pl.ds(b * (owners // 2), owners // 2), pl.ds(pl.multiple_of(s * slots, 16), slots), :] = y.reshape(
                owners // 2, slots, lanes
            )
        return carry

    lax.fori_loop(0, owners, first, 0, unroll=4)
    half = owned // 2
    spots = row_numbers(owned, owners * slots)

    def second(owner, carry):
        z = dot(hot(spots, target_ref[pl.ds(owner, 1), :]), y_ref[owner]).astype(BF)
        own_ref[owner] = z[:half]
        other_ref[owner] = z[half:]
        return carry

    lax.fori_loop(0, owners, second, 0, unroll=4)


def split(x):
    hi = x.astype(BF)
    return hi, (x - hi.astype(F32)).astype(BF)


def dot3(a, b, dims=NN):
    return dot(a[0], b[0], dims) + (dot(a[0], b[1], dims) + dot(a[1], b[0], dims))


def natural(position, parity, half):
    return jnp.where(position < half, 2 * position + parity, 2 * (position - half) + 1 - parity)


def inverse_factor(parity, a, w_ref, s_ref, t_ref):
    n = a.shape[0]
    half = n // 2
    row_at = lax.broadcasted_iota(jnp.int32, (n, n), 0)
    col_at = lax.broadcasted_iota(jnp.int32, (n, n), 1)
    row_nat = natural(row_at, parity, half)
    col_nat = natural(col_at, parity, half)
    on = row_at == col_at
    a = jnp.where(row_nat >= col_nat, a, a.T)
    phi = jnp.where(on, 0.5, jnp.where(row_nat > col_nat, 1.0, 0.0))
    unit = jnp.where(on, 1.0, 0.0)
    diagonal = jnp.where(on, a, 0.0)
    scale_row = lax.rsqrt(jnp.sum(diagonal, axis=0, keepdims=True))
    scale_col = lax.rsqrt(jnp.sum(diagonal, axis=1, keepdims=True))
    scaled = a * scale_row * scale_col
    s_ref[...] = scaled
    w_ref[...] = unit - phi * (scaled - unit)
    s_parts = split(scaled)

    def step(state):
        count, _ = state
        w = w_ref[...]
        w_parts = split(w)
        m_parts = split(dot3(w_parts, s_parts))
        e = dot3(m_parts, w_parts, NT) - unit
        w_ref[...] = w - dot3(split(phi * e), w_parts)
        return count + 1, jnp.sum(e * e)

    def more(state):
        count, size = state
        return jnp.logical_and(count < 16, jnp.logical_not(size < 1e-6))

    _, size = lax.while_loop(more, step, (jnp.int32(0), jnp.float32(1.0)))

    @pl.when(jnp.logical_not(size < 1e-6))
    def _():
        lane = lax.broadcasted_iota(jnp.int32, (1, n), 1)
        lane_nat = natural(lane, parity, half)

        def place(j):
            return jnp.where((j & 1) == parity, j >> 1, half + (j >> 1))

        def column(j, carry):
            p = place(j)
            row = jnp.where(lane_nat >= j, s_ref[pl.ds(p, 1), :], 0.0)
            pivot = jnp.sum(jnp.where(lane == p, row, 0.0))
            row = row * lax.rsqrt(jnp.full((1, n), pivot))
            t_ref[pl.ds(p, 1), :] = row
            col = jnp.sum(jnp.where(on, row, 0.0), axis=1, keepdims=True)
            s_ref[...] = s_ref[...] - col * row
            return carry

        lax.fori_loop(0, n, column, 0)
        w_ref[...] = jnp.zeros_like(w_ref)

        def solve(j, carry):
            p = place(j)
            col = jnp.sum(jnp.where(col_at == p, t_ref[...], 0.0), axis=1, keepdims=True)
            known = jnp.sum(col * w_ref[...], axis=0, keepdims=True)
            pivot = jnp.sum(jnp.where(lane == p, t_ref[pl.ds(p, 1), :], 0.0))
            w_ref[pl.ds(p, 1), :] = (jnp.where(lane == p, 1.0, 0.0) - known) / pivot
            return carry

        lax.fori_loop(0, n, solve, 0)

    return w_ref[...] * scale_row


def final_kernel(parity_ref, rows_ref, front_hbm, parent_hbm, *refs):
    own_hbm, recv_hbm = refs[:CHUNKS], refs[CHUNKS : 2 * CHUNKS]
    schur_ref, panel_ref, w_ref, s_ref, t_ref, lead_ref, cols_ref, parent_ref = refs[2 * CHUNKS : 2 * CHUNKS + 8]
    own_ref, recv_ref, sems = refs[2 * CHUNKS + 8 :]
    owned = rows_ref.shape[0]
    half = owned // 2
    strips = parent_ref.shape[0] // owned
    high = lax.Precision.HIGHEST
    copies = [
        pltpu.make_async_copy(front_hbm.at[pl.ds(0, 2)], lead_ref, sems.at[0]),
        pltpu.make_async_copy(front_hbm.at[:, pl.ds(0, half), :], cols_ref, sems.at[1]),
        pltpu.make_async_copy(parent_hbm, parent_ref, sems.at[2]),
    ]
    for c in range(CHUNKS):
        copies.append(pltpu.make_async_copy(own_hbm[c], own_ref.at[c], sems.at[3 + 2 * c]))
        copies.append(pltpu.make_async_copy(recv_hbm[c], recv_ref.at[c], sems.at[4 + 2 * c]))
    for copy in copies:
        copy.start()
    copies[0].wait()
    pieces = [(0, 0), (1, 0), (0, half), (1, half)]
    pivot = jnp.concatenate([lead_ref[b, i : i + half] for b, i in pieces], axis=0).astype(F32)
    low = jnp.concatenate([lead_ref[b, owned : owned + 1, i : i + half] for b, i in pieces], axis=1).astype(F32)
    pivot = pivot + eye(PW) * low
    lead_cols = split(pivot[: PW // 2])
    w = inverse_factor(parity_ref[0], pivot, w_ref, s_ref, t_ref)
    w_ref[...] = w
    factor = dot(rows_ref[...], w, NT, high)
    panel_ref[...] = factor[:, : panel_ref.shape[1]]
    g_hi, g_lo = split(dot(factor, w_ref[...], NN, high))
    for copy in copies[1:]:
        copy.wait()
    lanes = owned // CHUNKS
    unit = eye(lanes, BF)
    for pair in range(strips // 2):
        cols = cols_ref[pl.ds(2 * pair, 2)].reshape(2 * half, PW)
        if pair == 0:
            update = dot3((g_hi, g_lo), lead_cols, NT)
        else:
            update = dot(g_hi, cols, NT) + dot(g_lo, cols, NT)
        placed = []
        for c in range(CHUNKS):
            own = own_ref[c, pl.ds(2 * pair, 2)].reshape(2 * half, lanes)
            recv = recv_ref[c, pl.ds(2 * pair, 2)].reshape(2 * half, lanes)
            placed.append(dot(unit, own, NT) + dot(unit, recv, NT))
        change = jnp.concatenate(placed, axis=0) - update
        for side in range(2):
            at = pl.ds(2 * pair + side, owned, stride=strips)
            schur_ref[at, :] = parent_ref[at, :] + change[:, side * half : (side + 1) * half]


def swap_halves(x, axis):
    a, b = jnp.split(x, 2, axis=axis)
    return jnp.concatenate([b, a], axis=axis)


def swapped(block):
    count = lax.axis_size("cube")
    return lax.ppermute(block, "cube", [(i, i ^ 1) for i in range(count)])


def natural_position(row, parity):
    return ((row & 1) ^ parity) * (PW // 2) + (row >> 1) + jnp.where(row < PW, 0, PW)


def low_message(low):
    return jnp.pad(low.astype(BF)[None, :], ((0, LOW_ROWS - 1), (0, PW - low.shape[0])))


def exchanged(block):
    return lax.all_to_all(block, "grid", 0, 0, tiled=True)


def shards(parent_front, child_block, child_panel, row_map):
    owners = lax.axis_size("grid")
    cube_pos = lax.axis_index("cube")
    grid_pos = lax.axis_index("grid")
    parity = cube_pos % 2
    width = child_block.shape[1]
    owned = parent_front.shape[0]
    half_cols = parent_front.shape[2]
    capacity = 2 * width // owners
    slots = -(-capacity // 16) * 16
    total = owners * slots
    half = owned // 2
    lanes = owned // CHUNKS
    own_panel = child_panel[0]
    panel_all = lax.all_gather(own_panel, "grid")

    row_of = lax.dynamic_index_in_dim(row_map, cube_pos, 0, keepdims=False).reshape(owners, width)
    owner_of = row_of // owned
    local_of = row_of % owned
    earlier = lax.iota(jnp.int32, width)[:, None] < lax.iota(jnp.int32, width)[None, :]
    same = (owner_of[:, :, None] == owner_of[:, None, :]) & earlier[None]
    rank_of = jnp.sum(same.astype(jnp.int32), axis=1)
    slot_of = owner_of * slots + rank_of
    hits = slot_of[:, :, None] == lax.iota(jnp.int32, total)[None, None, :]
    target = jnp.sum(jnp.where(hits, local_of[:, :, None] + 1, 0), axis=1) - 1
    target = target.reshape(owners, owners, slots).transpose(1, 0, 2)
    target_nat = target.reshape(owners, total)
    target_own = jnp.where(
        target_nat >= 0, ((target_nat & 1) ^ parity) * half + (target_nat >> 1), -1
    ).astype(F32)
    slot_parts = slot_of[None] - jnp.array([0, total // 2])[:, None, None]
    slot_parts = jnp.where((slot_parts >= 0) & (slot_parts < total // 2), slot_parts, -1).astype(F32)
    my_slot = lax.dynamic_index_in_dim(slot_of, grid_pos, 0, keepdims=False)
    my_owner = lax.dynamic_index_in_dim(owner_of, grid_pos, 0, keepdims=False)
    my_rank = lax.dynamic_index_in_dim(rank_of, grid_pos, 0, keepdims=False)

    pivot_slot = jnp.where(my_owner < 2, my_owner * capacity + my_rank, -1)
    pivot_pick = (lax.iota(jnp.int32, 2 * capacity)[:, None] == pivot_slot[None, :]).astype(BF)
    pivot_rows = dot(pivot_pick, own_panel).astype(BF)
    pivot_rows = exchanged(jnp.broadcast_to(pivot_rows[None], (owners,) + pivot_rows.shape))

    outs = call(
        functools.partial(source_kernel, owners, slots, owned),
        [jax.ShapeDtypeStruct((owners, width, lanes), BF)] * CHUNKS + [jax.ShapeDtypeStruct((width, PW), BF)],
        [pltpu.VMEM((owners, total, width), BF)],
    )(child_block[0], slot_parts, target_nat.astype(F32), target_own)
    spread, block_pan = outs[:CHUNKS], outs[CHUNKS]
    pivot_target = target[:2, :, :capacity]
    pivot_pos = jnp.where(
        pivot_target >= 0,
        ((pivot_target & 1) ^ parity) * (PW // 2)
        + lax.iota(jnp.int32, 2)[:, None, None] * half
        + (pivot_target >> 1),
        -1,
    )
    pivot_pos = pivot_pos.transpose(1, 0, 2).reshape(-1)
    pivot_hot = (lax.iota(jnp.int32, PW)[:, None] == pivot_pos[None, :]).astype(BF)
    panel_pan = dot(pivot_hot, pivot_rows.reshape(-1, PW)).astype(BF)

    contrib_pan = (block_pan.astype(F32) - dot(own_panel, panel_pan, NT)).astype(BF)
    pack = (lax.iota(jnp.int32, total)[:, None] == my_slot[None, :]).astype(BF)
    packed = dot(pack, contrib_pan).astype(BF).reshape(owners, slots, PW)
    packed = [packed[:, :, i : i + lanes] for i in range(0, PW, lanes)]
    bulk_first = exchanged(jnp.concatenate([spread[0]] + packed, axis=1))
    bulk = [bulk_first] + [exchanged(part) for part in spread[1:]]
    packed = [bulk_first[:, width + i * slots : width + (i + 1) * slots] for i in range(PW // lanes)]
    packed = jnp.concatenate(packed, axis=2).reshape(total, PW)
    my_target = lax.dynamic_index_in_dim(target_nat, grid_pos, 0, keepdims=False)
    unpack = (lax.iota(jnp.int32, owned)[:, None] == my_target[None, :]).astype(BF)
    rows_mine = dot(unpack, packed) + jnp.pad(parent_front[:, 0, : PW // 2], ((0, 0), (0, PW // 2)))
    row_pos = natural_position(grid_pos * owned + lax.iota(jnp.int32, owned), parity)
    diagonal = row_pos[:, None] == lax.iota(jnp.int32, PW)[None, :]

    def rounded(x):
        return lax.reduce_precision(x, 8, 7)

    low_mine = jnp.sum(jnp.where(diagonal, rows_mine - rounded(rows_mine), 0.0), axis=1)
    rows_theirs = swapped(jnp.concatenate([rows_mine.astype(BF), low_message(low_mine)], axis=0))
    low_theirs = rows_theirs[owned, :owned].astype(F32)[:, None]
    rows = rows_mine + swap_halves(rows_theirs[:owned], 1).astype(F32)
    rows = rows + jnp.where(diagonal & (row_pos >= PW // 2)[:, None], low_theirs, 0.0)
    low_rows = jnp.sum(jnp.where(diagonal, rows - rounded(rows), 0.0), axis=1)
    local_order = natural(lax.iota(jnp.int32, owned), parity, half)
    choose = local_order[:, None] == lax.iota(jnp.int32, owned)[None, :]
    low_rows = jnp.sum(jnp.where(choose, low_rows[None, :], 0.0), axis=1)
    front_cols = dot(choose.astype(BF), rows.astype(BF)).astype(BF)
    front_cols = lax.all_gather(jnp.concatenate([front_cols, low_message(low_rows)], axis=0), "grid")

    local_here = jnp.where(owner_of == grid_pos, local_of, -1)
    own_t, other_t = [], []
    for c in range(CHUNKS):
        local_part = local_here - c * lanes
        local_part = jnp.where((local_here >= 0) & (local_part >= 0) & (local_part < lanes), local_part, -1)
        a, b = call(
            functools.partial(owner_kernel, owners, slots, owned),
            [jax.ShapeDtypeStruct((owners, half, lanes), BF)] * 2,
            [pltpu.VMEM((lanes, PW), F32), pltpu.VMEM((owners, total, lanes), BF)],
        )(bulk[c], panel_all, local_part.astype(F32), slot_parts, target_own)
        own_t.append(a)
        other_t.append(b)
    recv_t = [swapped(x) for x in other_t]

    strips = half_cols // 128
    anywhere = pl.BlockSpec(memory_space=pl.ANY)
    vmem = pl.BlockSpec(memory_space=pltpu.VMEM)
    schur, panel = call(
        final_kernel,
        [
            jax.ShapeDtypeStruct((owned * strips, 128), F32),
            jax.ShapeDtypeStruct((owned, PW // 2), F32),
        ],
        [
            pltpu.VMEM((PW, PW), F32),
            pltpu.VMEM((PW, PW), F32),
            pltpu.VMEM((PW, PW), F32),
            pltpu.VMEM((2, owned + LOW_ROWS, PW), BF),
            pltpu.VMEM((owners, half, PW), BF),
            pltpu.VMEM((owned * strips, 128), F32),
            pltpu.VMEM((CHUNKS, owners, half, lanes), BF),
            pltpu.VMEM((CHUNKS, owners, half, lanes), BF),
            pltpu.SemaphoreType.DMA((3 + 2 * CHUNKS,)),
        ],
        in_specs=[pl.BlockSpec(memory_space=pltpu.SMEM), vmem] + [anywhere] * (2 + 2 * CHUNKS),
        out_specs=[vmem, vmem],
    )(
        parity.reshape(1).astype(jnp.int32),
        rows,
        front_cols,
        parent_front.reshape(owned * strips, 128),
        *own_t,
        *recv_t,
    )
    return (schur.reshape(owned, 1, half_cols), panel[:, None, :])


def solution(mesh):
    in_specs = (P("grid", "cube", None), P("cube", "grid", None), P("cube", "grid", None), P())
    out_specs = (P("grid", "cube", None), P("grid", "cube", None))
    return jax.shard_map(shards, mesh=mesh, in_specs=in_specs, out_specs=out_specs, check_vma=False)
```

time: 294 us -> 207 us (0.70)
  waiting for transfers between devices: 132 us -> 59.7 us
  local copies, waits for them, and re-layouts: 19.6 us -> 12.6 us
  matrix products: 7.32 us -> 2.9 us
    all_to_all x4 -> x3, waiting for transfers between devices: 73.4 us -> 32.8 us  [exchanged(): return lax.all_to_all(block, 'grid', 0, 0, tiled=True)]
    ppermute x3, waiting for transfers between devices: 58.3 us -> 26.2 us  [swapped(): return lax.ppermute(block, 'cube', [(i, i ^ 1) for i in range(count)])]
    pallas_call x2 -> x1, Pallas kernels: 32.6 us -> 20.1 us  [shards(): call(functools.partial(source_kernel, owners, slots, owned), [jax.ShapeDt...]
    pallas_call x1 -> x2, Pallas kernels: 30.1 us -> 36.5 us  [shards(): call(functools.partial(owner_kernel, owners, slots, owned), [jax.ShapeDty...]
    pallas_call x1, Pallas kernels: 15.9 us -> 22 us  [shards(): call(final_kernel, [jax.ShapeDtypeStruct((owned * strips, 128), F32), jax...]
    unnamed x25 -> x22, local copies, waits for them, and re-layouts: 4.71 us -> 9.87 us
    dot_general x8 -> x5, matrix products: 7.32 us -> 2.9 us  [dot(): lax.dot_general(a, b, dims, precision=precision, preferred_element_type=F32)]
    slice x5 -> x3, local copies, waits for them, and re-layouts: 4.09 us -> 0.04 us  [the longest x1 0.03 us: shards(): bulk_first[:, width + i * slots:width + (i + 1) * slots]]
  transfers between devices with their start and end apart: 9 -> 8, of which waited for: 5 -> 4; matrix products, arithmetic and copies ran while one was open for 10% -> 9% of each run, Pallas kernels for 22% -> 27%
where the time goes in v2:
time: 207 us; the launch traced here: 206 us
  Pallas kernels  78.5 us (38%)
  waiting for transfers between devices  59.7 us (29%)
  starting transfers between devices  30.4 us (15%)
  between operations  14.3 us (7%)
  local copies, waits for them, and re-layouts  12.6 us (6%)
  other arithmetic  7.34 us (4%)
  matrix products  2.9 us (1%)
    pallas_call x2, Pallas kernels, shards(): call(functools.partial(owner_kernel, owners, slots, owned), [jax.ShapeDty...  36.5 us
    all_to_all x3, waiting for transfers between devices, exchanged(): return lax.all_to_all(block, 'grid', 0, 0, tiled=True)  32.8 us
    ppermute x3, waiting for transfers between devices, swapped(): return lax.ppermute(block, 'cube', [(i, i ^ 1) for i in range(count)])  26.2 us
    all_to_all x3, starting transfers between devices, exchanged(): return lax.all_to_all(block, 'grid', 0, 0, tiled=True)  25.8 us
    pallas_call x1, Pallas kernels, shards(): call(final_kernel, [jax.ShapeDtypeStruct((owned * strips, 128), F32), jax...  22 us
    pallas_call x1, Pallas kernels, shards(): call(functools.partial(source_kernel, owners, slots, owned), [jax.ShapeDt...  20.1 us
    unnamed x22, local copies, waits for them, and re-layouts  9.87 us
    ppermute x3, starting transfers between devices, swapped(): return lax.ppermute(block, 'cube', [(i, i ^ 1) for i in range(count)])  4.58 us
  transfers between devices with their start and end apart: 8, of which 4 were waited for; matrix products, arithmetic and copies ran while one was open for 9% of the time, Pallas kernels for 27%

profile of v2, /device:TPU:1, one launch (start us, length us, event | category | flops | bytes accessed | tf_op | source)
XLA Modules:
  0.0 205.8 jit_solution(15470040785733331402)
XLA Ops:
  7.2 0.0 copy-start
  7.2 0.0 all-gather.4.cloned.1.call-start
  7.2 0.7 all-gather.4.cloned.1.call-update
  7.9 0.1 copy-done
  8.1 0.1 dynamic-slice_reduce_fusion.1
  8.1 0.1 reshape.230
  8.3 1.4 convert_reduce_fusion
  9.7 1.1 convolution_convert_fusion.2
  10.8 0.9 broadcast_in_dim.104
  11.7 9.4 %all-to-all-start = ((bf16[32,24,512]{2,1,0:T(8,128)(2,1)}), bf16[32,24,512]{2,1,0:T(8,128)(2,1)S(1)}, u32[]{:S(2)}, u32[]{:S(2)}) async-start(bf16[32,24,512]{2,1,0:T(8,128)(2,1)} %broadcast_in_dim.104), calls=%async_computation | async-start | bytes 1572864 | tf_op jit(solution)/shard_map/all_to_all | solution.py:277
  21.2 0.7 select_convert_fusion.1
  21.8 2.3 %select_reduce_fusion = s32[32,512]{1,0:T(8,128)S(1)} fusion(s32[32,192]{1,0:T(8,128)S(1)} %get-tuple-element.44, s32[32,192]{1,0:T(8,128)S(1)} %get-tuple-element.43), kind=kLoop, calls=%fused_computation | loop fusion | flops 9420800 | bytes 114688 | tf_op jit(solution)/shard_map/reduce_sum | solution.py:304
  24.2 0.1 copy.41
  24.3 0.1 select_bitcast_fusion
  24.4 0.2 copy.42
  24.6 0.1 copy.43
  24.7 0.1 copy.47
  24.8 0.1 eq.137
  24.9 0.7 fusion.23.slot_ref
  25.7 0.7 select_convert_fusion
  26.3 20.1 %shard_map.68 = (bf16[32,192,128]{2,1,0:T(8,128)(2,1)}, bf16[32,192,128]{2,1,0:T(8,128)(2,1)}, bf16[192,512]{1,0:T(8,128)(2,1)}) custom-call(bf16[192,6144]{1,0:T(8,128)(2,1)} %bitcast.39, f32[2,32,192]{2,1,0:T(8,128)} %fusion.23.slot_ref, f32[32,512]{1,0:T(8,128)} %get-tuple-element.41.target_ref, f32[32,512]{1,0:T(8,128)} %get-tuple-element.40.pan_target_ref.target_ref), custom_call_target="tpu_custom_call" | custom-call | tf_op jit(solution)/shard_map/pallas_call | solution.py:321
  46.4 0.0 copy-start.6
  46.4 0.0 copy-start.7
  46.4 2.9 %constant_dynamic-update-slice_fusion = bf16[32,256,128]{2,1,0:T(8,128)(2,1)} fusion(bf16[32,192,128]{2,1,0:T(8,128)(2,1)} %get-tuple-element.11), kind=kLoop, calls=%fused_computation.72 | loop fusion | bytes 3145728
  49.3 0.0 all-to-all-done
  49.3 0.0 copy-done.6
  49.3 0.0 copy-done.7
  49.3 0.8 fusion.5
  50.1 0.3 convolution_convert_fusion
  50.4 0.7 slice_dynamic-update-slice_fusion.3
  51.1 0.7 slice_dynamic-update-slice_fusion.2
  51.8 0.7 slice_dynamic-update-slice_fusion.1
  52.5 0.7 slice_dynamic-update-slice_fusion
  53.1 7.5 %all-to-all-start.1 = ((bf16[32,256,128]{2,1,0:T(8,128)(2,1)}), bf16[32,256,128]{2,1,0:T(8,128)(2,1)S(1)}, u32[]{:S(2)}, u32[]{:S(2)}) async-start(bf16[32,256,128]{2,1,0:T(8,128)(2,1)} %slice_dynamic-update-slice_fusion), calls=%async_computation.1 | async-start | bytes 4194304 | tf_op jit(solution)/shard_map/all_to_all | solution.py:277
  60.7 0.0 all-gather.6.cloned.1.call-start
  60.7 0.0 slice-done
  60.8 0.2 dynamic-slice_reduce_fusion
  61.0 26.6 %all-to-all-done.1.recv_ref = bf16[32,256,128]{2,1,0:T(8,128)(2,1)S(1)} async-done(((bf16[32,256,128]{2,1,0:T(8,128)(2,1)}), bf16[32,256,128]{2,1,0:T(8,128)(2,1)S(1)}, u32[]{:S(2)}, u32[]{:S(2)}) %all-to-all-start.1) | async-done | bytes 2097184 | tf_op jit(solution)/shard_map/all_to_all | solution.py:277
  87.6 0.0 copy-start.1
  87.6 0.1 pad_maximum_fusion
  87.7 0.4 fusion.31
  88.2 0.7 copy-done.1
  88.9 1.7 collective-permute-start
  90.6 4.2 %collective-permute-done = bf16[272,512]{1,0:T(8,128)(2,1)S(1)} collective-permute-done((bf16[272,512]{1,0:T(8,128)(2,1)S(1)}, bf16[272,512]{1,0:T(8,128)(2,1)S(1)}, u32[]{:S(2)}, u32[]{:S(2)}) %collective-permute-start) | collective-permute-done | bytes 278560 | tf_op jit(solution)/shard_map/ppermute | solution.py:265
  94.8 0.4 fusion.13
  95.2 0.2 select_reduce_fusion.1
  95.4 0.3 convolution_convert_fusion.1
  95.7 0.7 fusion.16
  96.4 0.0 all-gather.6.cloned.1.call-update
  96.4 0.0 copy-done.3
  96.5 8.8 %all-to-all-start.2 = ((bf16[32,192,128]{2,1,0:T(8,128)(2,1)}), bf16[32,192,128]{2,1,0:T(8,128)(2,1)S(1)}, u32[]{:S(2)}, u32[]{:S(2)}) async-start(bf16[32,192,128]{2,1,0:T(8,128)(2,1)} %get-tuple-element.14), calls=%async_computation.2 | async-start | bytes 3145728 | tf_op jit(solution)/shard_map/all_to_all | solution.py:277
  105.3 0.0 all-gather.4.cloned.1.call-done.panel_ref
  105.3 18.3 %shard_map.69 = (bf16[32,128,128]{2,1,0:T(8,128)(2,1)}, bf16[32,128,128]{2,1,0:T(8,128)(2,1)}) custom-call(bf16[32,256,128]{2,1,0:T(8,128)(2,1)} %copy-done.1, bf16[32,192,512]{2,1,0:T(8,128)(2,1)} %all-gather.4.cloned.1.call-done.panel_ref, f32[32,192]{1,0:T(8,128)} %get-tuple-element.45.local_ref, f32[2,32,192]{2,1,0:T(8,128)} %fusion.23.slot_ref, ...), custom_call_target="tpu_custom_call" | custom-call | tf_op jit(solution)/shard_map/pallas_call | solution.py:373
  123.7 1.5 collective-permute-start.1
  125.1 6.3 %all-to-all-done.2.recv_ref = bf16[32,192,128]{2,1,0:T(8,128)(2,1)S(1)} async-done(((bf16[32,192,128]{2,1,0:T(8,128)(2,1)}), bf16[32,192,128]{2,1,0:T(8,128)(2,1)S(1)}, u32[]{:S(2)}, u32[]{:S(2)}) %all-to-all-start.2) | async-done | bytes 1572896 | tf_op jit(solution)/shard_map/all_to_all | solution.py:277
  131.4 1.1 copy-done.2
  132.5 18.1 %shard_map.70 = (bf16[32,128,128]{2,1,0:T(8,128)(2,1)}, bf16[32,128,128]{2,1,0:T(8,128)(2,1)}) custom-call(bf16[32,192,128]{2,1,0:T(8,128)(2,1)} %copy-done.2, bf16[32,192,512]{2,1,0:T(8,128)(2,1)} %all-gather.4.cloned.1.call-done.panel_ref, f32[32,192]{1,0:T(8,128)} %get-tuple-element.42.local_ref, f32[2,32,192]{2,1,0:T(8,128)} %fusion.23.slot_ref, ...), custom_call_target="tpu_custom_call" | custom-call | tf_op jit(solution)/shard_map/pallas_call | solution.py:373
  150.6 1.5 collective-permute-start.2
  152.1 0.0 collective-permute-done.1.refs_2_
  152.1 21.9 %collective-permute-done.2.refs_3_ = bf16[32,128,128]{2,1,0:T(8,128)(2,1)S(1)} collective-permute-done((bf16[32,128,128]{2,1,0:T(8,128)(2,1)}, bf16[32,128,128]{2,1,0:T(8,128)(2,1)S(1)}, u32[]{:S(2)}, u32[]{:S(2)}) %collective-permute-start.2) | collective-permute-done | bytes 1048608 | tf_op jit(solution)/shard_map/ppermute | solution.py:265
  174.1 0.0 copy-done.4
  174.1 1.0 copy-done.5
  175.0 22.0 %shard_map.71 = (f32[8192,128]{1,0:T(8,128)}, f32[256,256]{1,0:T(8,128)}) custom-call(s32[1]{0:T(128)} %bitcast.parity_ref, f32[256,512]{1,0:T(8,128)} %copy-done.3, bf16[32,272,512]{2,1,0:T(8,128)(2,1)} %bitcast.35, f32[8192,128]{1,0:T(8,128)} %bitcast.36, bf16[32,128,128]{2,1,0:T(8,128)(2,1)} %get-tuple-element.13.refs_0_, ...), custom_call_target="tpu_custom_call" | custom-call | tf_op jit(solution)/shard_map/pallas_call | solution.py:385
  197.0 1.9 copy.50
  (22 shorter events, 0.2 us)
Async XLA Ops:
  7.2 0.9 copy-start
  7.2 98.1 %all-gather.4.cloned.1.call-start = ((), (), s32[]{:S(2)}) async-start(), calls=%async_computation.3 | async-start | bytes 6488064 | tf_op jit(solution)/shard_map/all_gather | solution.py:294
  11.7 37.5 %all-to-all-start = ((bf16[32,24,512]{2,1,0:T(8,128)(2,1)}), bf16[32,24,512]{2,1,0:T(8,128)(2,1)S(1)}, u32[]{:S(2)}, u32[]{:S(2)}) async-start(bf16[32,24,512]{2,1,0:T(8,128)(2,1)} %broadcast_in_dim.104), calls=%async_computation | async-start | bytes 1572864 | tf_op jit(solution)/shard_map/all_to_all | solution.py:277
  46.4 2.9 %copy-start.6 = (bf16[1,192,512]{2,1,0:T(8,128)(2,1)S(1)}, bf16[1,192,512]{2,1,0:T(8,128)(2,1)}, u32[]{:S(2)}) copy-start(bf16[1,192,512]{2,1,0:T(8,128)(2,1)} %param.7) | copy-start | bytes 589828
  46.4 2.9 %copy-start.7 = (bf16[192,512]{1,0:T(8,128)(2,1)S(1)}, bf16[192,512]{1,0:T(8,128)(2,1)}, u32[]{:S(2)}) copy-start(bf16[192,512]{1,0:T(8,128)(2,1)} %get-tuple-element.12) | copy-start | bytes 589828
  53.1 7.6 %slice-start = ((f32[256,1,4096]{2,1,0:T(1,128)}), f32[256,1,256]{2,1,0:T(1,128)S(1)}, s32[]{:S(2)}) async-start(f32[256,1,4096]{2,1,0:T(1,128)} %param.5), calls=%async_computation.5 | async-start | bytes 524288 | tf_op jit(solution)/shard_map/slice | solution.py:349
  53.1 34.4 %all-to-all-start.1 = ((bf16[32,256,128]{2,1,0:T(8,128)(2,1)}), bf16[32,256,128]{2,1,0:T(8,128)(2,1)S(1)}, u32[]{:S(2)}, u32[]{:S(2)}) async-start(bf16[32,256,128]{2,1,0:T(8,128)(2,1)} %slice_dynamic-update-slice_fusion), calls=%async_computation.1 | async-start | bytes 4194304 | tf_op jit(solution)/shard_map/all_to_all | solution.py:277
  60.7 113.4 %all-gather.6.cloned.1.call-start = ((), (), s32[]{:S(2)}) async-start(), calls=%async_computation.4 | async-start | bytes 9191424 | tf_op jit(solution)/shard_map/all_gather | solution.py:366
  87.6 1.3 copy-start.1
  88.9 5.9 %collective-permute-start = (bf16[272,512]{1,0:T(8,128)(2,1)S(1)}, bf16[272,512]{1,0:T(8,128)(2,1)S(1)}, u32[]{:S(2)}, u32[]{:S(2)}) collective-permute-start(bf16[272,512]{1,0:T(8,128)(2,1)S(1)} %fusion.15), channel_id=1, source_target_pairs={{0,32},{32,0},{64,96},{96,64},{1,33},{33,1},{65,97},{97,65},{2,34}... | collective-permute-start | bytes 835592 | tf_op jit(solution)/shard_map/ppermute | solution.py:265
  95.2 1.2 copy-start.3
  96.5 34.9 %all-to-all-start.2 = ((bf16[32,192,128]{2,1,0:T(8,128)(2,1)}), bf16[32,192,128]{2,1,0:T(8,128)(2,1)S(1)}, u32[]{:S(2)}, u32[]{:S(2)}) async-start(bf16[32,192,128]{2,1,0:T(8,128)(2,1)} %get-tuple-element.14), calls=%async_computation.2 | async-start | bytes 3145728 | tf_op jit(solution)/shard_map/all_to_all | solution.py:277
  123.7 28.4 %collective-permute-start.1 = (bf16[32,128,128]{2,1,0:T(8,128)(2,1)}, bf16[32,128,128]{2,1,0:T(8,128)(2,1)S(1)}, u32[]{:S(2)}, u32[]{:S(2)}) collective-permute-start(bf16[32,128,128]{2,1,0:T(8,128)(2,1)} %get-tuple-element.16), channel_id=1, source_target_pairs={{0,32},{32,0},{64,96},{96,64},{1,33},{33,1},{65,97},{97,65},{2,34}... | collective-permute-start | bytes 3145736 | tf_op jit(solution)/shard_map/ppermute | solution.py:265
  131.4 1.1 copy-start.2
  150.6 23.4 %collective-permute-start.2 = (bf16[32,128,128]{2,1,0:T(8,128)(2,1)}, bf16[32,128,128]{2,1,0:T(8,128)(2,1)S(1)}, u32[]{:S(2)}, u32[]{:S(2)}) collective-permute-start(bf16[32,128,128]{2,1,0:T(8,128)(2,1)} %get-tuple-element.17), channel_id=1, source_target_pairs={{0,32},{32,0},{64,96},{96,64},{1,33},{33,1},{65,97},{97,65},{2,34}... | collective-permute-start | bytes 3145736 | tf_op jit(solution)/shard_map/ppermute | solution.py:265
  152.1 21.9 %copy-start.4 = (bf16[32,128,128]{2,1,0:T(8,128)(2,1)}, bf16[32,128,128]{2,1,0:T(8,128)(2,1)S(1)}, u32[]{:S(2)}) copy-start(bf16[32,128,128]{2,1,0:T(8,128)(2,1)S(1)} %collective-permute-done.1.refs_2_) | copy-start | bytes 3145732
  174.0 1.0 copy-start.5
Sparse Core Ops, SparseCore 0:
  10.3 60.4 all-gather.3
  96.6 67.6 all-gather.5

commit v3 on v2

--- a/solution.py
+++ b/solution.py
@@ -10,6 +10,8 @@
 PW = 512
 CHUNKS = 2
 LOW_ROWS = 16
+SOURCE_UNROLL = 4
+OWNER_UNROLL = 8
 BF = jnp.bfloat16
 F32 = jnp.float32
 NN = (((1,), (0,)), ((), ()))
@@ -36,18 +38,20 @@
     return jnp.where(r == c, 1.0, 0.0).astype(dtype)
 
 
-def call(kernel, out_shape, scratch=(), **kw):
+def call(kernel, out_shape, scratch=(), flops=0, **kw):
+    moved = sum(x.size * x.dtype.itemsize for x in jax.tree.leaves(out_shape))
     return pl.pallas_call(
         kernel,
         out_shape=out_shape,
         scratch_shapes=list(scratch),
+        cost_estimate=pl.CostEstimate(flops=flops, transcendentals=0, bytes_accessed=2 * moved),
         compiler_params=pltpu.CompilerParams(vmem_limit_bytes=VMEM_LIMIT),
         **kw,
     )
 
 
-def source_kernel(owners, slots, owned, block_ref, slot_ref, target_ref, pan_target_ref, *refs):
-    outs, pan_ref, y_ref = refs[:CHUNKS], refs[CHUNKS], refs[CHUNKS + 1]
+def source_kernel(owners, slots, owned, block_ref, slot_ref, target_ref, *refs):
+    outs, y_ref = refs[:CHUNKS], refs[CHUNKS]
     width = block_ref.shape[0]
     part = owners * slots // 2
     numbers = row_numbers(part, width)
@@ -63,35 +67,28 @@
                 y_ref[pl.ds(b * (owners // 2), owners // 2), pl.ds(pl.multiple_of(s * slots, 16), slots), :] = y
         return carry
 
-    lax.fori_loop(0, owners // 2, first, 0, unroll=2)
+    lax.fori_loop(0, owners // 2, first, 0, unroll=SOURCE_UNROLL)
     unit = eye(width, BF)
     spots = row_numbers(owned, owners * slots)
     lanes = owned // CHUNKS
 
-    def place(targets, owner):
-        turned = dot(hot(spots, targets), y_ref[owner]).astype(BF)
-        return dot(unit, turned, NT).astype(BF)
-
-    half = owned // 2
-    for b in range(2):
-        z = place(pan_target_ref[pl.ds(b, 1), :], b)
-        pan_ref[:, b * half : (b + 1) * half] = z[:, :half]
-        pan_ref[:, owned + b * half : owned + (b + 1) * half] = z[:, half:]
-
     def second(owner, carry):
-        z = place(target_ref[pl.ds(owner, 1), :], owner)
+        turned = dot(hot(spots, target_ref[pl.ds(owner, 1), :]), y_ref[owner]).astype(BF)
+        z = dot(unit, turned, NT).astype(BF)
         for c in range(CHUNKS):
             outs[c][owner] = z[:, c * lanes : (c + 1) * lanes]
         return carry
 
-    lax.fori_loop(0, owners, second, 0, unroll=2)
-
-
-def owner_kernel(owners, slots, owned, recv_ref, panel_ref, local_ref, slot_ref, target_ref, own_ref, other_ref, q_ref, y_ref):
-    width, lanes = panel_ref.shape[1], recv_ref.shape[2]
-    part = owners * slots // 2
+    lax.fori_loop(0, owners, second, 0, unroll=2 * SOURCE_UNROLL)
+
+
+def product_kernel(panel_ref, local_ref, *refs):
+    outs, q_ref = refs[:CHUNKS], refs[CHUNKS]
+    owners, width = panel_ref.shape[:2]
+    owned = q_ref.shape[0]
+    lanes = owned // CHUNKS
+    here = row_numbers(owned, width)
     q_ref[...] = jnp.zeros_like(q_ref)
-    here = row_numbers(lanes, width)
 
     def gather(s, carry):
         q_ref[...] += dot(hot(here, local_ref[pl.ds(s, 1), :]), panel_ref[s])
@@ -99,11 +96,23 @@
 
     lax.fori_loop(0, owners, gather, 0, unroll=4)
     q = q_ref[...].astype(BF)
-    numbers = row_numbers(part, width)
 
     def first(s, carry):
         product = dot(panel_ref[s], q, NT)
-        contrib = (recv_ref[s, :width].astype(F32) - product).astype(BF)
+        for c in range(CHUNKS):
+            outs[c][s] = product[:, c * lanes : (c + 1) * lanes]
+        return carry
+
+    lax.fori_loop(0, owners, first, 0, unroll=4)
+
+
+def owner_kernel(owners, slots, owned, recv_ref, product_ref, slot_ref, target_ref, own_ref, other_ref, y_ref):
+    width, lanes = recv_ref.shape[1:]
+    part = owners * slots // 2
+    numbers = row_numbers(part, width)
+
+    def first(s, carry):
+        contrib = (recv_ref[s].astype(F32) - product_ref[s]).astype(BF)
         for b in range(2):
             y = dot(hot(numbers, slot_ref[b, pl.ds(s, 1), :]), contrib).astype(BF)
             y_ref[pl.ds(b * (owners // 2), owners // 2), pl.ds(pl.multiple_of(s * slots, 16), slots), :] = y.reshape(
@@ -111,7 +120,7 @@
             )
         return carry
 
-    lax.fori_loop(0, owners, first, 0, unroll=4)
+    lax.fori_loop(0, owners, first, 0, unroll=OWNER_UNROLL)
     half = owned // 2
     spots = row_numbers(owned, owners * slots)
 
@@ -121,7 +130,7 @@
         other_ref[owner] = z[half:]
         return carry
 
-    lax.fori_loop(0, owners, second, 0, unroll=4)
+    lax.fori_loop(0, owners, second, 0, unroll=OWNER_UNROLL)
 
 
 def split(x):
@@ -205,10 +214,10 @@
     return w_ref[...] * scale_row
 
 
-def final_kernel(parity_ref, rows_ref, front_hbm, parent_hbm, *refs):
-    own_hbm, recv_hbm = refs[:CHUNKS], refs[CHUNKS : 2 * CHUNKS]
-    schur_ref, panel_ref, w_ref, s_ref, t_ref, lead_ref, cols_ref, parent_ref = refs[2 * CHUNKS : 2 * CHUNKS + 8]
-    own_ref, recv_ref, sems = refs[2 * CHUNKS + 8 :]
+def factor_kernel(parity_ref, rows_ref, front_hbm, parent_hbm, *refs):
+    own_hbm, recv_hbm = refs[:CHUNKS], refs[CHUNKS : 2 * CHUNKS - 1]
+    schur_ref, panel_ref, w_ref, s_ref, t_ref, lead_ref, cols_ref, parent_ref = refs[2 * CHUNKS - 1 : 2 * CHUNKS + 7]
+    own_ref, recv_ref, sems = refs[2 * CHUNKS + 7 :]
     owned = rows_ref.shape[0]
     half = owned // 2
     strips = parent_ref.shape[0] // owned
@@ -219,8 +228,9 @@
         pltpu.make_async_copy(parent_hbm, parent_ref, sems.at[2]),
     ]
     for c in range(CHUNKS):
-        copies.append(pltpu.make_async_copy(own_hbm[c], own_ref.at[c], sems.at[3 + 2 * c]))
-        copies.append(pltpu.make_async_copy(recv_hbm[c], recv_ref.at[c], sems.at[4 + 2 * c]))
+        copies.append(pltpu.make_async_copy(own_hbm[c], own_ref.at[c], sems.at[3 + c]))
+    for c in range(CHUNKS - 1):
+        copies.append(pltpu.make_async_copy(recv_hbm[c], recv_ref.at[c], sems.at[3 + CHUNKS + c]))
     for copy in copies:
         copy.start()
     copies[0].wait()
@@ -246,13 +256,29 @@
             update = dot(g_hi, cols, NT) + dot(g_lo, cols, NT)
         placed = []
         for c in range(CHUNKS):
-            own = own_ref[c, pl.ds(2 * pair, 2)].reshape(2 * half, lanes)
-            recv = recv_ref[c, pl.ds(2 * pair, 2)].reshape(2 * half, lanes)
-            placed.append(dot(unit, own, NT) + dot(unit, recv, NT))
+            z = dot(unit, own_ref[c, pl.ds(2 * pair, 2)].reshape(2 * half, lanes), NT)
+            if c < CHUNKS - 1:
+                z = z + dot(unit, recv_ref[c, pl.ds(2 * pair, 2)].reshape(2 * half, lanes), NT)
+            placed.append(z)
         change = jnp.concatenate(placed, axis=0) - update
         for side in range(2):
             at = pl.ds(2 * pair + side, owned, stride=strips)
             schur_ref[at, :] = parent_ref[at, :] + change[:, side * half : (side + 1) * half]
+
+
+def last_kernel(schur_ref, recv_ref, out_ref):
+    rows = pl.program_id(0)
+    lanes = recv_ref.shape[2]
+    strips = recv_ref.shape[0]
+    part = schur_ref.shape[0] // strips
+    r = lax.broadcasted_iota(jnp.int32, (part, lanes), 0) + rows * part
+    c = lax.broadcasted_iota(jnp.int32, (part, lanes), 1)
+    unit = jnp.where(r == c, 1.0, 0.0).astype(BF)
+    for pair in range(strips // 2):
+        z = dot(unit, recv_ref[pl.ds(2 * pair, 2)].reshape(-1, lanes), NT)
+        for side in range(2):
+            at = pl.ds(2 * pair + side, part, stride=strips)
+            out_ref[at, :] = schur_ref[at, :] + z[:, side * 128 : (side + 1) * 128]
 
 
 def swap_halves(x, axis):
@@ -318,12 +344,10 @@
     pivot_rows = dot(pivot_pick, own_panel).astype(BF)
     pivot_rows = exchanged(jnp.broadcast_to(pivot_rows[None], (owners,) + pivot_rows.shape))
 
-    outs = call(
-        functools.partial(source_kernel, owners, slots, owned),
-        [jax.ShapeDtypeStruct((owners, width, lanes), BF)] * CHUNKS + [jax.ShapeDtypeStruct((width, PW), BF)],
-        [pltpu.VMEM((owners, total, width), BF)],
-    )(child_block[0], slot_parts, target_nat.astype(F32), target_own)
-    spread, block_pan = outs[:CHUNKS], outs[CHUNKS]
+    row_flat = row_of.reshape(-1)
+    pan_of = jnp.where(row_flat < PW, ((row_flat & 1) ^ parity) * (PW // 2) + (row_flat >> 1), -1)
+    block_pan = dot(child_block[0], (pan_of[:, None] == lax.iota(jnp.int32, PW)[None, :]).astype(BF)).astype(BF)
+
     pivot_target = target[:2, :, :capacity]
     pivot_pos = jnp.where(
         pivot_target >= 0,
@@ -339,11 +363,16 @@
     contrib_pan = (block_pan.astype(F32) - dot(own_panel, panel_pan, NT)).astype(BF)
     pack = (lax.iota(jnp.int32, total)[:, None] == my_slot[None, :]).astype(BF)
     packed = dot(pack, contrib_pan).astype(BF).reshape(owners, slots, PW)
-    packed = [packed[:, :, i : i + lanes] for i in range(0, PW, lanes)]
-    bulk_first = exchanged(jnp.concatenate([spread[0]] + packed, axis=1))
-    bulk = [bulk_first] + [exchanged(part) for part in spread[1:]]
-    packed = [bulk_first[:, width + i * slots : width + (i + 1) * slots] for i in range(PW // lanes)]
-    packed = jnp.concatenate(packed, axis=2).reshape(total, PW)
+    packed, slot_parts = lax.optimization_barrier((packed, slot_parts))
+    packed = exchanged(packed)
+    spread = call(
+        functools.partial(source_kernel, owners, slots, owned),
+        [jax.ShapeDtypeStruct((owners, width, lanes), BF)] * CHUNKS,
+        [pltpu.VMEM((owners, total, width), BF)],
+        flops=6 * owners * total * width * width,
+    )(child_block[0], slot_parts, target_nat.astype(F32))
+    packed, spread = lax.optimization_barrier((packed, spread))
+    packed = packed.reshape(total, PW)
     my_target = lax.dynamic_index_in_dim(target_nat, grid_pos, 0, keepdims=False)
     unpack = (lax.iota(jnp.int32, owned)[:, None] == my_target[None, :]).astype(BF)
     rows_mine = dot(unpack, packed) + jnp.pad(parent_front[:, 0, : PW // 2], ((0, 0), (0, PW // 2)))
@@ -365,16 +394,24 @@
     front_cols = dot(choose.astype(BF), rows.astype(BF)).astype(BF)
     front_cols = lax.all_gather(jnp.concatenate([front_cols, low_message(low_rows)], axis=0), "grid")
 
-    local_here = jnp.where(owner_of == grid_pos, local_of, -1)
+    bulk = [exchanged(spread[0])]
+    local_here = jnp.where(owner_of == grid_pos, local_of, -1).astype(F32)
+    product = call(
+        product_kernel,
+        [jax.ShapeDtypeStruct((owners, width, lanes), F32)] * CHUNKS,
+        [pltpu.VMEM((owned, PW), F32)],
+        flops=4 * owners * width * owned * PW,
+    )(panel_all, local_here)
+    rest, product = lax.optimization_barrier((spread[1:], product))
+    bulk = bulk + [exchanged(part) for part in rest]
     own_t, other_t = [], []
     for c in range(CHUNKS):
-        local_part = local_here - c * lanes
-        local_part = jnp.where((local_here >= 0) & (local_part >= 0) & (local_part < lanes), local_part, -1)
         a, b = call(
             functools.partial(owner_kernel, owners, slots, owned),
             [jax.ShapeDtypeStruct((owners, half, lanes), BF)] * 2,
-            [pltpu.VMEM((lanes, PW), F32), pltpu.VMEM((owners, total, lanes), BF)],
-        )(bulk[c], panel_all, local_part.astype(F32), slot_parts, target_own)
+            [pltpu.VMEM((owners, total, lanes), BF)],
+            flops=8 * owners * total * width * lanes,
+        )(bulk[c], product[c], slot_parts, target_own)
         own_t.append(a)
         other_t.append(b)
     recv_t = [swapped(x) for x in other_t]
@@ -383,7 +420,7 @@
     anywhere = pl.BlockSpec(memory_space=pl.ANY)
     vmem = pl.BlockSpec(memory_space=pltpu.VMEM)
     schur, panel = call(
-        final_kernel,
+        factor_kernel,
         [
             jax.ShapeDtypeStruct((owned * strips, 128), F32),
             jax.ShapeDtypeStruct((owned, PW // 2), F32),
@@ -396,10 +433,11 @@
             pltpu.VMEM((owners, half, PW), BF),
             pltpu.VMEM((owned * strips, 128), F32),
             pltpu.VMEM((CHUNKS, owners, half, lanes), BF),
-            pltpu.VMEM((CHUNKS, owners, half, lanes), BF),
-            pltpu.SemaphoreType.DMA((3 + 2 * CHUNKS,)),
+            pltpu.VMEM((CHUNKS - 1, owners, half, lanes), BF),
+            pltpu.SemaphoreType.DMA((2 + 2 * CHUNKS,)),
         ],
-        in_specs=[pl.BlockSpec(memory_space=pltpu.SMEM), vmem] + [anywhere] * (2 + 2 * CHUNKS),
+        flops=60 * PW**3,
+        in_specs=[pl.BlockSpec(memory_space=pltpu.SMEM), vmem] + [anywhere] * (1 + 2 * CHUNKS),
         out_specs=[vmem, vmem],
     )(
         parity.reshape(1).astype(jnp.int32),
@@ -407,8 +445,18 @@
         front_cols,
         parent_front.reshape(owned * strips, 128),
         *own_t,
-        *recv_t,
+        *recv_t[:-1],
     )
+    steps = 4
+    last_rows = pl.BlockSpec((lanes * strips // steps, 128), lambda i: ((CHUNKS - 1) * steps + i, 0))
+    schur = call(
+        last_kernel,
+        jax.ShapeDtypeStruct((owned * strips, 128), F32),
+        grid=(steps,),
+        in_specs=[last_rows, pl.BlockSpec((owners, half, lanes), lambda i: (0, 0, 0))],
+        out_specs=last_rows,
+        input_output_aliases={0: 0},
+    )(schur, recv_t[-1])
     return (schur.reshape(owned, 1, half_cols), panel[:, None, :])
 
 

time: 207 us -> 198 us (0.957)
  waiting for transfers between devices: 59.7 us -> 52.6 us
  local copies, waits for them, and re-layouts: 12.6 us -> 5.83 us
  matrix products: 2.9 us -> 7.61 us
  Pallas kernels: 78.5 us -> 75.9 us
    ppermute x3, waiting for transfers between devices: 26.2 us -> 6.59 us  [swapped(): return lax.ppermute(block, 'cube', [(i, i ^ 1) for i in range(count)])]
    pallas_call x1 -> x3, Pallas kernels: 22 us -> 40.6 us  [the longest x1 21.8 us: shards(): call(factor_kernel, [jax.ShapeDtypeStruct((owned * strips, 128), F32), ja...]
    pallas_call x2, Pallas kernels: 36.5 us -> 18.6 us  [shards(): call(functools.partial(owner_kernel, owners, slots, owned), [jax.ShapeDty...]
    all_to_all x3 -> x4, waiting for transfers between devices: 32.8 us -> 45.3 us  [exchanged(): return lax.all_to_all(block, 'grid', 0, 0, tiled=True)]
    unnamed x22 -> x12, local copies, waits for them, and re-layouts: 9.87 us -> 3.89 us
    dot_general x5 -> x6, matrix products: 2.9 us -> 7.61 us  [dot(): lax.dot_general(a, b, dims, precision=precision, preferred_element_type=F32)]
    pallas_call x1, Pallas kernels: 20.1 us -> 16.7 us  [shards(): call(functools.partial(source_kernel, owners, slots, owned), [jax.ShapeDt...]
    all_to_all x3 -> x4, starting transfers between devices: 25.8 us -> 27.6 us  [exchanged(): return lax.all_to_all(block, 'grid', 0, 0, tiled=True)]
  transfers between devices with their start and end apart: 8 -> 9, of which waited for: 4 -> 4; matrix products, arithmetic and copies ran while one was open for 9% -> 10% of each run, Pallas kernels for 27% -> 36%
where the time goes in v3:
time: 198 us; the launch traced here: 196 us
  Pallas kernels  75.9 us (38%)
  waiting for transfers between devices  52.6 us (27%)
  starting transfers between devices  31.7 us (16%)
  between operations  14.3 us (7%)
  other arithmetic  8.28 us (4%)
  matrix products  7.61 us (4%)
  local copies, waits for them, and re-layouts  5.83 us (3%)
    all_to_all x4, waiting for transfers between devices, exchanged(): return lax.all_to_all(block, 'grid', 0, 0, tiled=True)  45.3 us
    all_to_all x4, starting transfers between devices, exchanged(): return lax.all_to_all(block, 'grid', 0, 0, tiled=True)  27.6 us
    pallas_call x1, Pallas kernels, shards(): call(factor_kernel, [jax.ShapeDtypeStruct((owned * strips, 128), F32), ja...  21.8 us
    pallas_call x2, Pallas kernels, shards(): call(functools.partial(owner_kernel, owners, slots, owned), [jax.ShapeDty...  18.6 us
    pallas_call x1, Pallas kernels, shards(): call(functools.partial(source_kernel, owners, slots, owned), [jax.ShapeDt...  16.7 us
    pallas_call x1, Pallas kernels, shards(): call(product_kernel, [jax.ShapeDtypeStruct((owners, width, lanes), F32)]...  12.9 us
    dot_general x6, matrix products, dot(): lax.dot_general(a, b, dims, precision=precision, preferred_element_type=F32)  7.61 us
    ppermute x3, waiting for transfers between devices, swapped(): return lax.ppermute(block, 'cube', [(i, i ^ 1) for i in range(count)])  6.59 us
  transfers between devices with their start and end apart: 9, of which 4 were waited for; matrix products, arithmetic and copies ran while one was open for 10% of the time, Pallas kernels for 36%

profile of v3, /device:TPU:1, one launch (start us, length us, event | category | flops | bytes accessed | tf_op | source)
XLA Modules:
  0.0 196.2 jit_solution(16631270066675504100)
XLA Ops:
  7.2 0.0 all-gather.4.cloned.1.call-start
  7.2 0.7 all-gather.4.cloned.1.call-update
  7.9 1.0 dynamic-slice_reduce_fusion.1
  8.9 0.1 reshape.258
  9.1 1.4 convert_reduce_fusion
  10.5 1.1 convolution_convert_fusion.2
  11.6 0.9 broadcast_in_dim.73
  12.5 9.4 %all-to-all-start = ((bf16[32,24,512]{2,1,0:T(8,128)(2,1)}), bf16[32,24,512]{2,1,0:T(8,128)(2,1)S(1)}, u32[]{:S(2)}, u32[]{:S(2)}) async-start(bf16[32,24,512]{2,1,0:T(8,128)(2,1)} %broadcast_in_dim.73), calls=%async_computation | async-start | bytes 1572864 | tf_op jit(solution)/shard_map/all_to_all | solution.py:303
  21.9 0.7 select_convert_fusion.1
  22.6 2.3 %select_reduce_fusion = s32[32,512]{1,0:T(8,128)S(1)} fusion(s32[32,192]{1,0:T(8,128)S(1)} %get-tuple-element.60, s32[32,192]{1,0:T(8,128)S(1)} %get-tuple-element.59), kind=kLoop, calls=%fused_computation.1 | loop fusion | flops 9420800 | bytes 114688 | tf_op jit(solution)/shard_map/reduce_sum | solution.py:330
  24.9 0.1 copy.42
  25.1 0.1 select_bitcast_fusion
  25.1 0.2 copy.43
  25.3 0.1 copy.45
  25.4 0.1 copy.44
  25.5 0.1 eq.153
  25.7 0.7 fusion.26.slot_ref
  26.4 0.0 copy-start.3
  26.4 3.9 %fusion.7 = f32[512,192]{0,1:T(8,128)S(1)} fusion(s32[6144]{0:T(1024)S(1)} %bitcast.42, bf16[1,192,6144]{2,1,0:T(8,128)(2,1)} %param.6), kind=kOutput, calls=%fused_computation.15 | convolution fusion | flops 1211301888 | bytes 2777088 | tf_op jit(solution)/shard_map/dot_general | solution.py:23
  30.3 0.0 slice-start
  30.3 8.2 %all-to-all-done = bf16[32,24,512]{2,1,0:T(8,128)(2,1)S(1)} async-done(((bf16[32,24,512]{2,1,0:T(8,128)(2,1)}), bf16[32,24,512]{2,1,0:T(8,128)(2,1)S(1)}, u32[]{:S(2)}, u32[]{:S(2)}) %all-to-all-start) | async-done | bytes 786464 | tf_op jit(solution)/shard_map/all_to_all | solution.py:303
  38.5 0.0 copy-done.3
  38.5 0.8 fusion.8
  39.4 1.1 convolution_convert_fusion
  40.5 4.1 %all-to-all-start.1 = ((bf16[32,16,512]{2,1,0:T(8,128)(2,1)}), bf16[32,16,512]{2,1,0:T(8,128)(2,1)S(1)}, u32[]{:S(2)}, u32[]{:S(2)}) async-start(bf16[32,16,512]{2,1,0:T(8,128)(2,1)} %bitcast.12), calls=%async_computation.1 | async-start | bytes 1048576 | tf_op jit(solution)/shard_map/all_to_all | solution.py:303
  44.6 0.0 all-gather.6.cloned.1.call-start
  44.6 0.7 select_convert_fusion
  45.3 0.0 slice-done
  45.3 0.2 dynamic-slice_reduce_fusion
  45.6 16.7 %shard_map.68 = (bf16[32,192,128]{2,1,0:T(8,128)(2,1)}, bf16[32,192,128]{2,1,0:T(8,128)(2,1)}) custom-call(bf16[192,6144]{1,0:T(8,128)(2,1)} %bitcast.47, f32[2,32,192]{2,1,0:T(8,128)} %fusion.26.slot_ref, f32[32,512]{1,0:T(8,128)} %get-tuple-element.57.target_ref), custom_call_target="tpu_custom_call" | custom-call | flops 3623878656 | bytes 6291456 | tf_op jit(solution)/shard_map/pallas_call | solution.py:368
  62.3 0.0 all-to-all-done.1
  62.3 0.4 fusion.34
  62.8 1.4 collective-permute-start
  64.2 6.6 %collective-permute-done = bf16[272,512]{1,0:T(8,128)(2,1)S(1)} collective-permute-done((bf16[272,512]{1,0:T(8,128)(2,1)S(1)}, bf16[272,512]{1,0:T(8,128)(2,1)S(1)}, u32[]{:S(2)}, u32[]{:S(2)}) %collective-permute-start) | collective-permute-done | bytes 278560 | tf_op jit(solution)/shard_map/ppermute | solution.py:291
  70.8 0.4 fusion.16
  71.1 0.0 copy-start
  71.2 0.2 select_reduce_fusion.1
  71.3 0.3 convolution_convert_fusion.1
  71.6 0.7 fusion.19
  72.4 0.0 all-gather.6.cloned.1.call-update
  72.4 8.3 %all-to-all-start.2 = ((bf16[32,192,128]{2,1,0:T(8,128)(2,1)}), bf16[32,192,128]{2,1,0:T(8,128)(2,1)S(1)}, u32[]{:S(2)}, u32[]{:S(2)}) async-start(bf16[32,192,128]{2,1,0:T(8,128)(2,1)} %get-tuple-element.25), calls=%async_computation.2 | async-start | bytes 3145728 | tf_op jit(solution)/shard_map/all_to_all | solution.py:303
  80.7 0.0 all-gather.4.cloned.1.call-done.panel_ref
  80.7 12.9 %shard_map.69 = (f32[32,192,128]{2,1,0:T(8,128)}, f32[32,192,128]{2,1,0:T(8,128)}) custom-call(bf16[32,192,512]{2,1,0:T(8,128)(2,1)} %all-gather.4.cloned.1.call-done.panel_ref, f32[32,192]{1,0:T(8,128)} %get-tuple-element.58.local_ref), custom_call_target="tpu_custom_call" | custom-call | flops 3221225472 | bytes 12582912 | tf_op jit(solution)/shard_map/pallas_call | solution.py:399
  93.6 0.0 copy-done
  93.6 13.2 %all-to-all-done.2.recv_ref = bf16[32,192,128]{2,1,0:T(8,128)(2,1)S(1)} async-done(((bf16[32,192,128]{2,1,0:T(8,128)(2,1)}), bf16[32,192,128]{2,1,0:T(8,128)(2,1)S(1)}, u32[]{:S(2)}, u32[]{:S(2)}) %all-to-all-start.2) | async-done | bytes 1572896 | tf_op jit(solution)/shard_map/all_to_all | solution.py:303
  106.8 0.0 copy-start.1
  106.8 5.8 %all-to-all-start.3 = ((bf16[32,192,128]{2,1,0:T(8,128)(2,1)}), bf16[32,192,128]{2,1,0:T(8,128)(2,1)}, u32[]{:S(2)}, u32[]{:S(2)}) async-start(bf16[32,192,128]{2,1,0:T(8,128)(2,1)} %get-tuple-element.31), calls=%async_computation.3 | async-start | bytes 3145728 | tf_op jit(solution)/shard_map/all_to_all | solution.py:303
  112.6 0.0 copy-done.1
  112.6 9.3 %shard_map.70 = (bf16[32,128,128]{2,1,0:T(8,128)(2,1)}, bf16[32,128,128]{2,1,0:T(8,128)(2,1)}) custom-call(bf16[32,192,128]{2,1,0:T(8,128)(2,1)} %copy-done.1, f32[32,192,128]{2,1,0:T(8,128)} %get-tuple-element.29.product_ref, f32[2,32,192]{2,1,0:T(8,128)} %fusion.26.slot_ref, f32[32,512]{1,0:T(8,128)} %get-tuple-element.56.target_ref), custom_call_target="tpu_custom_call" | custom-call | flops 3221225472 | bytes 4194304 | tf_op jit(solution)/shard_map/pallas_call | solution.py:409
  121.9 1.3 collective-permute-start.1
  123.2 23.9 %all-to-all-done.3.recv_ref = bf16[32,192,128]{2,1,0:T(8,128)(2,1)} async-done(((bf16[32,192,128]{2,1,0:T(8,128)(2,1)}), bf16[32,192,128]{2,1,0:T(8,128)(2,1)}, u32[]{:S(2)}, u32[]{:S(2)}) %all-to-all-start.3) | async-done | bytes 1572896 | tf_op jit(solution)/shard_map/all_to_all | solution.py:303
  147.1 9.3 %shard_map.71 = (bf16[32,128,128]{2,1,0:T(8,128)(2,1)}, bf16[32,128,128]{2,1,0:T(8,128)(2,1)}) custom-call(bf16[32,192,128]{2,1,0:T(8,128)(2,1)} %all-to-all-done.3.recv_ref, f32[32,192,128]{2,1,0:T(8,128)} %get-tuple-element.32.product_ref, f32[2,32,192]{2,1,0:T(8,128)} %fusion.26.slot_ref, f32[32,512]{1,0:T(8,128)} %get-tuple-element.56.target_ref), custom_call_target="tpu_custom_call" | custom-call | flops 3221225472 | bytes 4194304 | tf_op jit(solution)/shard_map/pallas_call | solution.py:409
  156.4 1.4 collective-permute-start.2
  157.8 0.0 collective-permute-done.1.refs_2_
  157.8 0.0 copy-start.4
  157.8 0.0 all-gather.6.cloned.1.call-done
  157.8 1.0 copy-done.4
  158.8 21.8 %shard_map.72 = (f32[8192,128]{1,0:T(8,128)}, f32[256,256]{1,0:T(8,128)}) custom-call(s32[1]{0:T(128)} %bitcast.parity_ref, f32[256,512]{1,0:T(8,128)} %copy-done, bf16[32,272,512]{2,1,0:T(8,128)(2,1)} %bitcast.46, f32[8192,128]{1,0:T(8,128)} %bitcast.37, bf16[32,128,128]{2,1,0:T(8,128)(2,1)} %get-tuple-element.30.refs_0_, ...), custom_call_target="tpu_custom_call" | custom-call | flops 8053063680 | bytes 8912896 | tf_op jit(solution)/shard_map/pallas_call | solution.py:422
  180.6 1.9 copy.51
  182.6 0.0 collective-permute-done.2.recv_ref
  182.6 0.0 copy-start.2
  182.6 1.0 copy-done.2
  183.5 5.8 %shard_map.73 = f32[8192,128]{1,0:T(8,128)} custom-call(f32[8192,128]{1,0:T(8,128)} %get-tuple-element.35.schur_ref, bf16[32,128,128]{2,1,0:T(8,128)(2,1)} %copy-done.2), custom_call_target="tpu_custom_call", output_to_operand_aliasing={{}: (0, {})} | custom-call | bytes 8388608 | tf_op jit(solution)/shard_map/pallas_call | solution.py:452
  (15 shorter events, 0.2 us)
Async XLA Ops:
  7.2 73.6 %all-gather.4.cloned.1.call-start = ((), (), s32[]{:S(2)}) async-start(), calls=%async_computation.4 | async-start | bytes 6488064 | tf_op jit(solution)/shard_map/all_gather | solution.py:320
  12.5 26.0 %all-to-all-start = ((bf16[32,24,512]{2,1,0:T(8,128)(2,1)}), bf16[32,24,512]{2,1,0:T(8,128)(2,1)S(1)}, u32[]{:S(2)}, u32[]{:S(2)}) async-start(bf16[32,24,512]{2,1,0:T(8,128)(2,1)} %broadcast_in_dim.73), calls=%async_computation | async-start | bytes 1572864 | tf_op jit(solution)/shard_map/all_to_all | solution.py:303
  26.4 12.1 %copy-start.3 = (bf16[1,192,512]{2,1,0:T(8,128)(2,1)S(1)}, bf16[1,192,512]{2,1,0:T(8,128)(2,1)}, u32[]{:S(2)}) copy-start(bf16[1,192,512]{2,1,0:T(8,128)(2,1)} %param.7) | copy-start | bytes 589828
  30.3 15.0 %slice-start = ((f32[256,1,4096]{2,1,0:T(1,128)}), f32[256,1,256]{2,1,0:T(1,128)S(1)}, s32[]{:S(2)}) async-start(f32[256,1,4096]{2,1,0:T(1,128)} %param.5), calls=%async_computation.6 | async-start | bytes 524288 | tf_op jit(solution)/shard_map/slice | solution.py:378
  40.5 21.8 %all-to-all-start.1 = ((bf16[32,16,512]{2,1,0:T(8,128)(2,1)}), bf16[32,16,512]{2,1,0:T(8,128)(2,1)S(1)}, u32[]{:S(2)}, u32[]{:S(2)}) async-start(bf16[32,16,512]{2,1,0:T(8,128)(2,1)} %bitcast.12), calls=%async_computation.1 | async-start | bytes 1048576 | tf_op jit(solution)/shard_map/all_to_all | solution.py:303
  44.6 113.3 %all-gather.6.cloned.1.call-start = ((), (), s32[]{:S(2)}) async-start(), calls=%async_computation.5 | async-start | bytes 9191424 | tf_op jit(solution)/shard_map/all_gather | solution.py:395
  62.8 8.0 %collective-permute-start = (bf16[272,512]{1,0:T(8,128)(2,1)S(1)}, bf16[272,512]{1,0:T(8,128)(2,1)S(1)}, u32[]{:S(2)}, u32[]{:S(2)}) collective-permute-start(bf16[272,512]{1,0:T(8,128)(2,1)S(1)} %fusion.18), channel_id=1, source_target_pairs={{0,32},{32,0},{64,96},{96,64},{1,33},{33,1},{65,97},{97,65},{2,34}... | collective-permute-start | bytes 835592 | tf_op jit(solution)/shard_map/ppermute | solution.py:291
  71.1 22.5 %copy-start = (f32[256,512]{1,0:T(8,128)}, f32[256,512]{1,0:T(8,128)S(1)}, u32[]{:S(2)}) copy-start(f32[256,512]{1,0:T(8,128)S(1)} %get-tuple-element.49.rows_ref) | copy-start | bytes 1572868
  72.4 34.4 %all-to-all-start.2 = ((bf16[32,192,128]{2,1,0:T(8,128)(2,1)}), bf16[32,192,128]{2,1,0:T(8,128)(2,1)S(1)}, u32[]{:S(2)}, u32[]{:S(2)}) async-start(bf16[32,192,128]{2,1,0:T(8,128)(2,1)} %get-tuple-element.25), calls=%async_computation.2 | async-start | bytes 3145728 | tf_op jit(solution)/shard_map/all_to_all | solution.py:303
  106.8 5.8 %copy-start.1 = (bf16[32,192,128]{2,1,0:T(8,128)(2,1)}, bf16[32,192,128]{2,1,0:T(8,128)(2,1)S(1)}, u32[]{:S(2)}) copy-start(bf16[32,192,128]{2,1,0:T(8,128)(2,1)S(1)} %all-to-all-done.2.recv_ref) | copy-start | bytes 4718596
  106.8 40.3 %all-to-all-start.3 = ((bf16[32,192,128]{2,1,0:T(8,128)(2,1)}), bf16[32,192,128]{2,1,0:T(8,128)(2,1)}, u32[]{:S(2)}, u32[]{:S(2)}) async-start(bf16[32,192,128]{2,1,0:T(8,128)(2,1)} %get-tuple-element.31), calls=%async_computation.3 | async-start | bytes 3145728 | tf_op jit(solution)/shard_map/all_to_all | solution.py:303
  121.9 35.9 %collective-permute-start.1 = (bf16[32,128,128]{2,1,0:T(8,128)(2,1)}, bf16[32,128,128]{2,1,0:T(8,128)(2,1)S(1)}, u32[]{:S(2)}, u32[]{:S(2)}) collective-permute-start(bf16[32,128,128]{2,1,0:T(8,128)(2,1)} %get-tuple-element.34), channel_id=1, source_target_pairs={{0,32},{32,0},{64,96},{96,64},{1,33},{33,1},{65,97},{97,65},{2,34}... | collective-permute-start | bytes 3145736 | tf_op jit(solution)/shard_map/ppermute | solution.py:291
  156.4 26.1 %collective-permute-start.2 = (bf16[32,128,128]{2,1,0:T(8,128)(2,1)}, bf16[32,128,128]{2,1,0:T(8,128)(2,1)S(1)}, u32[]{:S(2)}, u32[]{:S(2)}) collective-permute-start(bf16[32,128,128]{2,1,0:T(8,128)(2,1)} %get-tuple-element.36), channel_id=1, source_target_pairs={{0,32},{32,0},{64,96},{96,64},{1,33},{33,1},{65,97},{97,65},{2,34}... | collective-permute-start | bytes 3145736 | tf_op jit(solution)/shard_map/ppermute | solution.py:291
  157.8 1.0 copy-start.4
  182.6 1.0 copy-start.2
Sparse Core Ops, SparseCore 0:
  10.2 59.4 all-gather.3
  72.5 80.8 all-gather.5

commit v4 on v3

--- a/solution.py
+++ b/solution.py
@@ -82,20 +82,73 @@
     lax.fori_loop(0, owners, second, 0, unroll=2 * SOURCE_UNROLL)
 
 
-def product_kernel(panel_ref, local_ref, *refs):
-    outs, q_ref = refs[:CHUNKS], refs[CHUNKS]
-    owners, width = panel_ref.shape[:2]
+def panel_kernel(
+    owners, slots, place_ref, panel_ref, here_ref, slot_ref, targets_ref, mine_ref, packed_ref, parent_ref,
+    rows_ref, message_ref, q_ref, pick_ref,
+):
+    parity, grid_pos = place_ref[0], place_ref[1]
+    width = panel_ref.shape[1]
     owned = q_ref.shape[0]
-    lanes = owned // CHUNKS
-    here = row_numbers(owned, width)
-    q_ref[...] = jnp.zeros_like(q_ref)
-
-    def gather(s, carry):
-        q_ref[...] += dot(hot(here, local_ref[pl.ds(s, 1), :]), panel_ref[s])
-        return carry
-
-    lax.fori_loop(0, owners, gather, 0, unroll=4)
-    q = q_ref[...].astype(BF)
+    half = owned // 2
+    few, more = row_numbers(slots, width), row_numbers(2 * slots, width)
+
+    def select(s, carry):
+        pick = jnp.concatenate([hot(few, here_ref[pl.ds(s, 1), :]), hot(more, slot_ref[0, pl.ds(s, 1), :])], axis=0)
+        found = dot(pick, panel_ref[s]).astype(BF).reshape(3, slots, PW)
+        pick_ref[:, pl.ds(pl.multiple_of(s * slots, 16), slots), :] = found
+        return carry
+
+    lax.fori_loop(0, owners, select, 0, unroll=8)
+    spots = row_numbers(owned, owners * slots)
+    mine = hot(spots, mine_ref[...])
+    q = dot(mine, pick_ref[0]).astype(BF)
+    q_ref[...] = q
+    placed = dot(mine, packed_ref[...])
+    own, other = [], []
+    for b in range(2):
+        pan = dot(hot(spots, targets_ref[b : b + 1, :]), pick_ref[1 + b]).astype(BF)
+        product = dot(q, pan, NT)
+        own.append(product[:, :half])
+        other.append(product[:, half:])
+    contrib = (placed - jnp.concatenate(own + other, axis=1)).astype(BF).astype(F32)
+    rows = jnp.concatenate([contrib[:, :owned] + parent_ref[...], contrib[:, owned:]], axis=1)
+    rows_ref[...] = rows
+    rounded = rows.astype(BF)
+    low = jnp.where(diagonal_at(grid_pos, parity, owned), rows - rounded.astype(F32), 0.0)
+    message_ref[:owned] = rounded
+    message_ref[owned:] = jnp.broadcast_to(jnp.sum(low, axis=0, keepdims=True), (LOW_ROWS, PW)).astype(BF)
+
+
+def diagonal_at(grid_pos, parity, owned):
+    row = lax.broadcasted_iota(jnp.int32, (owned, PW), 0) + grid_pos * owned
+    return natural(lax.broadcasted_iota(jnp.int32, (owned, PW), 1), parity, PW // 2) == row
+
+
+def rows_kernel(place_ref, mine_ref, theirs_ref, rows_ref, message_ref):
+    parity, grid_pos = place_ref[0], place_ref[1]
+    owned = mine_ref.shape[0]
+    half = owned // 2
+    theirs = theirs_ref[...].astype(F32)
+    theirs = jnp.concatenate([theirs[:, PW // 2 :], theirs[:, : PW // 2]], axis=1)
+    on = diagonal_at(grid_pos, parity, owned)
+    rows = mine_ref[...] + theirs[:owned] + jnp.where(on, theirs[owned : owned + 1], 0.0)
+    rows_ref[...] = rows
+    rounded = rows.astype(BF)
+    low = jnp.sum(jnp.where(on, rows - rounded.astype(F32), 0.0), axis=0, keepdims=True)
+    at = lax.broadcasted_iota(jnp.int32, (owned, owned), 0)
+    pick = natural(at, parity, half) == lax.broadcasted_iota(jnp.int32, (owned, owned), 1)
+    ordered = dot(jnp.where(pick, 1.0, 0.0).astype(BF), rounded).astype(BF)
+    message_ref[:half] = ordered[:half]
+    message_ref[half : half + half // 2] = jnp.concatenate(
+        [ordered[half : half + half // 2, PW // 2 :], ordered[half + half // 2 :, PW // 2 :]], axis=1
+    )
+    message_ref[half + half // 2 :] = jnp.broadcast_to(low, (LOW_ROWS, PW)).astype(BF)
+
+
+def product_kernel(panel_ref, q_ref, *outs):
+    owners = panel_ref.shape[0]
+    lanes = q_ref.shape[0] // CHUNKS
+    q = q_ref[...]
 
     def first(s, carry):
         product = dot(panel_ref[s], q, NT)
@@ -103,7 +156,7 @@
             outs[c][s] = product[:, c * lanes : (c + 1) * lanes]
         return carry
 
-    lax.fori_loop(0, owners, first, 0, unroll=4)
+    lax.fori_loop(0, owners, first, 0, unroll=8)
 
 
 def owner_kernel(owners, slots, owned, recv_ref, product_ref, slot_ref, target_ref, own_ref, other_ref, y_ref):
@@ -215,9 +268,9 @@
 
 
 def factor_kernel(parity_ref, rows_ref, front_hbm, parent_hbm, *refs):
-    own_hbm, recv_hbm = refs[:CHUNKS], refs[CHUNKS : 2 * CHUNKS - 1]
-    schur_ref, panel_ref, w_ref, s_ref, t_ref, lead_ref, cols_ref, parent_ref = refs[2 * CHUNKS - 1 : 2 * CHUNKS + 7]
-    own_ref, recv_ref, sems = refs[2 * CHUNKS + 7 :]
+    own_hbm, recv_hbm = refs[:CHUNKS], refs[CHUNKS : 2 * CHUNKS]
+    schur_ref, panel_ref, w_ref, s_ref, t_ref, lead_ref, cols_ref, parent_ref = refs[2 * CHUNKS : 2 * CHUNKS + 8]
+    own_ref, recv_ref, sems = refs[2 * CHUNKS + 8 :]
     owned = rows_ref.shape[0]
     half = owned // 2
     strips = parent_ref.shape[0] // owned
@@ -229,15 +282,17 @@
     ]
     for c in range(CHUNKS):
         copies.append(pltpu.make_async_copy(own_hbm[c], own_ref.at[c], sems.at[3 + c]))
-    for c in range(CHUNKS - 1):
+    for c in range(CHUNKS):
         copies.append(pltpu.make_async_copy(recv_hbm[c], recv_ref.at[c], sems.at[3 + CHUNKS + c]))
     for copy in copies:
         copy.start()
     copies[0].wait()
-    pieces = [(0, 0), (1, 0), (0, half), (1, half)]
-    pivot = jnp.concatenate([lead_ref[b, i : i + half] for b, i in pieces], axis=0).astype(F32)
-    low = jnp.concatenate([lead_ref[b, owned : owned + 1, i : i + half] for b, i in pieces], axis=1).astype(F32)
-    pivot = pivot + eye(PW) * low
+    top = jnp.concatenate([lead_ref[0, :half], lead_ref[1, :half]], axis=0).astype(F32)
+    fold = lead_ref[:, half : half + half // 2].astype(F32)
+    corner = jnp.concatenate([fold[b, :, i : i + owned] for b in range(2) for i in (0, owned)], axis=0)
+    low = lead_ref[:, half + half // 2 : half + half // 2 + 1].astype(F32)
+    bottom = jnp.concatenate([top[:, owned:].T, corner], axis=1)
+    pivot = jnp.concatenate([top, bottom], axis=0) + eye(PW) * (low[0] + low[1])
     lead_cols = split(pivot[: PW // 2])
     w = inverse_factor(parity_ref[0], pivot, w_ref, s_ref, t_ref)
     w_ref[...] = w
@@ -257,46 +312,16 @@
         placed = []
         for c in range(CHUNKS):
             z = dot(unit, own_ref[c, pl.ds(2 * pair, 2)].reshape(2 * half, lanes), NT)
-            if c < CHUNKS - 1:
-                z = z + dot(unit, recv_ref[c, pl.ds(2 * pair, 2)].reshape(2 * half, lanes), NT)
-            placed.append(z)
+            placed.append(z + dot(unit, recv_ref[c, pl.ds(2 * pair, 2)].reshape(2 * half, lanes), NT))
         change = jnp.concatenate(placed, axis=0) - update
         for side in range(2):
             at = pl.ds(2 * pair + side, owned, stride=strips)
             schur_ref[at, :] = parent_ref[at, :] + change[:, side * half : (side + 1) * half]
 
 
-def last_kernel(schur_ref, recv_ref, out_ref):
-    rows = pl.program_id(0)
-    lanes = recv_ref.shape[2]
-    strips = recv_ref.shape[0]
-    part = schur_ref.shape[0] // strips
-    r = lax.broadcasted_iota(jnp.int32, (part, lanes), 0) + rows * part
-    c = lax.broadcasted_iota(jnp.int32, (part, lanes), 1)
-    unit = jnp.where(r == c, 1.0, 0.0).astype(BF)
-    for pair in range(strips // 2):
-        z = dot(unit, recv_ref[pl.ds(2 * pair, 2)].reshape(-1, lanes), NT)
-        for side in range(2):
-            at = pl.ds(2 * pair + side, part, stride=strips)
-            out_ref[at, :] = schur_ref[at, :] + z[:, side * 128 : (side + 1) * 128]
-
-
-def swap_halves(x, axis):
-    a, b = jnp.split(x, 2, axis=axis)
-    return jnp.concatenate([b, a], axis=axis)
-
-
 def swapped(block):
     count = lax.axis_size("cube")
     return lax.ppermute(block, "cube", [(i, i ^ 1) for i in range(count)])
-
-
-def natural_position(row, parity):
-    return ((row & 1) ^ parity) * (PW // 2) + (row >> 1) + jnp.where(row < PW, 0, PW)
-
-
-def low_message(low):
-    return jnp.pad(low.astype(BF)[None, :], ((0, LOW_ROWS - 1), (0, PW - low.shape[0])))
 
 
 def exchanged(block):
@@ -336,33 +361,13 @@
     slot_parts = slot_of[None] - jnp.array([0, total // 2])[:, None, None]
     slot_parts = jnp.where((slot_parts >= 0) & (slot_parts < total // 2), slot_parts, -1).astype(F32)
     my_slot = lax.dynamic_index_in_dim(slot_of, grid_pos, 0, keepdims=False)
-    my_owner = lax.dynamic_index_in_dim(owner_of, grid_pos, 0, keepdims=False)
-    my_rank = lax.dynamic_index_in_dim(rank_of, grid_pos, 0, keepdims=False)
-
-    pivot_slot = jnp.where(my_owner < 2, my_owner * capacity + my_rank, -1)
-    pivot_pick = (lax.iota(jnp.int32, 2 * capacity)[:, None] == pivot_slot[None, :]).astype(BF)
-    pivot_rows = dot(pivot_pick, own_panel).astype(BF)
-    pivot_rows = exchanged(jnp.broadcast_to(pivot_rows[None], (owners,) + pivot_rows.shape))
 
     row_flat = row_of.reshape(-1)
     pan_of = jnp.where(row_flat < PW, ((row_flat & 1) ^ parity) * (PW // 2) + (row_flat >> 1), -1)
     block_pan = dot(child_block[0], (pan_of[:, None] == lax.iota(jnp.int32, PW)[None, :]).astype(BF)).astype(BF)
 
-    pivot_target = target[:2, :, :capacity]
-    pivot_pos = jnp.where(
-        pivot_target >= 0,
-        ((pivot_target & 1) ^ parity) * (PW // 2)
-        + lax.iota(jnp.int32, 2)[:, None, None] * half
-        + (pivot_target >> 1),
-        -1,
-    )
-    pivot_pos = pivot_pos.transpose(1, 0, 2).reshape(-1)
-    pivot_hot = (lax.iota(jnp.int32, PW)[:, None] == pivot_pos[None, :]).astype(BF)
-    panel_pan = dot(pivot_hot, pivot_rows.reshape(-1, PW)).astype(BF)
-
-    contrib_pan = (block_pan.astype(F32) - dot(own_panel, panel_pan, NT)).astype(BF)
     pack = (lax.iota(jnp.int32, total)[:, None] == my_slot[None, :]).astype(BF)
-    packed = dot(pack, contrib_pan).astype(BF).reshape(owners, slots, PW)
+    packed = dot(pack, block_pan).astype(BF).reshape(owners, slots, PW)
     packed, slot_parts = lax.optimization_barrier((packed, slot_parts))
     packed = exchanged(packed)
     spread = call(
@@ -372,38 +377,42 @@
         flops=6 * owners * total * width * width,
     )(child_block[0], slot_parts, target_nat.astype(F32))
     packed, spread = lax.optimization_barrier((packed, spread))
-    packed = packed.reshape(total, PW)
-    my_target = lax.dynamic_index_in_dim(target_nat, grid_pos, 0, keepdims=False)
-    unpack = (lax.iota(jnp.int32, owned)[:, None] == my_target[None, :]).astype(BF)
-    rows_mine = dot(unpack, packed) + jnp.pad(parent_front[:, 0, : PW // 2], ((0, 0), (0, PW // 2)))
-    row_pos = natural_position(grid_pos * owned + lax.iota(jnp.int32, owned), parity)
-    diagonal = row_pos[:, None] == lax.iota(jnp.int32, PW)[None, :]
-
-    def rounded(x):
-        return lax.reduce_precision(x, 8, 7)
-
-    low_mine = jnp.sum(jnp.where(diagonal, rows_mine - rounded(rows_mine), 0.0), axis=1)
-    rows_theirs = swapped(jnp.concatenate([rows_mine.astype(BF), low_message(low_mine)], axis=0))
-    low_theirs = rows_theirs[owned, :owned].astype(F32)[:, None]
-    rows = rows_mine + swap_halves(rows_theirs[:owned], 1).astype(F32)
-    rows = rows + jnp.where(diagonal & (row_pos >= PW // 2)[:, None], low_theirs, 0.0)
-    low_rows = jnp.sum(jnp.where(diagonal, rows - rounded(rows), 0.0), axis=1)
-    local_order = natural(lax.iota(jnp.int32, owned), parity, half)
-    choose = local_order[:, None] == lax.iota(jnp.int32, owned)[None, :]
-    low_rows = jnp.sum(jnp.where(choose, low_rows[None, :], 0.0), axis=1)
-    front_cols = dot(choose.astype(BF), rows.astype(BF)).astype(BF)
-    front_cols = lax.all_gather(jnp.concatenate([front_cols, low_message(low_rows)], axis=0), "grid")
-
     bulk = [exchanged(spread[0])]
-    local_here = jnp.where(owner_of == grid_pos, local_of, -1).astype(F32)
+
+    smem, vmem = pl.BlockSpec(memory_space=pltpu.SMEM), pl.BlockSpec(memory_space=pltpu.VMEM)
+    place = jnp.stack([parity, grid_pos]).astype(jnp.int32)
+    here = slot_of - grid_pos * slots
+    here = jnp.where((here >= 0) & (here < slots), here, -1).astype(F32)
+    my_target = lax.dynamic_slice_in_dim(target_nat, grid_pos, 1).astype(F32)
+    rows_mine, message, q = call(
+        functools.partial(panel_kernel, owners, slots),
+        [
+            jax.ShapeDtypeStruct((owned, PW), F32),
+            jax.ShapeDtypeStruct((owned + LOW_ROWS, PW), BF),
+            jax.ShapeDtypeStruct((owned, PW), BF),
+        ],
+        [pltpu.VMEM((3, total, PW), BF)],
+        flops=4 * owners * width * owned * PW,
+        in_specs=[smem] + [vmem] * 7,
+    )(place, panel_all, here, slot_parts, target_own, my_target, packed.reshape(total, PW), parent_front[:, 0, : PW // 2])
     product = call(
         product_kernel,
         [jax.ShapeDtypeStruct((owners, width, lanes), F32)] * CHUNKS,
-        [pltpu.VMEM((owned, PW), F32)],
         flops=4 * owners * width * owned * PW,
-    )(panel_all, local_here)
+    )(panel_all, q)
+    theirs, bulk[0], product = lax.optimization_barrier((swapped(message), bulk[0], product))
     rest, product = lax.optimization_barrier((spread[1:], product))
     bulk = bulk + [exchanged(part) for part in rest]
+    rows, message = call(
+        rows_kernel,
+        [
+            jax.ShapeDtypeStruct((owned, PW), F32),
+            jax.ShapeDtypeStruct((half + half // 2 + LOW_ROWS, PW), BF),
+        ],
+        in_specs=[smem, vmem, vmem],
+    )(place, rows_mine, theirs)
+    front_cols = lax.all_gather(message, "grid")
+
     own_t, other_t = [], []
     for c in range(CHUNKS):
         a, b = call(
@@ -418,7 +427,6 @@
 
     strips = half_cols // 128
     anywhere = pl.BlockSpec(memory_space=pl.ANY)
-    vmem = pl.BlockSpec(memory_space=pltpu.VMEM)
     schur, panel = call(
         factor_kernel,
         [
@@ -429,34 +437,24 @@
             pltpu.VMEM((PW, PW), F32),
             pltpu.VMEM((PW, PW), F32),
             pltpu.VMEM((PW, PW), F32),
-            pltpu.VMEM((2, owned + LOW_ROWS, PW), BF),
+            pltpu.VMEM((2, half + half // 2 + LOW_ROWS, PW), BF),
             pltpu.VMEM((owners, half, PW), BF),
             pltpu.VMEM((owned * strips, 128), F32),
             pltpu.VMEM((CHUNKS, owners, half, lanes), BF),
-            pltpu.VMEM((CHUNKS - 1, owners, half, lanes), BF),
-            pltpu.SemaphoreType.DMA((2 + 2 * CHUNKS,)),
+            pltpu.VMEM((CHUNKS, owners, half, lanes), BF),
+            pltpu.SemaphoreType.DMA((3 + 2 * CHUNKS,)),
         ],
         flops=60 * PW**3,
-        in_specs=[pl.BlockSpec(memory_space=pltpu.SMEM), vmem] + [anywhere] * (1 + 2 * CHUNKS),
+        in_specs=[smem, vmem] + [anywhere] * (2 + 2 * CHUNKS),
         out_specs=[vmem, vmem],
     )(
-        parity.reshape(1).astype(jnp.int32),
+        place,
         rows,
         front_cols,
         parent_front.reshape(owned * strips, 128),
         *own_t,
-        *recv_t[:-1],
+        *recv_t,
     )
-    steps = 4
-    last_rows = pl.BlockSpec((lanes * strips // steps, 128), lambda i: ((CHUNKS - 1) * steps + i, 0))
-    schur = call(
-        last_kernel,
-        jax.ShapeDtypeStruct((owned * strips, 128), F32),
-        grid=(steps,),
-        in_specs=[last_rows, pl.BlockSpec((owners, half, lanes), lambda i: (0, 0, 0))],
-        out_specs=last_rows,
-        input_output_aliases={0: 0},
-    )(schur, recv_t[-1])
     return (schur.reshape(owned, 1, half_cols), panel[:, None, :])
 
 

time: 198 us -> 201 us (1.015)
  waiting for transfers between devices: 52.6 us -> 63 us
  starting transfers between devices: 31.7 us -> 27.4 us
  matrix products: 7.61 us -> 4.94 us
    all_to_all x4 -> x3, waiting for transfers between devices: 45.3 us -> 15.1 us  [exchanged(): return lax.all_to_all(block, 'grid', 0, 0, tiled=True)]
    all_gather x1, waiting for transfers between devices: 0.02 us -> 24.8 us  [shards(): panel_all = lax.all_gather(own_panel, 'grid')]
    ppermute x3, waiting for transfers between devices: 6.59 us -> 22.4 us  [swapped(): return lax.ppermute(block, 'cube', [(i, i ^ 1) for i in range(count)])]
    pallas_call x1, Pallas kernels: 12.9 us -> 8.95 us  [shards(): call(product_kernel, [jax.ShapeDtypeStruct((owners, width, lanes), F32)]...]
    all_to_all x4 -> x3, starting transfers between devices: 27.6 us -> 24.4 us  [exchanged(): return lax.all_to_all(block, 'grid', 0, 0, tiled=True)]
    pallas_call x1 -> x2, Pallas kernels: 5.83 us -> 8.91 us  [the longest x1 6.73 us: shards(): call(functools.partial(panel_kernel, owners, slots), [jax.ShapeDtypeStruc...]
    dot_general x6 -> x1, matrix products: 7.61 us -> 4.94 us  [dot(): lax.dot_general(a, b, dims, precision=precision, preferred_element_type=F32)]
    unnamed x12 -> x14, local copies, waits for them, and re-layouts: 3.89 us -> 5.56 us
  transfers between devices with their start and end apart: 9 -> 8, of which waited for: 4 -> 3; matrix products, arithmetic and copies ran while one was open for 10% -> 7% of each run, Pallas kernels for 36% -> 26%
where the time goes in v4:
time: 201 us; the launch traced here: 199 us
  Pallas kernels  75.2 us (37%)
  waiting for transfers between devices  63 us (31%)
  starting transfers between devices  27.4 us (14%)
  between operations  14.2 us (7%)
  other arithmetic  7.98 us (4%)
  local copies, waits for them, and re-layouts  6.06 us (3%)
  matrix products  4.94 us (2%)
    all_gather x1, waiting for transfers between devices, shards(): panel_all = lax.all_gather(own_panel, 'grid')  24.8 us
    all_to_all x3, starting transfers between devices, exchanged(): return lax.all_to_all(block, 'grid', 0, 0, tiled=True)  24.4 us
    ppermute x3, waiting for transfers between devices, swapped(): return lax.ppermute(block, 'cube', [(i, i ^ 1) for i in range(count)])  22.4 us
    pallas_call x1, Pallas kernels, shards(): call(factor_kernel, [jax.ShapeDtypeStruct((owned * strips, 128), F32), ja...  21.9 us
    pallas_call x2, Pallas kernels, shards(): call(functools.partial(owner_kernel, owners, slots, owned), [jax.ShapeDty...  18.6 us
    pallas_call x1, Pallas kernels, shards(): call(functools.partial(source_kernel, owners, slots, owned), [jax.ShapeDt...  16.8 us
    all_to_all x3, waiting for transfers between devices, exchanged(): return lax.all_to_all(block, 'grid', 0, 0, tiled=True)  15.1 us
    pallas_call x1, Pallas kernels, shards(): call(product_kernel, [jax.ShapeDtypeStruct((owners, width, lanes), F32)]...  8.95 us
  transfers between devices with their start and end apart: 8, of which 3 were waited for; matrix products, arithmetic and copies ran while one was open for 7% of the time, Pallas kernels for 26%

profile of v4, /device:TPU:1, one launch (start us, length us, event | category | flops | bytes accessed | tf_op | source)
XLA Modules:
  0.0 198.7 jit_solution(15340383910582408637)
XLA Ops:
  7.2 0.0 all-gather.4.cloned.1.call-start
  7.2 0.7 all-gather.4.cloned.1.call-update
  7.9 1.0 compare_select_fusion
  8.9 0.1 reshape.192
  9.1 1.4 convert_reduce_fusion
  10.5 0.6 select_convert_fusion.1
  11.1 0.7 fusion.4.slot_ref
  11.8 4.9 %convolution_convert_fusion = bf16[512,512]{1,0:T(8,128)(2,1)} fusion(s32[6144]{0:T(1024)S(1)} %bitcast.27, s32[192]{0:T(256)S(1)} %bitcast.28, bf16[1,192,6144]{2,1,0:T(8,128)(2,1)} %param.6), kind=kOutput, calls=%fused_computation.6 | convolution fusion | flops 1312227328 | bytes 2908928 | tf_op jit(solution)/shard_map/dot_general | solution.py:23
  16.8 9.4 %all-to-all-start = ((bf16[32,16,512]{2,1,0:T(8,128)(2,1)}), bf16[32,16,512]{2,1,0:T(8,128)(2,1)S(1)}, u32[]{:S(2)}, u32[]{:S(2)}) async-start(bf16[32,16,512]{2,1,0:T(8,128)(2,1)} %bitcast.5), calls=%async_computation | async-start | bytes 1048576 | tf_op jit(solution)/shard_map/all_to_all | solution.py:328
  26.2 2.3 %select_reduce_fusion = s32[32,512]{1,0:T(8,128)S(1)} fusion(s32[32,192]{1,0:T(8,128)S(1)} %get-tuple-element.70, s32[32,192]{1,0:T(8,128)S(1)} %get-tuple-element.65), kind=kLoop, calls=%fused_computation | loop fusion | flops 9420800 | bytes 114688 | tf_op jit(solution)/shard_map/reduce_sum | solution.py:355
  28.6 0.1 copy.31
  28.7 0.2 copy.32
  28.9 0.1 copy.33
  29.0 0.7 fusion.11
  29.7 16.8 %shard_map.68 = (bf16[32,192,128]{2,1,0:T(8,128)(2,1)}, bf16[32,192,128]{2,1,0:T(8,128)(2,1)}) custom-call(bf16[192,6144]{1,0:T(8,128)(2,1)} %bitcast.30, f32[2,32,192]{2,1,0:T(8,128)} %fusion.4.slot_ref, f32[32,512]{1,0:T(8,128)} %get-tuple-element.68.target_ref), custom_call_target="tpu_custom_call" | custom-call | flops 3623878656 | bytes 6291456 | tf_op jit(solution)/shard_map/pallas_call | solution.py:373
  46.4 0.0 slice-start
  46.4 0.0 all-to-all-done
  46.4 0.0 copy-start.2
  46.4 7.5 %all-to-all-start.1 = ((bf16[32,192,128]{2,1,0:T(8,128)(2,1)}), bf16[32,192,128]{2,1,0:T(8,128)(2,1)S(1)}, u32[]{:S(2)}, u32[]{:S(2)}) async-start(bf16[32,192,128]{2,1,0:T(8,128)(2,1)} %get-tuple-element.36), calls=%async_computation.1 | async-start | bytes 3145728 | tf_op jit(solution)/shard_map/all_to_all | solution.py:328
  54.0 0.0 all-gather.6.cloned.1.call-start
  54.0 0.0 slice-done
  54.0 0.7 copy.43
  54.7 0.6 pad_add_fusion.place_ref.parity_ref
  55.3 0.6 dynamic-slice_convert_fusion.mine_ref
  55.9 24.8 %all-gather.4.cloned.1.call-done.panel_ref = bf16[32,192,512]{2,1,0:T(8,128)(2,1)} async-done(((bf16[1,192,512]{2,1,0:T(8,128)(2,1)}), bf16[32,192,512]{2,1,0:T(8,128)(2,1)}) %all-gather.4.cloned.1.call-update) | async-done | bytes 6291472 | tf_op jit(solution)/shard_map/all_gather | solution.py:345
  80.7 0.0 copy-done.2
  80.7 6.7 %shard_map.69 = (f32[256,512]{1,0:T(8,128)}, bf16[272,512]{1,0:T(8,128)(2,1)}, bf16[256,512]{1,0:T(8,128)(2,1)}) custom-call(s32[2]{0:T(128)} %pad_add_fusion.place_ref.parity_ref, bf16[32,192,512]{2,1,0:T(8,128)(2,1)} %all-gather.4.cloned.1.call-done.panel_ref, f32[32,192]{1,0:T(8,128)} %get-tuple-element.64.here_ref, f32[2,32,192]{2,1,0:T(8,128)} %fusion.4.slot_ref, ...), custom_call_target="tpu_custom_call" | custom-call | flops 3221225472 | bytes 2129920 | tf_op jit(solution)/shard_map/pallas_call | solution.py:387
  87.4 1.1 collective-permute-start
  88.5 8.9 %shard_map.70 = (f32[32,192,128]{2,1,0:T(8,128)}, f32[32,192,128]{2,1,0:T(8,128)}) custom-call(bf16[32,192,512]{2,1,0:T(8,128)(2,1)} %all-gather.4.cloned.1.call-done.panel_ref, bf16[256,512]{1,0:T(8,128)(2,1)} %get-tuple-element.37.q_ref), custom_call_target="tpu_custom_call" | custom-call | flops 3221225472 | bytes 12582912 | tf_op jit(solution)/shard_map/pallas_call | solution.py:398
  97.4 0.0 all-to-all-done.1.recv_ref
  97.4 0.0 copy-start
  97.4 0.0 collective-permute-done.theirs_ref
  97.4 0.0 copy-start.3
  97.5 0.7 copy-done.3
  98.2 2.2 %shard_map.71 = (f32[256,512]{1,0:T(8,128)}, bf16[208,512]{1,0:T(8,128)(2,1)}) custom-call(s32[2]{0:T(128)} %pad_add_fusion.place_ref.parity_ref, f32[256,512]{1,0:T(8,128)} %get-tuple-element.34.mine_ref, bf16[272,512]{1,0:T(8,128)(2,1)} %copy-done.3), custom_call_target="tpu_custom_call" | custom-call | bytes 1474560 | tf_op jit(solution)/shard_map/pallas_call | solution.py:406
  100.4 0.0 all-gather.6.cloned.1.call-update
  100.4 7.4 %all-to-all-start.2 = ((bf16[32,192,128]{2,1,0:T(8,128)(2,1)}), bf16[32,192,128]{2,1,0:T(8,128)(2,1)S(1)}, u32[]{:S(2)}, u32[]{:S(2)}) async-start(bf16[32,192,128]{2,1,0:T(8,128)(2,1)} %get-tuple-element.49), calls=%async_computation.2 | async-start | bytes 3145728 | tf_op jit(solution)/shard_map/all_to_all | solution.py:328
  107.8 0.0 copy-done
  107.8 9.3 %shard_map.72 = (bf16[32,128,128]{2,1,0:T(8,128)(2,1)}, bf16[32,128,128]{2,1,0:T(8,128)(2,1)}) custom-call(bf16[32,192,128]{2,1,0:T(8,128)(2,1)} %copy-done, f32[32,192,128]{2,1,0:T(8,128)} %get-tuple-element.47.product_ref, f32[2,32,192]{2,1,0:T(8,128)} %fusion.4.slot_ref, f32[32,512]{1,0:T(8,128)} %get-tuple-element.69.targets_ref.target_ref), custom_call_target="tpu_custom_call" | custom-call | flops 3221225472 | bytes 4194304 | tf_op jit(solution)/shard_map/pallas_call | solution.py:418
  117.1 0.3 collective-permute-start.1
  117.3 15.1 %all-to-all-done.2.recv_ref = bf16[32,192,128]{2,1,0:T(8,128)(2,1)S(1)} async-done(((bf16[32,192,128]{2,1,0:T(8,128)(2,1)}), bf16[32,192,128]{2,1,0:T(8,128)(2,1)S(1)}, u32[]{:S(2)}, u32[]{:S(2)}) %all-to-all-start.2) | async-done | bytes 1572896 | tf_op jit(solution)/shard_map/all_to_all | solution.py:328
  132.4 0.0 copy-start.1
  132.4 1.1 copy-done.1
  133.6 9.4 %shard_map.73 = (bf16[32,128,128]{2,1,0:T(8,128)(2,1)}, bf16[32,128,128]{2,1,0:T(8,128)(2,1)}) custom-call(bf16[32,192,128]{2,1,0:T(8,128)(2,1)} %copy-done.1, f32[32,192,128]{2,1,0:T(8,128)} %get-tuple-element.50.product_ref, f32[2,32,192]{2,1,0:T(8,128)} %fusion.4.slot_ref, f32[32,512]{1,0:T(8,128)} %get-tuple-element.69.targets_ref.target_ref), custom_call_target="tpu_custom_call" | custom-call | flops 3221225472 | bytes 4194304 | tf_op jit(solution)/shard_map/pallas_call | solution.py:418
  142.9 1.6 collective-permute-start.2
  144.5 0.0 collective-permute-done.1.refs_2_
  144.5 0.0 copy-start.4
  144.5 22.4 %collective-permute-done.2.refs_3_ = bf16[32,128,128]{2,1,0:T(8,128)(2,1)S(1)} collective-permute-done((bf16[32,128,128]{2,1,0:T(8,128)(2,1)}, bf16[32,128,128]{2,1,0:T(8,128)(2,1)S(1)}, u32[]{:S(2)}, u32[]{:S(2)}) %collective-permute-start.2) | collective-permute-done | bytes 1048608 | tf_op jit(solution)/shard_map/ppermute | solution.py:324
  167.0 0.0 copy-start.5
  167.0 0.0 all-gather.6.cloned.1.call-done
  167.0 0.0 copy-done.4
  167.0 1.0 copy-done.5
  168.0 21.9 %shard_map.74 = (f32[8192,128]{1,0:T(8,128)}, f32[256,256]{1,0:T(8,128)}) custom-call(s32[2]{0:T(128)} %pad_add_fusion.place_ref.parity_ref, f32[256,512]{1,0:T(8,128)} %get-tuple-element.41.rows_ref, bf16[32,208,512]{2,1,0:T(8,128)(2,1)} %bitcast.29, f32[8192,128]{1,0:T(8,128)} %bitcast.23, bf16[32,128,128]{2,1,0:T(8,128)(2,1)} %get-tuple-element.48.refs_0_, ...), custom_call_target="tpu_custom_call" | custom-call | flops 8053063680 | bytes 8912896 | tf_op jit(solution)/shard_map/pallas_call | solution.py:430
  190.0 1.9 copy.40
  (5 shorter events, 0.1 us)
Async XLA Ops:
  7.2 73.5 %all-gather.4.cloned.1.call-start = ((), (), s32[]{:S(2)}) async-start(), calls=%async_computation.3 | async-start | bytes 6488064 | tf_op jit(solution)/shard_map/all_gather | solution.py:345
  16.8 29.7 %all-to-all-start = ((bf16[32,16,512]{2,1,0:T(8,128)(2,1)}), bf16[32,16,512]{2,1,0:T(8,128)(2,1)S(1)}, u32[]{:S(2)}, u32[]{:S(2)}) async-start(bf16[32,16,512]{2,1,0:T(8,128)(2,1)} %bitcast.5), calls=%async_computation | async-start | bytes 1048576 | tf_op jit(solution)/shard_map/all_to_all | solution.py:328
  46.4 7.6 %slice-start = ((f32[256,1,4096]{2,1,0:T(1,128)}), f32[256,1,256]{2,1,0:T(1,128)S(1)}, s32[]{:S(2)}) async-start(f32[256,1,4096]{2,1,0:T(1,128)} %param.5), calls=%async_computation.5 | async-start | bytes 524288 | tf_op jit(solution)/shard_map/slice | solution.py:397
  46.4 34.3 %copy-start.2 = (bf16[32,16,512]{2,1,0:T(8,128)(2,1)}, bf16[32,16,512]{2,1,0:T(8,128)(2,1)S(1)}, u32[]{:S(2)}) copy-start(bf16[32,16,512]{2,1,0:T(8,128)(2,1)S(1)} %all-to-all-done) | copy-start | bytes 1572868
  46.4 51.0 %all-to-all-start.1 = ((bf16[32,192,128]{2,1,0:T(8,128)(2,1)}), bf16[32,192,128]{2,1,0:T(8,128)(2,1)S(1)}, u32[]{:S(2)}, u32[]{:S(2)}) async-start(bf16[32,192,128]{2,1,0:T(8,128)(2,1)} %get-tuple-element.36), calls=%async_computation.1 | async-start | bytes 3145728 | tf_op jit(solution)/shard_map/all_to_all | solution.py:328
  54.0 113.0 %all-gather.6.cloned.1.call-start = ((), (), s32[]{:S(2)}) async-start(), calls=%async_computation.4 | async-start | bytes 7028736 | tf_op jit(solution)/shard_map/all_gather | solution.py:414
  87.4 10.0 %collective-permute-start = (bf16[272,512]{1,0:T(8,128)(2,1)}, bf16[272,512]{1,0:T(8,128)(2,1)S(1)}, u32[]{:S(2)}, u32[]{:S(2)}) collective-permute-start(bf16[272,512]{1,0:T(8,128)(2,1)} %get-tuple-element.35), channel_id=1, source_target_pairs={{0,32},{32,0},{64,96},{96,64},{1,33},{33,1},{65,97},{97,65},{2,34}... | collective-permute-start | bytes 835592 | tf_op jit(solution)/shard_map/ppermute | solution.py:324
  97.4 10.4 %copy-start = (bf16[32,192,128]{2,1,0:T(8,128)(2,1)}, bf16[32,192,128]{2,1,0:T(8,128)(2,1)S(1)}, u32[]{:S(2)}) copy-start(bf16[32,192,128]{2,1,0:T(8,128)(2,1)S(1)} %all-to-all-done.1.recv_ref) | copy-start | bytes 4718596
  97.4 0.7 copy-start.3
  100.4 32.0 %all-to-all-start.2 = ((bf16[32,192,128]{2,1,0:T(8,128)(2,1)}), bf16[32,192,128]{2,1,0:T(8,128)(2,1)S(1)}, u32[]{:S(2)}, u32[]{:S(2)}) async-start(bf16[32,192,128]{2,1,0:T(8,128)(2,1)} %get-tuple-element.49), calls=%async_computation.2 | async-start | bytes 3145728 | tf_op jit(solution)/shard_map/all_to_all | solution.py:328
  117.1 27.5 %collective-permute-start.1 = (bf16[32,128,128]{2,1,0:T(8,128)(2,1)}, bf16[32,128,128]{2,1,0:T(8,128)(2,1)S(1)}, u32[]{:S(2)}, u32[]{:S(2)}) collective-permute-start(bf16[32,128,128]{2,1,0:T(8,128)(2,1)} %get-tuple-element.52), channel_id=1, source_target_pairs={{0,32},{32,0},{64,96},{96,64},{1,33},{33,1},{65,97},{97,65},{2,34}... | collective-permute-start | bytes 3145736 | tf_op jit(solution)/shard_map/ppermute | solution.py:324
  132.4 1.1 copy-start.1
  142.9 24.0 %collective-permute-start.2 = (bf16[32,128,128]{2,1,0:T(8,128)(2,1)}, bf16[32,128,128]{2,1,0:T(8,128)(2,1)S(1)}, u32[]{:S(2)}, u32[]{:S(2)}) collective-permute-start(bf16[32,128,128]{2,1,0:T(8,128)(2,1)} %get-tuple-element.53), channel_id=1, source_target_pairs={{0,32},{32,0},{64,96},{96,64},{1,33},{33,1},{65,97},{97,65},{2,34}... | collective-permute-start | bytes 3145736 | tf_op jit(solution)/shard_map/ppermute | solution.py:324
  144.5 22.4 %copy-start.4 = (bf16[32,128,128]{2,1,0:T(8,128)(2,1)}, bf16[32,128,128]{2,1,0:T(8,128)(2,1)S(1)}, u32[]{:S(2)}) copy-start(bf16[32,128,128]{2,1,0:T(8,128)(2,1)S(1)} %collective-permute-done.1.refs_2_) | copy-start | bytes 3145732
  167.0 1.0 copy-start.5
Sparse Core Ops, SparseCore 0:
  10.2 70.3 all-gather.3
  100.5 61.2 all-gather.5

commit v5 on v4

--- a/solution.py
+++ b/solution.py
@@ -82,35 +82,20 @@
     lax.fori_loop(0, owners, second, 0, unroll=2 * SOURCE_UNROLL)
 
 
-def panel_kernel(
-    owners, slots, place_ref, panel_ref, here_ref, slot_ref, targets_ref, mine_ref, packed_ref, parent_ref,
-    rows_ref, message_ref, q_ref, pick_ref,
-):
+def panel_kernel(place_ref, received_ref, target_ref, parent_ref, rows_ref, message_ref, q_ref):
     parity, grid_pos = place_ref[0], place_ref[1]
-    width = panel_ref.shape[1]
     owned = q_ref.shape[0]
-    half = owned // 2
-    few, more = row_numbers(slots, width), row_numbers(2 * slots, width)
-
-    def select(s, carry):
-        pick = jnp.concatenate([hot(few, here_ref[pl.ds(s, 1), :]), hot(more, slot_ref[0, pl.ds(s, 1), :])], axis=0)
-        found = dot(pick, panel_ref[s]).astype(BF).reshape(3, slots, PW)
-        pick_ref[:, pl.ds(pl.multiple_of(s * slots, 16), slots), :] = found
-        return carry
-
-    lax.fori_loop(0, owners, select, 0, unroll=8)
-    spots = row_numbers(owned, owners * slots)
-    mine = hot(spots, mine_ref[...])
-    q = dot(mine, pick_ref[0]).astype(BF)
+
+    def chosen(rows, kind):
+        at = lax.broadcasted_iota(jnp.int32, (rows, target_ref.shape[1]), 0).astype(F32)
+        pick = jnp.where(at == target_ref[kind : kind + 1, :], 1.0, 0.0).astype(BF)
+        return dot(pick, received_ref[...])
+
+    placed = chosen(owned, 0)
+    q = chosen(owned, 1).astype(BF)
+    pan = chosen(PW, 2).astype(BF)
     q_ref[...] = q
-    placed = dot(mine, packed_ref[...])
-    own, other = [], []
-    for b in range(2):
-        pan = dot(hot(spots, targets_ref[b : b + 1, :]), pick_ref[1 + b]).astype(BF)
-        product = dot(q, pan, NT)
-        own.append(product[:, :half])
-        other.append(product[:, half:])
-    contrib = (placed - jnp.concatenate(own + other, axis=1)).astype(BF).astype(F32)
+    contrib = (placed - dot(q, pan, NT)).astype(BF).astype(F32)
     rows = jnp.concatenate([contrib[:, :owned] + parent_ref[...], contrib[:, owned:]], axis=1)
     rows_ref[...] = rows
     rounded = rows.astype(BF)
@@ -268,9 +253,9 @@
 
 
 def factor_kernel(parity_ref, rows_ref, front_hbm, parent_hbm, *refs):
-    own_hbm, recv_hbm = refs[:CHUNKS], refs[CHUNKS : 2 * CHUNKS]
-    schur_ref, panel_ref, w_ref, s_ref, t_ref, lead_ref, cols_ref, parent_ref = refs[2 * CHUNKS : 2 * CHUNKS + 8]
-    own_ref, recv_ref, sems = refs[2 * CHUNKS + 8 :]
+    own_hbm, recv_hbm = refs[:CHUNKS], refs[CHUNKS : 2 * CHUNKS - 1]
+    schur_ref, panel_ref, w_ref, s_ref, t_ref, lead_ref, cols_ref, parent_ref = refs[2 * CHUNKS - 1 : 2 * CHUNKS + 7]
+    own_ref, recv_ref, sems = refs[2 * CHUNKS + 7 :]
     owned = rows_ref.shape[0]
     half = owned // 2
     strips = parent_ref.shape[0] // owned
@@ -282,7 +267,7 @@
     ]
     for c in range(CHUNKS):
         copies.append(pltpu.make_async_copy(own_hbm[c], own_ref.at[c], sems.at[3 + c]))
-    for c in range(CHUNKS):
+    for c in range(CHUNKS - 1):
         copies.append(pltpu.make_async_copy(recv_hbm[c], recv_ref.at[c], sems.at[3 + CHUNKS + c]))
     for copy in copies:
         copy.start()
@@ -312,11 +297,28 @@
         placed = []
         for c in range(CHUNKS):
             z = dot(unit, own_ref[c, pl.ds(2 * pair, 2)].reshape(2 * half, lanes), NT)
-            placed.append(z + dot(unit, recv_ref[c, pl.ds(2 * pair, 2)].reshape(2 * half, lanes), NT))
+            if c < CHUNKS - 1:
+                z = z + dot(unit, recv_ref[c, pl.ds(2 * pair, 2)].reshape(2 * half, lanes), NT)
+            placed.append(z)
         change = jnp.concatenate(placed, axis=0) - update
         for side in range(2):
             at = pl.ds(2 * pair + side, owned, stride=strips)
             schur_ref[at, :] = parent_ref[at, :] + change[:, side * half : (side + 1) * half]
+
+
+def last_kernel(schur_ref, recv_ref, out_ref):
+    rows = pl.program_id(0)
+    lanes = recv_ref.shape[2]
+    strips = recv_ref.shape[0]
+    part = schur_ref.shape[0] // strips
+    r = lax.broadcasted_iota(jnp.int32, (part, lanes), 0) + rows * part
+    c = lax.broadcasted_iota(jnp.int32, (part, lanes), 1)
+    unit = jnp.where(r == c, 1.0, 0.0).astype(BF)
+    for pair in range(strips // 2):
+        z = dot(unit, recv_ref[pl.ds(2 * pair, 2)].reshape(-1, lanes), NT)
+        for side in range(2):
+            at = pl.ds(2 * pair + side, part, stride=strips)
+            out_ref[at, :] = schur_ref[at, :] + z[:, side * 128 : (side + 1) * 128]
 
 
 def swapped(block):
@@ -360,14 +362,22 @@
     ).astype(F32)
     slot_parts = slot_of[None] - jnp.array([0, total // 2])[:, None, None]
     slot_parts = jnp.where((slot_parts >= 0) & (slot_parts < total // 2), slot_parts, -1).astype(F32)
-    my_slot = lax.dynamic_index_in_dim(slot_of, grid_pos, 0, keepdims=False)
 
     row_flat = row_of.reshape(-1)
     pan_of = jnp.where(row_flat < PW, ((row_flat & 1) ^ parity) * (PW // 2) + (row_flat >> 1), -1)
     block_pan = dot(child_block[0], (pan_of[:, None] == lax.iota(jnp.int32, PW)[None, :]).astype(BF)).astype(BF)
 
-    pack = (lax.iota(jnp.int32, total)[:, None] == my_slot[None, :]).astype(BF)
-    packed = dot(pack, block_pan).astype(BF).reshape(owners, slots, PW)
+    my_owner = lax.dynamic_index_in_dim(owner_of, grid_pos, 0, keepdims=False)
+    my_rank = lax.dynamic_index_in_dim(rank_of, grid_pos, 0, keepdims=False)
+    kinds = 4 * capacity
+    code = my_owner * kinds + my_rank
+    pivot_code = jnp.where(my_owner < 2, (2 + my_owner) * capacity + my_rank, -1)
+    never = jnp.full((width,), -1, jnp.int32)
+    code = jnp.concatenate([code, code + capacity])
+    pivot_code = jnp.concatenate([never, pivot_code])
+    at = lax.iota(jnp.int32, owners * kinds)[:, None]
+    pack = ((at == code[None, :]) | (at % kinds == pivot_code[None, :])).astype(BF)
+    packed = dot(pack, jnp.concatenate([block_pan, own_panel], axis=0)).astype(BF).reshape(owners, kinds, PW)
     packed, slot_parts = lax.optimization_barrier((packed, slot_parts))
     packed = exchanged(packed)
     spread = call(
@@ -377,32 +387,40 @@
         flops=6 * owners * total * width * width,
     )(child_block[0], slot_parts, target_nat.astype(F32))
     packed, spread = lax.optimization_barrier((packed, spread))
-    bulk = [exchanged(spread[0])]
 
     smem, vmem = pl.BlockSpec(memory_space=pltpu.SMEM), pl.BlockSpec(memory_space=pltpu.VMEM)
     place = jnp.stack([parity, grid_pos]).astype(jnp.int32)
-    here = slot_of - grid_pos * slots
-    here = jnp.where((here >= 0) & (here < slots), here, -1).astype(F32)
-    my_target = lax.dynamic_slice_in_dim(target_nat, grid_pos, 1).astype(F32)
+    my_target = lax.dynamic_index_in_dim(target, grid_pos, 0, keepdims=False)[:, :capacity]
+    pivot_target = target[:2, :, :capacity]
+    pivot_pos = jnp.where(
+        pivot_target >= 0,
+        ((pivot_target & 1) ^ parity) * (PW // 2)
+        + lax.iota(jnp.int32, 2)[:, None, None] * half
+        + (pivot_target >> 1),
+        -1,
+    )
+    pivot_pos = pivot_pos.transpose(1, 0, 2).reshape(owners, 2 * capacity)
+    none = jnp.full((owners, capacity), -1, jnp.int32)
+    kind_targets = jnp.stack(
+        [
+            jnp.concatenate([my_target, none, none, none], axis=1),
+            jnp.concatenate([none, my_target, none, none], axis=1),
+            jnp.concatenate([none, none, pivot_pos], axis=1),
+        ]
+    )
+    kind_targets = kind_targets.reshape(3, owners * kinds).astype(F32)
     rows_mine, message, q = call(
-        functools.partial(panel_kernel, owners, slots),
+        panel_kernel,
         [
             jax.ShapeDtypeStruct((owned, PW), F32),
             jax.ShapeDtypeStruct((owned + LOW_ROWS, PW), BF),
             jax.ShapeDtypeStruct((owned, PW), BF),
         ],
-        [pltpu.VMEM((3, total, PW), BF)],
-        flops=4 * owners * width * owned * PW,
-        in_specs=[smem] + [vmem] * 7,
-    )(place, panel_all, here, slot_parts, target_own, my_target, packed.reshape(total, PW), parent_front[:, 0, : PW // 2])
-    product = call(
-        product_kernel,
-        [jax.ShapeDtypeStruct((owners, width, lanes), F32)] * CHUNKS,
-        flops=4 * owners * width * owned * PW,
-    )(panel_all, q)
-    theirs, bulk[0], product = lax.optimization_barrier((swapped(message), bulk[0], product))
-    rest, product = lax.optimization_barrier((spread[1:], product))
-    bulk = bulk + [exchanged(part) for part in rest]
+        flops=8 * owned * owners * kinds * PW,
+        in_specs=[smem] + [vmem] * 3,
+    )(place, packed.reshape(owners * kinds, PW), kind_targets, parent_front[:, 0, : PW // 2])
+    theirs = swapped(message)
+    bulk = [exchanged(spread[0])]
     rows, message = call(
         rows_kernel,
         [
@@ -412,6 +430,14 @@
         in_specs=[smem, vmem, vmem],
     )(place, rows_mine, theirs)
     front_cols = lax.all_gather(message, "grid")
+
+    product = call(
+        product_kernel,
+        [jax.ShapeDtypeStruct((owners, width, lanes), F32)] * CHUNKS,
+        flops=4 * owners * width * owned * PW,
+    )(panel_all, q)
+    rest, product = lax.optimization_barrier((spread[1:], product))
+    bulk = bulk + [exchanged(part) for part in rest]
 
     own_t, other_t = [], []
     for c in range(CHUNKS):
@@ -441,11 +467,11 @@
             pltpu.VMEM((owners, half, PW), BF),
             pltpu.VMEM((owned * strips, 128), F32),
             pltpu.VMEM((CHUNKS, owners, half, lanes), BF),
-            pltpu.VMEM((CHUNKS, owners, half, lanes), BF),
-            pltpu.SemaphoreType.DMA((3 + 2 * CHUNKS,)),
+            pltpu.VMEM((CHUNKS - 1, owners, half, lanes), BF),
+            pltpu.SemaphoreType.DMA((2 + 2 * CHUNKS,)),
         ],
         flops=60 * PW**3,
-        in_specs=[smem, vmem] + [anywhere] * (2 + 2 * CHUNKS),
+        in_specs=[smem, vmem] + [anywhere] * (1 + 2 * CHUNKS),
         out_specs=[vmem, vmem],
     )(
         place,
@@ -453,8 +479,18 @@
         front_cols,
         parent_front.reshape(owned * strips, 128),
         *own_t,
-        *recv_t,
+        *recv_t[:-1],
     )
+    steps = 4
+    last_rows = pl.BlockSpec((lanes * strips // steps, 128), lambda i: ((CHUNKS - 1) * steps + i, 0))
+    schur = call(
+        last_kernel,
+        jax.ShapeDtypeStruct((owned * strips, 128), F32),
+        grid=(steps,),
+        in_specs=[last_rows, pl.BlockSpec((owners, half, lanes), lambda i: (0, 0, 0))],
+        out_specs=last_rows,
+        input_output_aliases={0: 0},
+    )(schur, recv_t[-1])
     return (schur.reshape(owned, 1, half_cols), panel[:, None, :])
 
 

time: 201 us -> 186 us (0.925)
  waiting for transfers between devices: 63 us -> 37.9 us
  local copies, waits for them, and re-layouts: 6.06 us -> 10.3 us
  Pallas kernels: 75.2 us -> 78.7 us
    all_gather x1, waiting for transfers between devices: 24.8 us -> 1.06 us  [shards(): panel_all = lax.all_gather(own_panel, 'grid')]
    ppermute x3, waiting for transfers between devices: 22.4 us -> 5.3 us  [swapped(): return lax.ppermute(block, 'cube', [(i, i ^ 1) for i in range(count)])]
    all_to_all x3, waiting for transfers between devices: 15.1 us -> 30.9 us  [exchanged(): return lax.all_to_all(block, 'grid', 0, 0, tiled=True)]
    pallas_call x1 -> x2, Pallas kernels: 6.73 us -> 10.3 us  [the longest x1 5.83 us: shards(): call(last_kernel, jax.ShapeDtypeStruct((owned * strips, 128), F32), grid=...]
    convert_element_type x0 -> x4, local copies, waits for them, and re-layouts: none -> 2.79 us  [the longest x2 1.87 us: shards(): target_own = jnp.where(target_nat >= 0, (target_nat & 1 ^ parity) * half...]
    unnamed x14 -> x16, local copies, waits for them, and re-layouts: 5.56 us -> 6.81 us
    dot_general x1 -> x2, matrix products: 4.94 us -> 6.09 us  [dot(): lax.dot_general(a, b, dims, precision=precision, preferred_element_type=F32)]
  transfers between devices with their start and end apart: 8 -> 8, of which waited for: 3 -> 5; matrix products, arithmetic and copies ran while one was open for 7% -> 11% of each run, Pallas kernels for 26% -> 40%
where the time goes in v5:
time: 186 us; the launch traced here: 184 us
  Pallas kernels  78.7 us (42%)
  waiting for transfers between devices  37.9 us (20%)
  starting transfers between devices  28.9 us (16%)
  between operations  14.3 us (8%)
  local copies, waits for them, and re-layouts  10.3 us (6%)
  other arithmetic  7.79 us (4%)
  matrix products  6.09 us (3%)
    all_to_all x3, waiting for transfers between devices, exchanged(): return lax.all_to_all(block, 'grid', 0, 0, tiled=True)  30.9 us
    all_to_all x3, starting transfers between devices, exchanged(): return lax.all_to_all(block, 'grid', 0, 0, tiled=True)  24.5 us
    pallas_call x1, Pallas kernels, shards(): call(factor_kernel, [jax.ShapeDtypeStruct((owned * strips, 128), F32), ja...  21.8 us
    pallas_call x2, Pallas kernels, shards(): call(functools.partial(owner_kernel, owners, slots, owned), [jax.ShapeDty...  18.7 us
    pallas_call x1, Pallas kernels, shards(): call(functools.partial(source_kernel, owners, slots, owned), [jax.ShapeDt...  16.8 us
    pallas_call x1, Pallas kernels, shards(): call(product_kernel, [jax.ShapeDtypeStruct((owners, width, lanes), F32)]...  8.88 us
    unnamed x16, local copies, waits for them, and re-layouts  6.81 us
    dot_general x2, matrix products, dot(): lax.dot_general(a, b, dims, precision=precision, preferred_element_type=F32)  6.09 us
  transfers between devices with their start and end apart: 8, of which 5 were waited for; matrix products, arithmetic and copies ran while one was open for 11% of the time, Pallas kernels for 40%

profile of v5, /device:TPU:1, one launch (start us, length us, event | category | flops | bytes accessed | tf_op | source)
XLA Modules:
  0.0 183.9 jit_solution(5663804008692726789)
XLA Ops:
  7.2 0.0 all-gather.4.cloned.1.call-start
  7.2 0.7 all-gather.4.cloned.1.call-update
  7.9 1.0 compare_select_fusion
  8.9 0.1 reshape.248
  9.1 1.4 convert_reduce_fusion
  10.5 0.1 concatenate.21
  10.6 0.1 pad_add_fusion
  10.7 0.7 fusion.13.slot_ref
  11.4 3.9 %fusion.9 = bf16[192,512]{1,0:T(8,128)(2,1)S(1)} fusion(s32[6144]{0:T(1024)S(1)} %bitcast.45, bf16[1,192,6144]{2,1,0:T(8,128)(2,1)} %param.6), kind=kOutput, calls=%fused_computation.14 | convolution fusion | flops 1211203584 | bytes 2580480 | tf_op jit(solution)/shard_map/dot_general | solution.py:23
  15.3 0.0 copy-done.5
  15.3 2.2 %convolution_convert_fusion = bf16[1536,512]{1,0:T(8,128)(2,1)} fusion(s32[384]{0:T(512)S(1)} %concatenate.21, s32[384]{0:T(512)S(1)} %pad_add_fusion, s32[1536]{0:T(1024)S(1)} %add_select_fusion.2, bf16[192,512]{1,0:T(8,128)(2,1)S(1)} %bitcast.43, bf16[192,512]{1,0:T(8,128)(2,1)S(1)} %fusion.9), kind=kOutput, calls=%fused_computation.6 | convolution fusion | flops 607322112 | bytes 1975296 | tf_op jit(solution)/shard_map/dot_general | solution.py:23
  17.5 0.0 slice-start
  17.5 9.6 %all-to-all-start = ((bf16[32,48,512]{2,1,0:T(8,128)(2,1)}), bf16[32,48,512]{2,1,0:T(8,128)(2,1)S(1)}, u32[]{:S(2)}, u32[]{:S(2)}) async-start(bf16[32,48,512]{2,1,0:T(8,128)(2,1)} %bitcast.8), calls=%async_computation | async-start | bytes 3145728 | tf_op jit(solution)/shard_map/all_to_all | solution.py:330
  27.1 0.0 all-gather.6.cloned.1.call-start
  27.2 0.1 pad.8.clone
  27.3 2.3 %select_reduce_fusion = s32[32,512]{1,0:T(8,128)S(1)} fusion(s32[32,192]{1,0:T(8,128)S(1)} %get-tuple-element.62, s32[32,192]{1,0:T(8,128)S(1)} %get-tuple-element.63), kind=kLoop, calls=%fused_computation | loop fusion | flops 9420800 | bytes 114688 | tf_op jit(solution)/shard_map/reduce_sum | solution.py:357
  29.6 0.1 copy.42
  29.8 0.1 copy.55
  29.8 0.1 fusion.23
  29.9 0.1 stack.24
  30.0 0.1 stack.25
  30.1 0.1 select_bitcast_fusion
  30.2 0.1 copy.56
  30.3 0.1 concatenate.25.clone
  30.4 0.1 stack.26
  30.5 0.2 copy.43
  30.7 0.7 copy.44.target_ref
  31.4 0.0 slice-done
  31.4 0.7 copy.58
  32.1 0.6 pad_add_fusion.1.place_ref.parity_ref
  32.7 0.6 add_convert_fusion.target_ref
  33.3 16.8 %shard_map.68 = (bf16[32,192,128]{2,1,0:T(8,128)(2,1)}, bf16[32,192,128]{2,1,0:T(8,128)(2,1)}) custom-call(bf16[192,6144]{1,0:T(8,128)(2,1)} %bitcast.50, f32[2,32,192]{2,1,0:T(8,128)} %fusion.13.slot_ref, f32[32,512]{1,0:T(8,128)} %copy.44.target_ref), custom_call_target="tpu_custom_call" | custom-call | flops 3623878656 | bytes 6291456 | tf_op jit(solution)/shard_map/pallas_call | solution.py:383
  50.1 0.5 all-to-all-done
  50.5 0.0 copy-start
  50.6 1.1 copy-done
  51.7 4.5 %shard_map.69 = (f32[256,512]{1,0:T(8,128)}, bf16[272,512]{1,0:T(8,128)(2,1)}, bf16[256,512]{1,0:T(8,128)(2,1)}) custom-call(s32[2]{0:T(128)} %pad_add_fusion.1.place_ref.parity_ref, bf16[1536,512]{1,0:T(8,128)(2,1)} %bitcast.37, f32[3,1536]{1,0:T(4,128)} %add_convert_fusion.target_ref, f32[256,256]{1,0:T(8,128)} %bitcast.41), custom_call_target="tpu_custom_call" | custom-call | flops 1610612736 | bytes 2129920 | tf_op jit(solution)/shard_map/pallas_call | solution.py:412
  56.2 1.5 collective-permute-start
  57.7 5.3 %collective-permute-done.theirs_ref = bf16[272,512]{1,0:T(8,128)(2,1)S(1)} collective-permute-done((bf16[272,512]{1,0:T(8,128)(2,1)}, bf16[272,512]{1,0:T(8,128)(2,1)S(1)}, u32[]{:S(2)}, u32[]{:S(2)}) %collective-permute-start) | collective-permute-done | bytes 278560 | tf_op jit(solution)/shard_map/ppermute | solution.py:326
  63.0 0.0 copy-start.4
  63.0 0.7 copy-done.4
  63.7 2.2 %shard_map.70 = (f32[256,512]{1,0:T(8,128)}, bf16[208,512]{1,0:T(8,128)(2,1)}) custom-call(s32[2]{0:T(128)} %pad_add_fusion.1.place_ref.parity_ref, f32[256,512]{1,0:T(8,128)} %get-tuple-element.30.mine_ref, bf16[272,512]{1,0:T(8,128)(2,1)} %copy-done.4), custom_call_target="tpu_custom_call" | custom-call | bytes 1474560 | tf_op jit(solution)/shard_map/pallas_call | solution.py:424
  66.0 0.0 all-gather.6.cloned.1.call-update
  66.0 8.9 %all-to-all-start.1 = ((bf16[32,192,128]{2,1,0:T(8,128)(2,1)}), bf16[32,192,128]{2,1,0:T(8,128)(2,1)S(1)}, u32[]{:S(2)}, u32[]{:S(2)}) async-start(bf16[32,192,128]{2,1,0:T(8,128)(2,1)} %get-tuple-element.34), calls=%async_computation.1 | async-start | bytes 3145728 | tf_op jit(solution)/shard_map/all_to_all | solution.py:330
  74.9 1.1 all-gather.4.cloned.1.call-done.panel_ref
  76.0 8.9 %shard_map.71 = (f32[32,192,128]{2,1,0:T(8,128)}, f32[32,192,128]{2,1,0:T(8,128)}) custom-call(bf16[32,192,512]{2,1,0:T(8,128)(2,1)} %all-gather.4.cloned.1.call-done.panel_ref, bf16[256,512]{1,0:T(8,128)(2,1)} %get-tuple-element.36.q_ref), custom_call_target="tpu_custom_call" | custom-call | flops 3221225472 | bytes 12582912 | tf_op jit(solution)/shard_map/pallas_call | solution.py:434
  84.9 13.2 %all-to-all-done.1.recv_ref = bf16[32,192,128]{2,1,0:T(8,128)(2,1)S(1)} async-done(((bf16[32,192,128]{2,1,0:T(8,128)(2,1)}), bf16[32,192,128]{2,1,0:T(8,128)(2,1)S(1)}, u32[]{:S(2)}, u32[]{:S(2)}) %all-to-all-start.1) | async-done | bytes 1572896 | tf_op jit(solution)/shard_map/all_to_all | solution.py:330
  98.0 0.0 copy-start.1
  98.0 6.0 %all-to-all-start.2 = ((bf16[32,192,128]{2,1,0:T(8,128)(2,1)}), bf16[32,192,128]{2,1,0:T(8,128)(2,1)S(1)}, u32[]{:S(2)}, u32[]{:S(2)}) async-start(bf16[32,192,128]{2,1,0:T(8,128)(2,1)} %get-tuple-element.41), calls=%async_computation.2 | async-start | bytes 3145728 | tf_op jit(solution)/shard_map/all_to_all | solution.py:330
  104.0 0.8 select_convert_fusion
  104.8 1.1 copy.49
  105.9 0.7 copy.50.target_ref
  106.7 0.0 copy-done.1
  106.7 9.3 %shard_map.72 = (bf16[32,128,128]{2,1,0:T(8,128)(2,1)}, bf16[32,128,128]{2,1,0:T(8,128)(2,1)}) custom-call(bf16[32,192,128]{2,1,0:T(8,128)(2,1)} %copy-done.1, f32[32,192,128]{2,1,0:T(8,128)} %get-tuple-element.39.product_ref, f32[2,32,192]{2,1,0:T(8,128)} %fusion.13.slot_ref, f32[32,512]{1,0:T(8,128)} %copy.50.target_ref), custom_call_target="tpu_custom_call" | custom-call | flops 3221225472 | bytes 4194304 | tf_op jit(solution)/shard_map/pallas_call | solution.py:444
  116.0 1.3 collective-permute-start.1
  117.3 17.2 %all-to-all-done.2.recv_ref = bf16[32,192,128]{2,1,0:T(8,128)(2,1)S(1)} async-done(((bf16[32,192,128]{2,1,0:T(8,128)(2,1)}), bf16[32,192,128]{2,1,0:T(8,128)(2,1)S(1)}, u32[]{:S(2)}, u32[]{:S(2)}) %all-to-all-start.2) | async-done | bytes 1572896 | tf_op jit(solution)/shard_map/all_to_all | solution.py:330
  134.5 1.1 copy-done.2
  135.7 9.4 %shard_map.73 = (bf16[32,128,128]{2,1,0:T(8,128)(2,1)}, bf16[32,128,128]{2,1,0:T(8,128)(2,1)}) custom-call(bf16[32,192,128]{2,1,0:T(8,128)(2,1)} %copy-done.2, f32[32,192,128]{2,1,0:T(8,128)} %get-tuple-element.42.product_ref, f32[2,32,192]{2,1,0:T(8,128)} %fusion.13.slot_ref, f32[32,512]{1,0:T(8,128)} %copy.50.target_ref), custom_call_target="tpu_custom_call" | custom-call | flops 3221225472 | bytes 4194304 | tf_op jit(solution)/shard_map/pallas_call | solution.py:444
  145.0 1.4 collective-permute-start.2
  146.5 0.0 collective-permute-done.1.refs_2_
  146.5 21.8 %shard_map.74 = (f32[8192,128]{1,0:T(8,128)}, f32[256,256]{1,0:T(8,128)}) custom-call(s32[2]{0:T(128)} %pad_add_fusion.1.place_ref.parity_ref, f32[256,512]{1,0:T(8,128)} %get-tuple-element.32.rows_ref, bf16[32,208,512]{2,1,0:T(8,128)(2,1)} %bitcast.49, f32[8192,128]{1,0:T(8,128)} %bitcast.40, bf16[32,128,128]{2,1,0:T(8,128)(2,1)} %get-tuple-element.40.refs_0_, ...), custom_call_target="tpu_custom_call" | custom-call | flops 8053063680 | bytes 8912896 | tf_op jit(solution)/shard_map/pallas_call | solution.py:456
  168.3 1.9 %copy.53 = f32[256,1,256]{2,1,0:T(1,128)} copy(f32[256,1,256]{2,0,1:T(8,128)} %bitcast.42) | data formatting | bytes 524288
  170.2 0.0 collective-permute-done.2.recv_ref
  170.2 1.0 copy-done.3
  171.3 5.8 %shard_map.75 = f32[8192,128]{1,0:T(8,128)} custom-call(f32[8192,128]{1,0:T(8,128)} %get-tuple-element.45.schur_ref, bf16[32,128,128]{2,1,0:T(8,128)(2,1)} %copy-done.3), custom_call_target="tpu_custom_call", output_to_operand_aliasing={{}: (0, {})} | custom-call | bytes 8388608 | tf_op jit(solution)/shard_map/pallas_call | solution.py:486
  (19 shorter events, 0.2 us)
Async XLA Ops:
  7.2 68.8 %all-gather.4.cloned.1.call-start = ((), (), s32[]{:S(2)}) async-start(), calls=%async_computation.3 | async-start | bytes 6488064 | tf_op jit(solution)/shard_map/all_gather | solution.py:347
  11.4 3.9 %copy-start.5 = (bf16[1,192,512]{2,1,0:T(8,128)(2,1)S(1)}, bf16[1,192,512]{2,1,0:T(8,128)(2,1)}, u32[]{:S(2)}) copy-start(bf16[1,192,512]{2,1,0:T(8,128)(2,1)} %param.7) | copy-start | bytes 589828
  17.5 13.9 %slice-start = ((f32[256,1,4096]{2,1,0:T(1,128)}), f32[256,1,256]{2,1,0:T(1,128)S(1)}, s32[]{:S(2)}) async-start(f32[256,1,4096]{2,1,0:T(1,128)} %param.5), calls=%async_computation.5 | async-start | bytes 524288 | tf_op jit(solution)/shard_map/slice | solution.py:421
  17.5 33.0 %all-to-all-start = ((bf16[32,48,512]{2,1,0:T(8,128)(2,1)}), bf16[32,48,512]{2,1,0:T(8,128)(2,1)S(1)}, u32[]{:S(2)}, u32[]{:S(2)}) async-start(bf16[32,48,512]{2,1,0:T(8,128)(2,1)} %bitcast.8), calls=%async_computation | async-start | bytes 3145728 | tf_op jit(solution)/shard_map/all_to_all | solution.py:330
  27.1 119.4 %all-gather.6.cloned.1.call-start = ((), (), s32[]{:S(2)}) async-start(), calls=%async_computation.4 | async-start | bytes 7028736 | tf_op jit(solution)/shard_map/all_gather | solution.py:432
  50.5 1.1 copy-start
  56.2 6.8 %collective-permute-start = (bf16[272,512]{1,0:T(8,128)(2,1)}, bf16[272,512]{1,0:T(8,128)(2,1)S(1)}, u32[]{:S(2)}, u32[]{:S(2)}) collective-permute-start(bf16[272,512]{1,0:T(8,128)(2,1)} %get-tuple-element.31), channel_id=1, source_target_pairs={{0,32},{32,0},{64,96},{96,64},{1,33},{33,1},{65,97},{97,65},{2,34}... | collective-permute-start | bytes 835592 | tf_op jit(solution)/shard_map/ppermute | solution.py:326
  63.0 0.7 copy-start.4
  66.0 32.0 %all-to-all-start.1 = ((bf16[32,192,128]{2,1,0:T(8,128)(2,1)}), bf16[32,192,128]{2,1,0:T(8,128)(2,1)S(1)}, u32[]{:S(2)}, u32[]{:S(2)}) async-start(bf16[32,192,128]{2,1,0:T(8,128)(2,1)} %get-tuple-element.34), calls=%async_computation.1 | async-start | bytes 3145728 | tf_op jit(solution)/shard_map/all_to_all | solution.py:330
  98.0 8.7 %copy-start.1 = (bf16[32,192,128]{2,1,0:T(8,128)(2,1)}, bf16[32,192,128]{2,1,0:T(8,128)(2,1)S(1)}, u32[]{:S(2)}) copy-start(bf16[32,192,128]{2,1,0:T(8,128)(2,1)S(1)} %all-to-all-done.1.recv_ref) | copy-start | bytes 4718596
  98.0 36.5 %all-to-all-start.2 = ((bf16[32,192,128]{2,1,0:T(8,128)(2,1)}), bf16[32,192,128]{2,1,0:T(8,128)(2,1)S(1)}, u32[]{:S(2)}, u32[]{:S(2)}) async-start(bf16[32,192,128]{2,1,0:T(8,128)(2,1)} %get-tuple-element.41), calls=%async_computation.2 | async-start | bytes 3145728 | tf_op jit(solution)/shard_map/all_to_all | solution.py:330
  116.0 30.5 %collective-permute-start.1 = (bf16[32,128,128]{2,1,0:T(8,128)(2,1)}, bf16[32,128,128]{2,1,0:T(8,128)(2,1)}, u32[]{:S(2)}, u32[]{:S(2)}) collective-permute-start(bf16[32,128,128]{2,1,0:T(8,128)(2,1)} %get-tuple-element.44), channel_id=1, source_target_pairs={{0,32},{32,0},{64,96},{96,64},{1,33},{33,1},{65,97},{97,65},{2,34}... | collective-permute-start | bytes 3145736 | tf_op jit(solution)/shard_map/ppermute | solution.py:326
  134.5 1.1 copy-start.2
  145.0 25.2 %collective-permute-start.2 = (bf16[32,128,128]{2,1,0:T(8,128)(2,1)}, bf16[32,128,128]{2,1,0:T(8,128)(2,1)S(1)}, u32[]{:S(2)}, u32[]{:S(2)}) collective-permute-start(bf16[32,128,128]{2,1,0:T(8,128)(2,1)} %get-tuple-element.46), channel_id=1, source_target_pairs={{0,32},{32,0},{64,96},{96,64},{1,33},{33,1},{65,97},{97,65},{2,34}... | collective-permute-start | bytes 3145736 | tf_op jit(solution)/shard_map/ppermute | solution.py:326
  170.2 1.0 copy-start.3
Sparse Core Ops, SparseCore 0:
  10.2 65.6 all-gather.3
  78.2 62.2 all-gather.5

commit v6 on v5

--- a/solution.py
+++ b/solution.py
@@ -12,6 +12,7 @@
 LOW_ROWS = 16
 SOURCE_UNROLL = 4
 OWNER_UNROLL = 8
+OWNER_COST = 2500
 BF = jnp.bfloat16
 F32 = jnp.float32
 NN = (((1,), (0,)), ((), ()))
@@ -203,6 +204,11 @@
     w_ref[...] = unit - phi * (scaled - unit)
     s_parts = split(scaled)
 
+    w = w_ref[...]
+    w_hi = w.astype(BF)
+    e = dot(dot(w_hi, s_parts[0]).astype(BF), w_hi, NT) - unit
+    w_ref[...] = w - dot((phi * e).astype(BF), w_hi)
+
     def step(state):
         count, _ = state
         w = w_ref[...]
@@ -252,73 +258,45 @@
     return w_ref[...] * scale_row
 
 
-def factor_kernel(parity_ref, rows_ref, front_hbm, parent_hbm, *refs):
-    own_hbm, recv_hbm = refs[:CHUNKS], refs[CHUNKS : 2 * CHUNKS - 1]
-    schur_ref, panel_ref, w_ref, s_ref, t_ref, lead_ref, cols_ref, parent_ref = refs[2 * CHUNKS - 1 : 2 * CHUNKS + 7]
-    own_ref, recv_ref, sems = refs[2 * CHUNKS + 7 :]
+def factor_kernel(place_ref, rows_ref, lead_ref, panel_ref, g_ref, pivot_ref, w_ref, s_ref, t_ref):
     owned = rows_ref.shape[0]
     half = owned // 2
-    strips = parent_ref.shape[0] // owned
     high = lax.Precision.HIGHEST
-    copies = [
-        pltpu.make_async_copy(front_hbm.at[pl.ds(0, 2)], lead_ref, sems.at[0]),
-        pltpu.make_async_copy(front_hbm.at[:, pl.ds(0, half), :], cols_ref, sems.at[1]),
-        pltpu.make_async_copy(parent_hbm, parent_ref, sems.at[2]),
-    ]
-    for c in range(CHUNKS):
-        copies.append(pltpu.make_async_copy(own_hbm[c], own_ref.at[c], sems.at[3 + c]))
-    for c in range(CHUNKS - 1):
-        copies.append(pltpu.make_async_copy(recv_hbm[c], recv_ref.at[c], sems.at[3 + CHUNKS + c]))
-    for copy in copies:
-        copy.start()
-    copies[0].wait()
     top = jnp.concatenate([lead_ref[0, :half], lead_ref[1, :half]], axis=0).astype(F32)
     fold = lead_ref[:, half : half + half // 2].astype(F32)
     corner = jnp.concatenate([fold[b, :, i : i + owned] for b in range(2) for i in (0, owned)], axis=0)
     low = lead_ref[:, half + half // 2 : half + half // 2 + 1].astype(F32)
     bottom = jnp.concatenate([top[:, owned:].T, corner], axis=1)
     pivot = jnp.concatenate([top, bottom], axis=0) + eye(PW) * (low[0] + low[1])
-    lead_cols = split(pivot[: PW // 2])
-    w = inverse_factor(parity_ref[0], pivot, w_ref, s_ref, t_ref)
+    pivot_ref[0], pivot_ref[1] = split(pivot[: PW // 2])
+    w = inverse_factor(place_ref[0], pivot, w_ref, s_ref, t_ref)
     w_ref[...] = w
     factor = dot(rows_ref[...], w, NT, high)
     panel_ref[...] = factor[:, : panel_ref.shape[1]]
-    g_hi, g_lo = split(dot(factor, w_ref[...], NN, high))
-    for copy in copies[1:]:
-        copy.wait()
-    lanes = owned // CHUNKS
-    unit = eye(lanes, BF)
-    for pair in range(strips // 2):
-        cols = cols_ref[pl.ds(2 * pair, 2)].reshape(2 * half, PW)
-        if pair == 0:
-            update = dot3((g_hi, g_lo), lead_cols, NT)
-        else:
-            update = dot(g_hi, cols, NT) + dot(g_lo, cols, NT)
-        placed = []
-        for c in range(CHUNKS):
-            z = dot(unit, own_ref[c, pl.ds(2 * pair, 2)].reshape(2 * half, lanes), NT)
-            if c < CHUNKS - 1:
-                z = z + dot(unit, recv_ref[c, pl.ds(2 * pair, 2)].reshape(2 * half, lanes), NT)
-            placed.append(z)
-        change = jnp.concatenate(placed, axis=0) - update
-        for side in range(2):
-            at = pl.ds(2 * pair + side, owned, stride=strips)
-            schur_ref[at, :] = parent_ref[at, :] + change[:, side * half : (side + 1) * half]
-
-
-def last_kernel(schur_ref, recv_ref, out_ref):
-    rows = pl.program_id(0)
-    lanes = recv_ref.shape[2]
-    strips = recv_ref.shape[0]
-    part = schur_ref.shape[0] // strips
-    r = lax.broadcasted_iota(jnp.int32, (part, lanes), 0) + rows * part
-    c = lax.broadcasted_iota(jnp.int32, (part, lanes), 1)
+    g_ref[0], g_ref[1] = split(dot(factor, w_ref[...], NN, high))
+
+
+def update_kernel(g_ref, pivot_ref, cols_ref, parent_ref, own_ref, recv_ref, *refs):
+    schur_ref = refs[-1]
+    rows = g_ref.shape[1]
+    strips, half, lanes = own_ref.shape
+    both = jnp.concatenate([g_ref[0], g_ref[1]], axis=0)
+    r = lax.broadcasted_iota(jnp.int32, (rows, lanes), 0) + pl.program_id(0) * rows
+    c = lax.broadcasted_iota(jnp.int32, (rows, lanes), 1)
     unit = jnp.where(r == c, 1.0, 0.0).astype(BF)
     for pair in range(strips // 2):
-        z = dot(unit, recv_ref[pl.ds(2 * pair, 2)].reshape(-1, lanes), NT)
+        if pair == 0:
+            update = dot(both, pivot_ref[0], NT)
+            update = update[:rows] + update[rows:] + dot(g_ref[0], pivot_ref[1], NT)
+        else:
+            update = dot(both, cols_ref[pl.ds(2 * pair, 2)].reshape(2 * half, PW), NT)
+            update = update[:rows] + update[rows:]
+        own = own_ref[pl.ds(2 * pair, 2)].reshape(2 * half, lanes)
+        recv = recv_ref[pl.ds(2 * pair, 2)].reshape(2 * half, lanes)
+        change = dot(unit, own, NT) + dot(unit, recv, NT) - update
         for side in range(2):
-            at = pl.ds(2 * pair + side, part, stride=strips)
-            out_ref[at, :] = schur_ref[at, :] + z[:, side * 128 : (side + 1) * 128]
+            at = pl.ds(2 * pair + side, rows, stride=strips)
+            schur_ref[at, :] = parent_ref[at, :] + change[:, side * half : (side + 1) * half]
 
 
 def swapped(block):
@@ -445,52 +423,62 @@
             functools.partial(owner_kernel, owners, slots, owned),
             [jax.ShapeDtypeStruct((owners, half, lanes), BF)] * 2,
             [pltpu.VMEM((owners, total, lanes), BF)],
-            flops=8 * owners * total * width * lanes,
+            flops=OWNER_COST * owners * total * width * lanes,
         )(bulk[c], product[c], slot_parts, target_own)
         own_t.append(a)
         other_t.append(b)
     recv_t = [swapped(x) for x in other_t]
 
     strips = half_cols // 128
-    anywhere = pl.BlockSpec(memory_space=pl.ANY)
-    schur, panel = call(
+    lead_rows = half + half // 2 + LOW_ROWS
+    square = pltpu.VMEM((PW, PW), F32)
+    panel, g, pivot = call(
         factor_kernel,
         [
-            jax.ShapeDtypeStruct((owned * strips, 128), F32),
             jax.ShapeDtypeStruct((owned, PW // 2), F32),
+            jax.ShapeDtypeStruct((2, owned, PW), BF),
+            jax.ShapeDtypeStruct((2, PW // 2, PW), BF),
         ],
-        [
-            pltpu.VMEM((PW, PW), F32),
-            pltpu.VMEM((PW, PW), F32),
-            pltpu.VMEM((PW, PW), F32),
-            pltpu.VMEM((2, half + half // 2 + LOW_ROWS, PW), BF),
-            pltpu.VMEM((owners, half, PW), BF),
-            pltpu.VMEM((owned * strips, 128), F32),
-            pltpu.VMEM((CHUNKS, owners, half, lanes), BF),
-            pltpu.VMEM((CHUNKS - 1, owners, half, lanes), BF),
-            pltpu.SemaphoreType.DMA((2 + 2 * CHUNKS,)),
+        [square, square, square],
+        flops=60 * PW**3,
+        grid=(1,),
+        in_specs=[smem, pl.BlockSpec((owned, PW), lambda i: (0, 0)), pl.BlockSpec((2, lead_rows, PW), lambda i: (0, 0, 0))],
+        out_specs=[
+            pl.BlockSpec((owned, PW // 2), lambda i: (0, 0)),
+            pl.BlockSpec((2, owned, PW), lambda i: (0, 0, 0)),
+            pl.BlockSpec((2, PW // 2, PW), lambda i: (0, 0, 0)),
         ],
-        flops=60 * PW**3,
-        in_specs=[smem, vmem] + [anywhere] * (1 + 2 * CHUNKS),
-        out_specs=[vmem, vmem],
-    )(
-        place,
-        rows,
-        front_cols,
-        parent_front.reshape(owned * strips, 128),
-        *own_t,
-        *recv_t[:-1],
-    )
-    steps = 4
-    last_rows = pl.BlockSpec((lanes * strips // steps, 128), lambda i: ((CHUNKS - 1) * steps + i, 0))
-    schur = call(
-        last_kernel,
-        jax.ShapeDtypeStruct((owned * strips, 128), F32),
-        grid=(steps,),
-        in_specs=[last_rows, pl.BlockSpec((owners, half, lanes), lambda i: (0, 0, 0))],
-        out_specs=last_rows,
-        input_output_aliases={0: 0},
-    )(schur, recv_t[-1])
+    )(place, rows, front_cols)
+    parent_rows = parent_front.reshape(owned * strips, 128)
+    steps = 2
+    schur = []
+    for c in range(CHUNKS):
+
+        def part(i, c=c):
+            return c * steps + i
+
+        row_block = pl.BlockSpec((lanes * strips // steps, 128), lambda i: (part(i), 0))
+        chunk_block = pl.BlockSpec((owners, half, lanes), lambda i: (0, 0, 0))
+        schur = [
+            call(
+                update_kernel,
+                jax.ShapeDtypeStruct((owned * strips, 128), F32),
+                flops=16 * lanes * half_cols * PW,
+                grid=(steps,),
+                in_specs=[
+                    pl.BlockSpec((2, lanes // steps, PW), lambda i: (0, part(i), 0)),
+                    pl.BlockSpec((2, PW // 2, PW), lambda i: (0, 0, 0)),
+                    pl.BlockSpec((owners, half, PW), lambda i: (0, 0, 0)),
+                    row_block,
+                    chunk_block,
+                    chunk_block,
+                ]
+                + [pl.BlockSpec(memory_space=pl.ANY)] * len(schur),
+                out_specs=row_block,
+                input_output_aliases={6: 0} if schur else {},
+            )(g, pivot, front_cols, parent_rows, own_t[c], recv_t[c], *schur)
+        ]
+    schur = schur[0]
     return (schur.reshape(owned, 1, half_cols), panel[:, None, :])
 
 

time: 186 us -> 195 us (1.048)
  waiting for transfers between devices: 37.9 us -> 52.6 us
  starting transfers between devices: 28.9 us -> 24.7 us
  Pallas kernels: 78.7 us -> 81.4 us
  local copies, waits for them, and re-layouts: 10.3 us -> 8.18 us
    all_gather x1, waiting for transfers between devices: 1.06 us -> 14.9 us  [shards(): panel_all = lax.all_gather(own_panel, 'grid')]
    all_gather x1, waiting for transfers between devices: 0.01 us -> 13.5 us  [shards(): front_cols = lax.all_gather(message, 'grid')]
    all_to_all x3, waiting for transfers between devices: 30.9 us -> 17.5 us  [exchanged(): return lax.all_to_all(block, 'grid', 0, 0, tiled=True)]
    all_to_all x3, starting transfers between devices: 24.5 us -> 21.1 us  [exchanged(): return lax.all_to_all(block, 'grid', 0, 0, tiled=True)]
    pallas_call x2 -> x3, Pallas kernels: 27.7 us -> 30.6 us  [the longest x2 19.3 us: shards(): call(update_kernel, jax.ShapeDtypeStruct((owned * strips, 128), F32), flo...]
    unnamed x16 -> x14, local copies, waits for them, and re-layouts: 6.81 us -> 5.63 us
  transfers between devices with their start and end apart: 8 -> 8, of which waited for: 5 -> 5; matrix products, arithmetic and copies ran while one was open for 11% -> 10% of each run, Pallas kernels for 40% -> 37%
where the time goes in v6:
time: 195 us; the launch traced here: 194 us
  Pallas kernels  81.4 us (42%)
  waiting for transfers between devices  52.6 us (27%)
  starting transfers between devices  24.7 us (13%)
  between operations  14.3 us (7%)
  local copies, waits for them, and re-layouts  8.18 us (4%)
  other arithmetic  7.12 us (4%)
  matrix products  6.09 us (3%)
    all_to_all x3, starting transfers between devices, exchanged(): return lax.all_to_all(block, 'grid', 0, 0, tiled=True)  21.1 us
    pallas_call x2, Pallas kernels, shards(): call(update_kernel, jax.ShapeDtypeStruct((owned * strips, 128), F32), flo...  19.3 us
    pallas_call x2, Pallas kernels, shards(): call(functools.partial(owner_kernel, owners, slots, owned), [jax.ShapeDty...  18.6 us
    all_to_all x3, waiting for transfers between devices, exchanged(): return lax.all_to_all(block, 'grid', 0, 0, tiled=True)  17.5 us
    pallas_call x1, Pallas kernels, shards(): call(functools.partial(source_kernel, owners, slots, owned), [jax.ShapeDt...  16.7 us
    all_gather x1, waiting for transfers between devices, shards(): panel_all = lax.all_gather(own_panel, 'grid')  14.9 us
    all_gather x1, waiting for transfers between devices, shards(): front_cols = lax.all_gather(message, 'grid')  13.5 us
    pallas_call x1, Pallas kernels, shards(): call(factor_kernel, [jax.ShapeDtypeStruct((owned, PW // 2), F32), jax.Sha...  11.3 us
  transfers between devices with their start and end apart: 8, of which 5 were waited for; matrix products, arithmetic and copies ran while one was open for 10% of the time, Pallas kernels for 37%

profile of v6, /device:TPU:1, one launch (start us, length us, event | category | flops | bytes accessed | tf_op | source)
XLA Modules:
  0.0 194.4 jit_solution(10971094039372078786)
XLA Ops:
  7.2 0.0 all-gather.4.cloned.1.call-start
  7.2 0.7 all-gather.4.cloned.1.call-update
  7.9 1.0 compare_select_fusion
  8.9 0.1 reshape.248
  9.1 1.4 convert_reduce_fusion
  10.5 0.1 concatenate.21
  10.6 0.1 pad_add_fusion
  10.7 0.7 fusion.13.slot_ref
  11.4 0.0 copy-start.4
  11.4 3.9 %fusion.9 = bf16[192,512]{1,0:T(8,128)(2,1)S(1)} fusion(s32[6144]{0:T(1024)S(1)} %bitcast.50, bf16[1,192,6144]{2,1,0:T(8,128)(2,1)} %param.6), kind=kOutput, calls=%fused_computation.14 | convolution fusion | flops 1211203584 | bytes 2580480 | tf_op jit(solution)/shard_map/dot_general | solution.py:24
  15.3 0.0 copy-done.4
  15.3 2.2 %convolution_convert_fusion = bf16[1536,512]{1,0:T(8,128)(2,1)} fusion(s32[384]{0:T(512)S(1)} %concatenate.21, s32[384]{0:T(512)S(1)} %pad_add_fusion, s32[1536]{0:T(1024)S(1)} %add_select_fusion.2, bf16[192,512]{1,0:T(8,128)(2,1)S(1)} %bitcast.48, bf16[192,512]{1,0:T(8,128)(2,1)S(1)} %fusion.9), kind=kOutput, calls=%fused_computation.6 | convolution fusion | flops 607322112 | bytes 1975296 | tf_op jit(solution)/shard_map/dot_general | solution.py:24
  17.5 9.4 %all-to-all-start = ((bf16[32,48,512]{2,1,0:T(8,128)(2,1)}), bf16[32,48,512]{2,1,0:T(8,128)(2,1)S(1)}, u32[]{:S(2)}, u32[]{:S(2)}) async-start(bf16[32,48,512]{2,1,0:T(8,128)(2,1)} %bitcast.43), calls=%async_computation | async-start | bytes 3145728 | tf_op jit(solution)/shard_map/all_to_all | solution.py:308
  27.0 0.1 pad.8.clone
  27.1 2.3 %select_reduce_fusion = s32[32,512]{1,0:T(8,128)S(1)} fusion(s32[32,192]{1,0:T(8,128)S(1)} %get-tuple-element.64, s32[32,192]{1,0:T(8,128)S(1)} %get-tuple-element.65), kind=kLoop, calls=%fused_computation | loop fusion | flops 9420800 | bytes 114688 | tf_op jit(solution)/shard_map/reduce_sum | solution.py:335
  29.4 0.1 copy.42
  29.6 0.1 copy.55
  29.7 0.2 copy.43
  29.9 0.7 copy.44.target_ref
  30.6 16.7 %shard_map.68 = (bf16[32,192,128]{2,1,0:T(8,128)(2,1)}, bf16[32,192,128]{2,1,0:T(8,128)(2,1)}) custom-call(bf16[192,6144]{1,0:T(8,128)(2,1)} %bitcast.54, f32[2,32,192]{2,1,0:T(8,128)} %fusion.13.slot_ref, f32[32,512]{1,0:T(8,128)} %copy.44.target_ref), custom_call_target="tpu_custom_call" | custom-call | flops 3623878656 | bytes 6291456 | tf_op jit(solution)/shard_map/pallas_call | solution.py:361
  47.3 0.0 slice-start
  47.3 3.0 %all-to-all-done = bf16[32,48,512]{2,1,0:T(8,128)(2,1)S(1)} async-done(((bf16[32,48,512]{2,1,0:T(8,128)(2,1)}), bf16[32,48,512]{2,1,0:T(8,128)(2,1)S(1)}, u32[]{:S(2)}, u32[]{:S(2)}) %all-to-all-start) | async-done | bytes 1572896 | tf_op jit(solution)/shard_map/all_to_all | solution.py:308
  50.3 0.0 copy-start.1
  50.4 1.1 copy-done.1
  51.5 5.7 %all-to-all-start.2 = ((bf16[32,192,128]{2,1,0:T(8,128)(2,1)}), bf16[32,192,128]{2,1,0:T(8,128)(2,1)S(1)}, u32[]{:S(2)}, u32[]{:S(2)}) async-start(bf16[32,192,128]{2,1,0:T(8,128)(2,1)} %get-tuple-element.45), calls=%async_computation.2 | async-start | bytes 3145728 | tf_op jit(solution)/shard_map/all_to_all | solution.py:308
  57.2 0.0 all-gather.6.cloned.1.call-start
  57.2 0.1 fusion.23
  57.3 0.1 stack.24
  57.4 0.1 stack.25
  57.5 0.1 select_bitcast_fusion
  57.6 0.1 copy.56
  57.7 0.1 concatenate.25.clone
  57.7 0.1 stack.26
  57.8 0.0 slice-done
  57.8 0.7 copy.58
  58.6 0.6 pad_add_fusion.1.place_ref
  59.2 0.6 add_convert_fusion.target_ref
  59.8 4.5 %shard_map.69 = (f32[256,512]{1,0:T(8,128)}, bf16[272,512]{1,0:T(8,128)(2,1)}, bf16[256,512]{1,0:T(8,128)(2,1)}) custom-call(s32[2]{0:T(128)} %pad_add_fusion.1.place_ref, bf16[1536,512]{1,0:T(8,128)(2,1)} %bitcast.42, f32[3,1536]{1,0:T(4,128)} %add_convert_fusion.target_ref, f32[256,256]{1,0:T(8,128)} %bitcast.46), custom_call_target="tpu_custom_call" | custom-call | flops 1610612736 | bytes 2129920 | tf_op jit(solution)/shard_map/pallas_call | solution.py:390
  64.3 1.1 collective-permute-start
  65.4 0.1 select_convert_fusion
  65.5 0.2 copy.49
  65.7 0.7 copy.50.target_ref
  66.4 6.1 %collective-permute-done.theirs_ref = bf16[272,512]{1,0:T(8,128)(2,1)S(1)} collective-permute-done((bf16[272,512]{1,0:T(8,128)(2,1)}, bf16[272,512]{1,0:T(8,128)(2,1)S(1)}, u32[]{:S(2)}, u32[]{:S(2)}) %collective-permute-start) | collective-permute-done | bytes 278560 | tf_op jit(solution)/shard_map/ppermute | solution.py:304
  72.5 0.7 copy-done.3
  73.2 2.2 %shard_map.70 = (f32[256,512]{1,0:T(8,128)}, bf16[208,512]{1,0:T(8,128)(2,1)}) custom-call(s32[2]{0:T(128)} %pad_add_fusion.1.place_ref, f32[256,512]{1,0:T(8,128)} %get-tuple-element.31.mine_ref, bf16[272,512]{1,0:T(8,128)(2,1)} %copy-done.3), custom_call_target="tpu_custom_call" | custom-call | bytes 1474560 | tf_op jit(solution)/shard_map/pallas_call | solution.py:402
  75.4 0.0 all-gather.6.cloned.1.call-update
  75.4 14.9 %all-gather.4.cloned.1.call-done.panel_ref = bf16[32,192,512]{2,1,0:T(8,128)(2,1)} async-done(((bf16[1,192,512]{2,1,0:T(8,128)(2,1)}), bf16[32,192,512]{2,1,0:T(8,128)(2,1)}) %all-gather.4.cloned.1.call-update) | async-done | bytes 6291472 | tf_op jit(solution)/shard_map/all_gather | solution.py:325
  90.3 8.9 %shard_map.72 = (f32[32,192,128]{2,1,0:T(8,128)}, f32[32,192,128]{2,1,0:T(8,128)}) custom-call(bf16[32,192,512]{2,1,0:T(8,128)(2,1)} %all-gather.4.cloned.1.call-done.panel_ref, bf16[256,512]{1,0:T(8,128)(2,1)} %get-tuple-element.38.q_ref), custom_call_target="tpu_custom_call" | custom-call | flops 3221225472 | bytes 12582912 | tf_op jit(solution)/shard_map/pallas_call | solution.py:412
  99.1 0.0 all-to-all-done.2.recv_ref
  99.2 5.9 %all-to-all-start.1 = ((bf16[32,192,128]{2,1,0:T(8,128)(2,1)}), bf16[32,192,128]{2,1,0:T(8,128)(2,1)}, u32[]{:S(2)}, u32[]{:S(2)}) async-start(bf16[32,192,128]{2,1,0:T(8,128)(2,1)} %get-tuple-element.41), calls=%async_computation.1 | async-start | bytes 3145728 | tf_op jit(solution)/shard_map/all_to_all | solution.py:308
  105.1 0.0 copy-done
  105.1 9.3 %shard_map.74 = (bf16[32,128,128]{2,1,0:T(8,128)(2,1)}, bf16[32,128,128]{2,1,0:T(8,128)(2,1)}) custom-call(bf16[32,192,128]{2,1,0:T(8,128)(2,1)} %copy-done, f32[32,192,128]{2,1,0:T(8,128)} %get-tuple-element.46.product_ref, f32[2,32,192]{2,1,0:T(8,128)} %fusion.13.slot_ref, f32[32,512]{1,0:T(8,128)} %copy.50.target_ref), custom_call_target="tpu_custom_call" | custom-call | flops 1006632960000 | bytes 4194304 | tf_op jit(solution)/shard_map/pallas_call | solution.py:422
  114.4 1.2 collective-permute-start.2
  115.6 14.4 %all-to-all-done.1.recv_ref = bf16[32,192,128]{2,1,0:T(8,128)(2,1)} async-done(((bf16[32,192,128]{2,1,0:T(8,128)(2,1)}), bf16[32,192,128]{2,1,0:T(8,128)(2,1)}, u32[]{:S(2)}, u32[]{:S(2)}) %all-to-all-start.1) | async-done | bytes 1572896 | tf_op jit(solution)/shard_map/all_to_all | solution.py:308
  130.0 9.3 %shard_map.73 = (bf16[32,128,128]{2,1,0:T(8,128)(2,1)}, bf16[32,128,128]{2,1,0:T(8,128)(2,1)}) custom-call(bf16[32,192,128]{2,1,0:T(8,128)(2,1)} %all-to-all-done.1.recv_ref, f32[32,192,128]{2,1,0:T(8,128)} %get-tuple-element.42.product_ref, f32[2,32,192]{2,1,0:T(8,128)} %fusion.13.slot_ref, f32[32,512]{1,0:T(8,128)} %copy.50.target_ref), custom_call_target="tpu_custom_call" | custom-call | flops 1006632960000 | bytes 4194304 | tf_op jit(solution)/shard_map/pallas_call | solution.py:422
  139.3 1.2 collective-permute-start.1
  140.5 13.5 %all-gather.6.cloned.1.call-done = bf16[6656,512]{1,0:T(8,128)(2,1)} async-done(((bf16[208,512]{1,0:T(8,128)(2,1)}), bf16[6656,512]{1,0:T(8,128)(2,1)}) %all-gather.6.cloned.1.call-update) | async-done | bytes 6815760 | tf_op jit(solution)/shard_map/all_gather | solution.py:410
  154.0 11.3 %shard_map.71 = (f32[256,256]{1,0:T(8,128)}, bf16[2,256,512]{2,1,0:T(8,128)(2,1)}, bf16[2,256,512]{2,1,0:T(8,128)(2,1)}) custom-call(s32[2]{0:T(128)} %pad_add_fusion.1.place_ref, f32[256,512]{1,0:T(8,128)} %get-tuple-element.33.rows_ref, bf16[32,208,512]{2,1,0:T(8,128)(2,1)} %bitcast.32), custom_call_target="tpu_custom_call" | custom-call | flops 8053063680 | bytes 2621440 | tf_op jit(solution)/shard_map/pallas_call | solution.py:435
  165.3 1.9 copy.53
  167.3 0.0 collective-permute-done.2.recv_ref
  167.3 9.6 %shard_map.75.refs_0_ = f32[8192,128]{1,0:T(8,128)} custom-call(bf16[2,256,512]{2,1,0:T(8,128)(2,1)} %get-tuple-element.35.g_ref, bf16[2,256,512]{2,1,0:T(8,128)(2,1)} %get-tuple-element.36.pivot_ref, bf16[32,208,512]{2,1,0:T(8,128)(2,1)} %bitcast.33, f32[8192,128]{1,0:T(8,128)} %bitcast.35, bf16[32,128,128]{2,1,0:T(8,128)(2,1)} %get-tuple-element.47.own_ref, ...), custom_call_target="tpu_custom_call" | custom-call | flops 4294967296 | bytes 8388608 | tf_op jit(solution)/shard_map/pallas_call | solution.py:463
  176.9 0.0 collective-permute-done.1.recv_ref
  176.9 1.0 copy-done.2
  177.9 9.7 %shard_map.76 = f32[8192,128]{1,0:T(8,128)} custom-call(bf16[2,256,512]{2,1,0:T(8,128)(2,1)} %get-tuple-element.35.g_ref, bf16[2,256,512]{2,1,0:T(8,128)(2,1)} %get-tuple-element.36.pivot_ref, bf16[32,208,512]{2,1,0:T(8,128)(2,1)} %bitcast.34, f32[8192,128]{1,0:T(8,128)} %bitcast.36, ...), custom_call_target="tpu_custom_call", output_to_operand_aliasing={{}: (6, {})} | custom-call | flops 4294967296 | bytes 8388608 | tf_op jit(solution)/shard_map/pallas_call | solution.py:463
  (18 shorter events, 0.2 us)
Async XLA Ops:
  7.2 83.1 %all-gather.4.cloned.1.call-start = ((), (), s32[]{:S(2)}) async-start(), calls=%async_computation.3 | async-start | bytes 6488064 | tf_op jit(solution)/shard_map/all_gather | solution.py:325
  11.4 3.9 %copy-start.4 = (bf16[1,192,512]{2,1,0:T(8,128)(2,1)S(1)}, bf16[1,192,512]{2,1,0:T(8,128)(2,1)}, u32[]{:S(2)}) copy-start(bf16[1,192,512]{2,1,0:T(8,128)(2,1)} %param.7) | copy-start | bytes 589828
  17.5 32.8 %all-to-all-start = ((bf16[32,48,512]{2,1,0:T(8,128)(2,1)}), bf16[32,48,512]{2,1,0:T(8,128)(2,1)S(1)}, u32[]{:S(2)}, u32[]{:S(2)}) async-start(bf16[32,48,512]{2,1,0:T(8,128)(2,1)} %bitcast.43), calls=%async_computation | async-start | bytes 3145728 | tf_op jit(solution)/shard_map/all_to_all | solution.py:308
  47.3 10.5 %slice-start = ((f32[256,1,4096]{2,1,0:T(1,128)}), f32[256,1,256]{2,1,0:T(1,128)S(1)}, s32[]{:S(2)}) async-start(f32[256,1,4096]{2,1,0:T(1,128)} %param.5), calls=%async_computation.5 | async-start | bytes 524288 | tf_op jit(solution)/shard_map/slice | solution.py:399
  50.3 1.1 copy-start.1
  51.5 47.7 %all-to-all-start.2 = ((bf16[32,192,128]{2,1,0:T(8,128)(2,1)}), bf16[32,192,128]{2,1,0:T(8,128)(2,1)S(1)}, u32[]{:S(2)}, u32[]{:S(2)}) async-start(bf16[32,192,128]{2,1,0:T(8,128)(2,1)} %get-tuple-element.45), calls=%async_computation.2 | async-start | bytes 3145728 | tf_op jit(solution)/shard_map/all_to_all | solution.py:308
  57.2 96.9 %all-gather.6.cloned.1.call-start = ((), (), s32[]{:S(2)}) async-start(), calls=%async_computation.4 | async-start | bytes 7028736 | tf_op jit(solution)/shard_map/all_gather | solution.py:410
  64.3 8.2 %collective-permute-start = (bf16[272,512]{1,0:T(8,128)(2,1)}, bf16[272,512]{1,0:T(8,128)(2,1)S(1)}, u32[]{:S(2)}, u32[]{:S(2)}) collective-permute-start(bf16[272,512]{1,0:T(8,128)(2,1)} %get-tuple-element.32), channel_id=1, source_target_pairs={{0,32},{32,0},{64,96},{96,64},{1,33},{33,1},{65,97},{97,65},{2,34}... | collective-permute-start | bytes 835592 | tf_op jit(solution)/shard_map/ppermute | solution.py:304
  72.5 0.7 copy-start.3
  99.1 6.0 %copy-start = (bf16[32,192,128]{2,1,0:T(8,128)(2,1)}, bf16[32,192,128]{2,1,0:T(8,128)(2,1)S(1)}, u32[]{:S(2)}) copy-start(bf16[32,192,128]{2,1,0:T(8,128)(2,1)S(1)} %all-to-all-done.2.recv_ref) | copy-start | bytes 4718596
  99.2 30.9 %all-to-all-start.1 = ((bf16[32,192,128]{2,1,0:T(8,128)(2,1)}), bf16[32,192,128]{2,1,0:T(8,128)(2,1)}, u32[]{:S(2)}, u32[]{:S(2)}) async-start(bf16[32,192,128]{2,1,0:T(8,128)(2,1)} %get-tuple-element.41), calls=%async_computation.1 | async-start | bytes 3145728 | tf_op jit(solution)/shard_map/all_to_all | solution.py:308
  114.4 52.9 %collective-permute-start.2 = (bf16[32,128,128]{2,1,0:T(8,128)(2,1)}, bf16[32,128,128]{2,1,0:T(8,128)(2,1)}, u32[]{:S(2)}, u32[]{:S(2)}) collective-permute-start(bf16[32,128,128]{2,1,0:T(8,128)(2,1)} %get-tuple-element.48), channel_id=1, source_target_pairs={{0,32},{32,0},{64,96},{96,64},{1,33},{33,1},{65,97},{97,65},{2,34}... | collective-permute-start | bytes 3145736 | tf_op jit(solution)/shard_map/ppermute | solution.py:304
  139.3 37.5 %collective-permute-start.1 = (bf16[32,128,128]{2,1,0:T(8,128)(2,1)}, bf16[32,128,128]{2,1,0:T(8,128)(2,1)S(1)}, u32[]{:S(2)}, u32[]{:S(2)}) collective-permute-start(bf16[32,128,128]{2,1,0:T(8,128)(2,1)} %get-tuple-element.44), channel_id=1, source_target_pairs={{0,32},{32,0},{64,96},{96,64},{1,33},{33,1},{65,97},{97,65},{2,34}... | collective-permute-start | bytes 3145736 | tf_op jit(solution)/shard_map/ppermute | solution.py:304
  176.9 1.0 copy-start.2
Sparse Core Ops, SparseCore 0:
  10.2 79.9 all-gather.3
  93.1 60.8 all-gather.5

commit v7 on v5

--- a/solution.py
+++ b/solution.py
@@ -11,7 +11,6 @@
 CHUNKS = 2
 LOW_ROWS = 16
 SOURCE_UNROLL = 4
-OWNER_UNROLL = 8
 BF = jnp.bfloat16
 F32 = jnp.float32
 NN = (((1,), (0,)), ((), ()))
@@ -131,44 +130,41 @@
 
 
 def product_kernel(panel_ref, q_ref, *outs):
-    owners = panel_ref.shape[0]
     lanes = q_ref.shape[0] // CHUNKS
     q = q_ref[...]
-
-    def first(s, carry):
+    for s in range(panel_ref.shape[0]):
         product = dot(panel_ref[s], q, NT)
         for c in range(CHUNKS):
             outs[c][s] = product[:, c * lanes : (c + 1) * lanes]
-        return carry
-
-    lax.fori_loop(0, owners, first, 0, unroll=8)
 
 
 def owner_kernel(owners, slots, owned, recv_ref, product_ref, slot_ref, target_ref, own_ref, other_ref, y_ref):
-    width, lanes = recv_ref.shape[1:]
+    group, width, lanes = recv_ref.shape
     part = owners * slots // 2
-    numbers = row_numbers(part, width)
-
-    def first(s, carry):
-        contrib = (recv_ref[s].astype(F32) - product_ref[s]).astype(BF)
-        for b in range(2):
-            y = dot(hot(numbers, slot_ref[b, pl.ds(s, 1), :]), contrib).astype(BF)
-            y_ref[pl.ds(b * (owners // 2), owners // 2), pl.ds(pl.multiple_of(s * slots, 16), slots), :] = y.reshape(
-                owners // 2, slots, lanes
-            )
-        return carry
-
-    lax.fori_loop(0, owners, first, 0, unroll=OWNER_UNROLL)
     half = owned // 2
-    spots = row_numbers(owned, owners * slots)
-
-    def second(owner, carry):
-        z = dot(hot(spots, target_ref[pl.ds(owner, 1), :]), y_ref[owner]).astype(BF)
-        own_ref[owner] = z[:half]
-        other_ref[owner] = z[half:]
-        return carry
-
-    lax.fori_loop(0, owners, second, 0, unroll=OWNER_UNROLL)
+    phases = owners // group
+    at = pl.program_id(0)
+
+    @pl.when(at < phases)
+    def _():
+        numbers = row_numbers(part, width)
+        for i in range(group):
+            s = at * group + i
+            contrib = (recv_ref[i].astype(F32) - product_ref[i]).astype(BF)
+            for b in range(2):
+                y = dot(hot(numbers, slot_ref[b, pl.ds(s, 1), :]), contrib).astype(BF)
+                y_ref[pl.ds(b * (owners // 2), owners // 2), pl.ds(pl.multiple_of(s * slots, 16), slots), :] = y.reshape(
+                    owners // 2, slots, lanes
+                )
+
+    @pl.when(at >= phases)
+    def _():
+        spots = row_numbers(owned, owners * slots)
+        for i in range(group):
+            owner = (at - phases) * group + i
+            z = dot(hot(spots, target_ref[pl.ds(owner, 1), :]), y_ref[owner]).astype(BF)
+            own_ref[i] = z[:half]
+            other_ref[i] = z[half:]
 
 
 def split(x):
@@ -202,6 +198,11 @@
     s_ref[...] = scaled
     w_ref[...] = unit - phi * (scaled - unit)
     s_parts = split(scaled)
+
+    w = w_ref[...]
+    w_hi = w.astype(BF)
+    e = dot(dot(w_hi, s_parts[0]).astype(BF), w_hi, NT) - unit
+    w_ref[...] = w - dot((phi * e).astype(BF), w_hi)
 
     def step(state):
         count, _ = state
@@ -282,7 +283,8 @@
     w = inverse_factor(parity_ref[0], pivot, w_ref, s_ref, t_ref)
     w_ref[...] = w
     factor = dot(rows_ref[...], w, NT, high)
-    panel_ref[...] = factor[:, : panel_ref.shape[1]]
+    for b in range(2):
+        panel_ref[pl.ds(b, owned, stride=2), :] = factor[:, b * half : (b + 1) * half]
     g_hi, g_lo = split(dot(factor, w_ref[...], NN, high))
     for copy in copies[1:]:
         copy.wait()
@@ -431,10 +433,15 @@
     )(place, rows_mine, theirs)
     front_cols = lax.all_gather(message, "grid")
 
+    phases = 4
+    group = owners // phases
     product = call(
         product_kernel,
         [jax.ShapeDtypeStruct((owners, width, lanes), F32)] * CHUNKS,
         flops=4 * owners * width * owned * PW,
+        grid=(phases,),
+        in_specs=[pl.BlockSpec((group, width, PW), lambda i: (i, 0, 0)), pl.BlockSpec((owned, PW), lambda i: (0, 0))],
+        out_specs=[pl.BlockSpec((group, width, lanes), lambda i: (i, 0, 0))] * CHUNKS,
     )(panel_all, q)
     rest, product = lax.optimization_barrier((spread[1:], product))
     bulk = bulk + [exchanged(part) for part in rest]
@@ -446,6 +453,14 @@
             [jax.ShapeDtypeStruct((owners, half, lanes), BF)] * 2,
             [pltpu.VMEM((owners, total, lanes), BF)],
             flops=8 * owners * total * width * lanes,
+            grid=(2 * phases,),
+            in_specs=[
+                pl.BlockSpec((group, width, lanes), lambda i: (jnp.minimum(i, phases - 1), 0, 0)),
+                pl.BlockSpec((group, width, lanes), lambda i: (jnp.minimum(i, phases - 1), 0, 0)),
+                pl.BlockSpec((2, owners, width), lambda i: (0, 0, 0)),
+                pl.BlockSpec((owners, total), lambda i: (0, 0)),
+            ],
+            out_specs=[pl.BlockSpec((group, half, lanes), lambda i: (jnp.maximum(i - phases, 0), 0, 0))] * 2,
         )(bulk[c], product[c], slot_parts, target_own)
         own_t.append(a)
         other_t.append(b)
@@ -457,7 +472,7 @@
         factor_kernel,
         [
             jax.ShapeDtypeStruct((owned * strips, 128), F32),
-            jax.ShapeDtypeStruct((owned, PW // 2), F32),
+            jax.ShapeDtypeStruct((2 * owned, half), F32),
         ],
         [
             pltpu.VMEM((PW, PW), F32),
@@ -481,7 +496,7 @@
         *own_t,
         *recv_t[:-1],
     )
-    steps = 4
+    steps = 2
     last_rows = pl.BlockSpec((lanes * strips // steps, 128), lambda i: ((CHUNKS - 1) * steps + i, 0))
     schur = call(
         last_kernel,
@@ -491,7 +506,7 @@
         out_specs=last_rows,
         input_output_aliases={0: 0},
     )(schur, recv_t[-1])
-    return (schur.reshape(owned, 1, half_cols), panel[:, None, :])
+    return (schur.reshape(owned, 1, half_cols), panel.reshape(owned, 1, PW // 2))
 
 
 def solution(mesh):

time: 186 us -> 184 us (0.989)
  Pallas kernels: 78.7 us -> 73.5 us
  waiting for transfers between devices: 37.9 us -> 41.7 us
  local copies, waits for them, and re-layouts: 10.3 us -> 8.37 us
    all_to_all x3, waiting for transfers between devices: 30.9 us -> 32.9 us  [exchanged(): return lax.all_to_all(block, 'grid', 0, 0, tiled=True)]
    pallas_call x1, Pallas kernels: 21.8 us -> 19.9 us  [shards(): call(factor_kernel, [jax.ShapeDtypeStruct((owned * strips, 128), F32), ja...]
    unnamed x16 -> x15, local copies, waits for them, and re-layouts: 6.81 us -> 4.88 us
  transfers between devices with their start and end apart: 8 -> 8, of which waited for: 5 -> 6; matrix products, arithmetic and copies ran while one was open for 11% -> 10% of each run, Pallas kernels for 40% -> 38%
where the time goes in v7:
time: 184 us; the launch traced here: 181 us
  Pallas kernels  73.5 us (40%)
  waiting for transfers between devices  41.7 us (23%)
  starting transfers between devices  28.8 us (16%)
  between operations  14.3 us (8%)
  local copies, waits for them, and re-layouts  8.37 us (5%)
  other arithmetic  7.79 us (4%)
  matrix products  6.09 us (3%)
    all_to_all x3, waiting for transfers between devices, exchanged(): return lax.all_to_all(block, 'grid', 0, 0, tiled=True)  32.9 us
    all_to_all x3, starting transfers between devices, exchanged(): return lax.all_to_all(block, 'grid', 0, 0, tiled=True)  24.5 us
    pallas_call x1, Pallas kernels, shards(): call(factor_kernel, [jax.ShapeDtypeStruct((owned * strips, 128), F32), ja...  19.9 us
    pallas_call x2, Pallas kernels, shards(): call(functools.partial(owner_kernel, owners, slots, owned), [jax.ShapeDty...  17.2 us
    pallas_call x1, Pallas kernels, shards(): call(functools.partial(source_kernel, owners, slots, owned), [jax.ShapeDt...  16.8 us
    pallas_call x1, Pallas kernels, shards(): call(product_kernel, [jax.ShapeDtypeStruct((owners, width, lanes), F32)]...  7.56 us
    ppermute x3, waiting for transfers between devices, swapped(): return lax.ppermute(block, 'cube', [(i, i ^ 1) for i in range(count)])  7.07 us
    dot_general x2, matrix products, dot(): lax.dot_general(a, b, dims, precision=precision, preferred_element_type=F32)  6.09 us
  transfers between devices with their start and end apart: 8, of which 6 were waited for; matrix products, arithmetic and copies ran while one was open for 10% of the time, Pallas kernels for 38%

profile of v7, /device:TPU:1, one launch (start us, length us, event | category | flops | bytes accessed | tf_op | source)
XLA Modules:
  0.0 180.5 jit_solution(5884316479656506780)
XLA Ops:
  7.2 0.0 all-gather.4.cloned.1.call-start
  7.2 0.7 all-gather.4.cloned.1.call-update
  7.9 1.0 compare_select_fusion
  8.9 0.1 reshape.251
  9.1 1.4 convert_reduce_fusion
  10.5 0.1 concatenate.21
  10.6 0.1 pad_add_fusion
  10.7 0.7 fusion.13.slot_ref
  11.4 0.0 copy-start.5
  11.4 3.9 %fusion.9 = bf16[192,512]{1,0:T(8,128)(2,1)S(1)} fusion(s32[6144]{0:T(1024)S(1)} %bitcast.44, bf16[1,192,6144]{2,1,0:T(8,128)(2,1)} %param.6), kind=kOutput, calls=%fused_computation.14 | convolution fusion | flops 1211203584 | bytes 2580480 | tf_op jit(solution)/shard_map/dot_general | solution.py:22
  15.3 0.0 copy-done.5
  15.3 2.2 %convolution_convert_fusion = bf16[1536,512]{1,0:T(8,128)(2,1)} fusion(s32[384]{0:T(512)S(1)} %concatenate.21, s32[384]{0:T(512)S(1)} %pad_add_fusion, s32[1536]{0:T(1024)S(1)} %add_select_fusion.2, bf16[192,512]{1,0:T(8,128)(2,1)S(1)} %bitcast.42, bf16[192,512]{1,0:T(8,128)(2,1)S(1)} %fusion.9), kind=kOutput, calls=%fused_computation.6 | convolution fusion | flops 607322112 | bytes 1975296 | tf_op jit(solution)/shard_map/dot_general | solution.py:22
  17.5 0.0 slice-start
  17.5 9.6 %all-to-all-start = ((bf16[32,48,512]{2,1,0:T(8,128)(2,1)}), bf16[32,48,512]{2,1,0:T(8,128)(2,1)S(1)}, u32[]{:S(2)}, u32[]{:S(2)}) async-start(bf16[32,48,512]{2,1,0:T(8,128)(2,1)} %bitcast.8), calls=%async_computation | async-start | bytes 3145728 | tf_op jit(solution)/shard_map/all_to_all | solution.py:332
  27.1 0.0 all-gather.6.cloned.1.call-start
  27.2 0.1 pad.8.clone
  27.3 2.3 %select_reduce_fusion = s32[32,512]{1,0:T(8,128)S(1)} fusion(s32[32,192]{1,0:T(8,128)S(1)} %get-tuple-element.62, s32[32,192]{1,0:T(8,128)S(1)} %get-tuple-element.63), kind=kLoop, calls=%fused_computation | loop fusion | flops 9420800 | bytes 114688 | tf_op jit(solution)/shard_map/reduce_sum | solution.py:359
  29.6 0.1 copy.42
  29.8 0.1 copy.55
  29.8 0.1 fusion.23
  29.9 0.1 stack.24
  30.0 0.1 stack.25
  30.1 0.1 select_bitcast_fusion
  30.2 0.1 copy.56
  30.3 0.1 concatenate.25.clone
  30.4 0.1 stack.26
  30.5 0.2 copy.43
  30.7 0.7 copy.44.target_ref
  31.4 0.0 slice-done
  31.4 0.7 copy.58
  32.1 0.6 pad_add_fusion.1.place_ref.parity_ref
  32.7 0.6 add_convert_fusion.target_ref
  33.3 16.8 %shard_map.68 = (bf16[32,192,128]{2,1,0:T(8,128)(2,1)}, bf16[32,192,128]{2,1,0:T(8,128)(2,1)}) custom-call(bf16[192,6144]{1,0:T(8,128)(2,1)} %bitcast.49, f32[2,32,192]{2,1,0:T(8,128)} %fusion.13.slot_ref, f32[32,512]{1,0:T(8,128)} %copy.44.target_ref), custom_call_target="tpu_custom_call" | custom-call | flops 3623878656 | bytes 6291456 | tf_op jit(solution)/shard_map/pallas_call | solution.py:385
  50.1 0.5 all-to-all-done
  50.5 0.0 copy-start
  50.6 1.1 copy-done
  51.7 4.5 %shard_map.69 = (f32[256,512]{1,0:T(8,128)}, bf16[272,512]{1,0:T(8,128)(2,1)}, bf16[256,512]{1,0:T(8,128)(2,1)}) custom-call(s32[2]{0:T(128)} %pad_add_fusion.1.place_ref.parity_ref, bf16[1536,512]{1,0:T(8,128)(2,1)} %bitcast.37, f32[3,1536]{1,0:T(4,128)} %add_convert_fusion.target_ref, f32[256,256]{1,0:T(8,128)} %bitcast.41), custom_call_target="tpu_custom_call" | custom-call | flops 1610612736 | bytes 2129920 | tf_op jit(solution)/shard_map/pallas_call | solution.py:414
  56.2 1.5 collective-permute-start
  57.7 5.3 %collective-permute-done.theirs_ref = bf16[272,512]{1,0:T(8,128)(2,1)S(1)} collective-permute-done((bf16[272,512]{1,0:T(8,128)(2,1)}, bf16[272,512]{1,0:T(8,128)(2,1)S(1)}, u32[]{:S(2)}, u32[]{:S(2)}) %collective-permute-start) | collective-permute-done | bytes 278560 | tf_op jit(solution)/shard_map/ppermute | solution.py:328
  63.0 0.0 copy-start.4
  63.0 0.7 copy-done.4
  63.7 2.2 %shard_map.70 = (f32[256,512]{1,0:T(8,128)}, bf16[208,512]{1,0:T(8,128)(2,1)}) custom-call(s32[2]{0:T(128)} %pad_add_fusion.1.place_ref.parity_ref, f32[256,512]{1,0:T(8,128)} %get-tuple-element.30.mine_ref, bf16[272,512]{1,0:T(8,128)(2,1)} %copy-done.4), custom_call_target="tpu_custom_call" | custom-call | bytes 1474560 | tf_op jit(solution)/shard_map/pallas_call | solution.py:426
  66.0 0.0 all-gather.6.cloned.1.call-update
  66.0 8.9 %all-to-all-start.1 = ((bf16[32,192,128]{2,1,0:T(8,128)(2,1)}), bf16[32,192,128]{2,1,0:T(8,128)(2,1)S(1)}, u32[]{:S(2)}, u32[]{:S(2)}) async-start(bf16[32,192,128]{2,1,0:T(8,128)(2,1)} %get-tuple-element.34), calls=%async_computation.1 | async-start | bytes 3145728 | tf_op jit(solution)/shard_map/all_to_all | solution.py:332
  74.9 1.1 all-gather.4.cloned.1.call-done.panel_ref
  76.0 7.6 %shard_map.71 = (f32[32,192,128]{2,1,0:T(8,128)}, f32[32,192,128]{2,1,0:T(8,128)}) custom-call(bf16[32,192,512]{2,1,0:T(8,128)(2,1)} %all-gather.4.cloned.1.call-done.panel_ref, bf16[256,512]{1,0:T(8,128)(2,1)} %get-tuple-element.36.q_ref), custom_call_target="tpu_custom_call" | custom-call | flops 3221225472 | bytes 12582912 | tf_op jit(solution)/shard_map/pallas_call | solution.py:438
  83.5 14.5 %all-to-all-done.1.recv_ref = bf16[32,192,128]{2,1,0:T(8,128)(2,1)S(1)} async-done(((bf16[32,192,128]{2,1,0:T(8,128)(2,1)}), bf16[32,192,128]{2,1,0:T(8,128)(2,1)S(1)}, u32[]{:S(2)}, u32[]{:S(2)}) %all-to-all-start.1) | async-done | bytes 1572896 | tf_op jit(solution)/shard_map/all_to_all | solution.py:332
  98.0 0.0 copy-start.1
  98.0 6.0 %all-to-all-start.2 = ((bf16[32,192,128]{2,1,0:T(8,128)(2,1)}), bf16[32,192,128]{2,1,0:T(8,128)(2,1)S(1)}, u32[]{:S(2)}, u32[]{:S(2)}) async-start(bf16[32,192,128]{2,1,0:T(8,128)(2,1)} %get-tuple-element.41), calls=%async_computation.2 | async-start | bytes 3145728 | tf_op jit(solution)/shard_map/all_to_all | solution.py:332
  104.0 0.8 select_convert_fusion
  104.8 1.1 copy.49
  105.9 0.7 copy.50.target_ref
  106.7 0.0 copy-done.1
  106.7 8.6 %shard_map.72 = (bf16[32,128,128]{2,1,0:T(8,128)(2,1)}, bf16[32,128,128]{2,1,0:T(8,128)(2,1)}) custom-call(bf16[32,192,128]{2,1,0:T(8,128)(2,1)} %copy-done.1, f32[32,192,128]{2,1,0:T(8,128)} %get-tuple-element.39.product_ref, f32[2,32,192]{2,1,0:T(8,128)} %fusion.13.slot_ref, f32[32,512]{1,0:T(8,128)} %copy.50.target_ref), custom_call_target="tpu_custom_call" | custom-call | flops 3221225472 | bytes 4194304 | tf_op jit(solution)/shard_map/pallas_call | solution.py:451
  115.3 1.3 collective-permute-start.1
  116.6 17.9 %all-to-all-done.2.recv_ref = bf16[32,192,128]{2,1,0:T(8,128)(2,1)S(1)} async-done(((bf16[32,192,128]{2,1,0:T(8,128)(2,1)}), bf16[32,192,128]{2,1,0:T(8,128)(2,1)S(1)}, u32[]{:S(2)}, u32[]{:S(2)}) %all-to-all-start.2) | async-done | bytes 1572896 | tf_op jit(solution)/shard_map/all_to_all | solution.py:332
  134.5 1.1 copy-done.2
  135.7 8.6 %shard_map.73 = (bf16[32,128,128]{2,1,0:T(8,128)(2,1)}, bf16[32,128,128]{2,1,0:T(8,128)(2,1)}) custom-call(bf16[32,192,128]{2,1,0:T(8,128)(2,1)} %copy-done.2, f32[32,192,128]{2,1,0:T(8,128)} %get-tuple-element.42.product_ref, f32[2,32,192]{2,1,0:T(8,128)} %fusion.13.slot_ref, f32[32,512]{1,0:T(8,128)} %copy.50.target_ref), custom_call_target="tpu_custom_call" | custom-call | flops 3221225472 | bytes 4194304 | tf_op jit(solution)/shard_map/pallas_call | solution.py:451
  144.3 1.4 collective-permute-start.2
  145.7 0.0 collective-permute-done.1.refs_2_
  145.7 19.9 %shard_map.74 = (f32[8192,128]{1,0:T(8,128)}, f32[512,128]{1,0:T(8,128)}) custom-call(s32[2]{0:T(128)} %pad_add_fusion.1.place_ref.parity_ref, f32[256,512]{1,0:T(8,128)} %get-tuple-element.32.rows_ref, bf16[32,208,512]{2,1,0:T(8,128)(2,1)} %bitcast.48, f32[8192,128]{1,0:T(8,128)} %bitcast.40, bf16[32,128,128]{2,1,0:T(8,128)(2,1)} %get-tuple-element.40.refs_0_, ...), custom_call_target="tpu_custom_call" | custom-call | flops 8053063680 | bytes 8912896 | tf_op jit(solution)/shard_map/pallas_call | solution.py:471
  165.6 1.8 collective-permute-done.2.recv_ref
  167.4 1.0 copy-done.3
  168.4 5.3 %shard_map.75 = f32[8192,128]{1,0:T(8,128)} custom-call(f32[8192,128]{1,0:T(8,128)} %get-tuple-element.45.schur_ref, bf16[32,128,128]{2,1,0:T(8,128)(2,1)} %copy-done.3), custom_call_target="tpu_custom_call", output_to_operand_aliasing={{}: (0, {})} | custom-call | bytes 8388608 | tf_op jit(solution)/shard_map/pallas_call | solution.py:501
  (18 shorter events, 0.2 us)
Async XLA Ops:
  7.2 68.8 %all-gather.4.cloned.1.call-start = ((), (), s32[]{:S(2)}) async-start(), calls=%async_computation.3 | async-start | bytes 6488064 | tf_op jit(solution)/shard_map/all_gather | solution.py:349
  11.4 3.9 %copy-start.5 = (bf16[1,192,512]{2,1,0:T(8,128)(2,1)S(1)}, bf16[1,192,512]{2,1,0:T(8,128)(2,1)}, u32[]{:S(2)}) copy-start(bf16[1,192,512]{2,1,0:T(8,128)(2,1)} %param.7) | copy-start | bytes 589828
  17.5 13.9 %slice-start = ((f32[256,1,4096]{2,1,0:T(1,128)}), f32[256,1,256]{2,1,0:T(1,128)S(1)}, s32[]{:S(2)}) async-start(f32[256,1,4096]{2,1,0:T(1,128)} %param.5), calls=%async_computation.5 | async-start | bytes 524288 | tf_op jit(solution)/shard_map/slice | solution.py:423
  17.5 33.0 %all-to-all-start = ((bf16[32,48,512]{2,1,0:T(8,128)(2,1)}), bf16[32,48,512]{2,1,0:T(8,128)(2,1)S(1)}, u32[]{:S(2)}, u32[]{:S(2)}) async-start(bf16[32,48,512]{2,1,0:T(8,128)(2,1)} %bitcast.8), calls=%async_computation | async-start | bytes 3145728 | tf_op jit(solution)/shard_map/all_to_all | solution.py:332
  27.1 118.6 %all-gather.6.cloned.1.call-start = ((), (), s32[]{:S(2)}) async-start(), calls=%async_computation.4 | async-start | bytes 7028736 | tf_op jit(solution)/shard_map/all_gather | solution.py:434
  50.5 1.1 copy-start
  56.2 6.8 %collective-permute-start = (bf16[272,512]{1,0:T(8,128)(2,1)}, bf16[272,512]{1,0:T(8,128)(2,1)S(1)}, u32[]{:S(2)}, u32[]{:S(2)}) collective-permute-start(bf16[272,512]{1,0:T(8,128)(2,1)} %get-tuple-element.31), channel_id=1, source_target_pairs={{0,32},{32,0},{64,96},{96,64},{1,33},{33,1},{65,97},{97,65},{2,34}... | collective-permute-start | bytes 835592 | tf_op jit(solution)/shard_map/ppermute | solution.py:328
  63.0 0.7 copy-start.4
  66.0 32.0 %all-to-all-start.1 = ((bf16[32,192,128]{2,1,0:T(8,128)(2,1)}), bf16[32,192,128]{2,1,0:T(8,128)(2,1)S(1)}, u32[]{:S(2)}, u32[]{:S(2)}) async-start(bf16[32,192,128]{2,1,0:T(8,128)(2,1)} %get-tuple-element.34), calls=%async_computation.1 | async-start | bytes 3145728 | tf_op jit(solution)/shard_map/all_to_all | solution.py:332
  98.0 8.7 %copy-start.1 = (bf16[32,192,128]{2,1,0:T(8,128)(2,1)}, bf16[32,192,128]{2,1,0:T(8,128)(2,1)S(1)}, u32[]{:S(2)}) copy-start(bf16[32,192,128]{2,1,0:T(8,128)(2,1)S(1)} %all-to-all-done.1.recv_ref) | copy-start | bytes 4718596
  98.0 36.5 %all-to-all-start.2 = ((bf16[32,192,128]{2,1,0:T(8,128)(2,1)}), bf16[32,192,128]{2,1,0:T(8,128)(2,1)S(1)}, u32[]{:S(2)}, u32[]{:S(2)}) async-start(bf16[32,192,128]{2,1,0:T(8,128)(2,1)} %get-tuple-element.41), calls=%async_computation.2 | async-start | bytes 3145728 | tf_op jit(solution)/shard_map/all_to_all | solution.py:332
  115.3 30.4 %collective-permute-start.1 = (bf16[32,128,128]{2,1,0:T(8,128)(2,1)}, bf16[32,128,128]{2,1,0:T(8,128)(2,1)}, u32[]{:S(2)}, u32[]{:S(2)}) collective-permute-start(bf16[32,128,128]{2,1,0:T(8,128)(2,1)} %get-tuple-element.44), channel_id=1, source_target_pairs={{0,32},{32,0},{64,96},{96,64},{1,33},{33,1},{65,97},{97,65},{2,34}... | collective-permute-start | bytes 3145736 | tf_op jit(solution)/shard_map/ppermute | solution.py:328
  134.5 1.1 copy-start.2
  144.3 23.1 %collective-permute-start.2 = (bf16[32,128,128]{2,1,0:T(8,128)(2,1)}, bf16[32,128,128]{2,1,0:T(8,128)(2,1)S(1)}, u32[]{:S(2)}, u32[]{:S(2)}) collective-permute-start(bf16[32,128,128]{2,1,0:T(8,128)(2,1)} %get-tuple-element.46), channel_id=1, source_target_pairs={{0,32},{32,0},{64,96},{96,64},{1,33},{33,1},{65,97},{97,65},{2,34}... | collective-permute-start | bytes 3145736 | tf_op jit(solution)/shard_map/ppermute | solution.py:328
  167.4 1.0 copy-start.3
Sparse Core Ops, SparseCore 0:
  10.2 65.6 all-gather.3
  78.2 62.2 all-gather.5

commit v8 on v7

--- a/solution.py
+++ b/solution.py
@@ -210,7 +210,7 @@
         w_parts = split(w)
         m_parts = split(dot3(w_parts, s_parts))
         e = dot3(m_parts, w_parts, NT) - unit
-        w_ref[...] = w - dot3(split(phi * e), w_parts)
+        w_ref[...] = w - dot((phi * e).astype(BF), w_parts[0])
         return count + 1, jnp.sum(e * e)
 
     def more(state):
@@ -290,22 +290,25 @@
         copy.wait()
     lanes = owned // CHUNKS
     unit = eye(lanes, BF)
+    twice = jnp.concatenate([unit, unit], axis=1)
+    both = jnp.concatenate([g_hi, g_lo], axis=0)
     for pair in range(strips // 2):
-        cols = cols_ref[pl.ds(2 * pair, 2)].reshape(2 * half, PW)
         if pair == 0:
             update = dot3((g_hi, g_lo), lead_cols, NT)
         else:
-            update = dot(g_hi, cols, NT) + dot(g_lo, cols, NT)
-        placed = []
+            update = dot(both, cols_ref[pl.ds(2 * pair, 2)].reshape(2 * half, PW), NT)
+            update = update[:owned] + update[owned:]
         for c in range(CHUNKS):
-            z = dot(unit, own_ref[c, pl.ds(2 * pair, 2)].reshape(2 * half, lanes), NT)
+            own = own_ref[c, pl.ds(2 * pair, 2)].reshape(2 * half, lanes)
             if c < CHUNKS - 1:
-                z = z + dot(unit, recv_ref[c, pl.ds(2 * pair, 2)].reshape(2 * half, lanes), NT)
-            placed.append(z)
-        change = jnp.concatenate(placed, axis=0) - update
-        for side in range(2):
-            at = pl.ds(2 * pair + side, owned, stride=strips)
-            schur_ref[at, :] = parent_ref[at, :] + change[:, side * half : (side + 1) * half]
+                recv = recv_ref[c, pl.ds(2 * pair, 2)].reshape(2 * half, lanes)
+                placed = dot(twice, jnp.concatenate([own, recv], axis=1), NT)
+            else:
+                placed = dot(unit, own, NT)
+            change = placed - update[c * lanes : (c + 1) * lanes]
+            for side in range(2):
+                at = pl.ds(c * lanes * strips + 2 * pair + side, lanes, stride=strips)
+                schur_ref[at, :] = parent_ref[at, :] + change[:, side * half : (side + 1) * half]
 
 
 def last_kernel(schur_ref, recv_ref, out_ref):

time: 184 us -> 184 us (level)
  transfers between devices with their start and end apart: 8 -> 8, of which waited for: 6 -> 6; matrix products, arithmetic and copies ran while one was open for 10% -> 10% of each run, Pallas kernels for 38% -> 37%
where the time goes in v8:
time: 184 us; the launch traced here: 181 us
  Pallas kernels  72.2 us (39%)
  waiting for transfers between devices  43 us (23%)
  starting transfers between devices  28.8 us (16%)
  between operations  14.3 us (8%)
  local copies, waits for them, and re-layouts  8.37 us (5%)
  other arithmetic  7.79 us (4%)
  matrix products  6.09 us (3%)
    all_to_all x3, waiting for transfers between devices, exchanged(): return lax.all_to_all(block, 'grid', 0, 0, tiled=True)  32.9 us
    all_to_all x3, starting transfers between devices, exchanged(): return lax.all_to_all(block, 'grid', 0, 0, tiled=True)  24.5 us
    pallas_call x1, Pallas kernels, shards(): call(factor_kernel, [jax.ShapeDtypeStruct((owned * strips, 128), F32), ja...  18.5 us
    pallas_call x2, Pallas kernels, shards(): call(functools.partial(owner_kernel, owners, slots, owned), [jax.ShapeDty...  17.2 us
    pallas_call x1, Pallas kernels, shards(): call(functools.partial(source_kernel, owners, slots, owned), [jax.ShapeDt...  16.8 us
    ppermute x3, waiting for transfers between devices, swapped(): return lax.ppermute(block, 'cube', [(i, i ^ 1) for i in range(count)])  8.41 us
    pallas_call x1, Pallas kernels, shards(): call(product_kernel, [jax.ShapeDtypeStruct((owners, width, lanes), F32)]...  7.56 us
    dot_general x2, matrix products, dot(): lax.dot_general(a, b, dims, precision=precision, preferred_element_type=F32)  6.09 us
  transfers between devices with their start and end apart: 8, of which 6 were waited for; matrix products, arithmetic and copies ran while one was open for 10% of the time, Pallas kernels for 37%

profile of v8, /device:TPU:1, one launch (start us, length us, event | category | flops | bytes accessed | tf_op | source)
XLA Modules:
  0.0 180.5 jit_solution(3612396265496413832)
XLA Ops:
  7.2 0.0 all-gather.4.cloned.1.call-start
  7.2 0.7 all-gather.4.cloned.1.call-update
  7.9 1.0 compare_select_fusion
  8.9 0.1 reshape.251
  9.1 1.4 convert_reduce_fusion
  10.5 0.1 concatenate.21
  10.6 0.1 pad_add_fusion
  10.7 0.7 fusion.13.slot_ref
  11.4 0.0 copy-start.5
  11.4 3.9 %fusion.9 = bf16[192,512]{1,0:T(8,128)(2,1)S(1)} fusion(s32[6144]{0:T(1024)S(1)} %bitcast.44, bf16[1,192,6144]{2,1,0:T(8,128)(2,1)} %param.6), kind=kOutput, calls=%fused_computation.14 | convolution fusion | flops 1211203584 | bytes 2580480 | tf_op jit(solution)/shard_map/dot_general | solution.py:22
  15.3 0.0 copy-done.5
  15.3 2.2 %convolution_convert_fusion = bf16[1536,512]{1,0:T(8,128)(2,1)} fusion(s32[384]{0:T(512)S(1)} %concatenate.21, s32[384]{0:T(512)S(1)} %pad_add_fusion, s32[1536]{0:T(1024)S(1)} %add_select_fusion.2, bf16[192,512]{1,0:T(8,128)(2,1)S(1)} %bitcast.42, bf16[192,512]{1,0:T(8,128)(2,1)S(1)} %fusion.9), kind=kOutput, calls=%fused_computation.6 | convolution fusion | flops 607322112 | bytes 1975296 | tf_op jit(solution)/shard_map/dot_general | solution.py:22
  17.5 0.0 slice-start
  17.5 9.6 %all-to-all-start = ((bf16[32,48,512]{2,1,0:T(8,128)(2,1)}), bf16[32,48,512]{2,1,0:T(8,128)(2,1)S(1)}, u32[]{:S(2)}, u32[]{:S(2)}) async-start(bf16[32,48,512]{2,1,0:T(8,128)(2,1)} %bitcast.8), calls=%async_computation | async-start | bytes 3145728 | tf_op jit(solution)/shard_map/all_to_all | solution.py:335
  27.1 0.0 all-gather.6.cloned.1.call-start
  27.2 0.1 pad.8.clone
  27.3 2.3 %select_reduce_fusion = s32[32,512]{1,0:T(8,128)S(1)} fusion(s32[32,192]{1,0:T(8,128)S(1)} %get-tuple-element.62, s32[32,192]{1,0:T(8,128)S(1)} %get-tuple-element.63), kind=kLoop, calls=%fused_computation | loop fusion | flops 9420800 | bytes 114688 | tf_op jit(solution)/shard_map/reduce_sum | solution.py:362
  29.6 0.1 copy.42
  29.8 0.1 copy.55
  29.8 0.1 fusion.23
  29.9 0.1 stack.24
  30.0 0.1 stack.25
  30.1 0.1 select_bitcast_fusion
  30.2 0.1 copy.56
  30.3 0.1 concatenate.25.clone
  30.4 0.1 stack.26
  30.5 0.2 copy.43
  30.7 0.7 copy.44.target_ref
  31.4 0.0 slice-done
  31.4 0.7 copy.58
  32.1 0.6 pad_add_fusion.1.place_ref.parity_ref
  32.7 0.6 add_convert_fusion.target_ref
  33.3 16.8 %shard_map.68 = (bf16[32,192,128]{2,1,0:T(8,128)(2,1)}, bf16[32,192,128]{2,1,0:T(8,128)(2,1)}) custom-call(bf16[192,6144]{1,0:T(8,128)(2,1)} %bitcast.49, f32[2,32,192]{2,1,0:T(8,128)} %fusion.13.slot_ref, f32[32,512]{1,0:T(8,128)} %copy.44.target_ref), custom_call_target="tpu_custom_call" | custom-call | flops 3623878656 | bytes 6291456 | tf_op jit(solution)/shard_map/pallas_call | solution.py:388
  50.1 0.5 all-to-all-done
  50.5 0.0 copy-start
  50.6 1.1 copy-done
  51.7 4.5 %shard_map.69 = (f32[256,512]{1,0:T(8,128)}, bf16[272,512]{1,0:T(8,128)(2,1)}, bf16[256,512]{1,0:T(8,128)(2,1)}) custom-call(s32[2]{0:T(128)} %pad_add_fusion.1.place_ref.parity_ref, bf16[1536,512]{1,0:T(8,128)(2,1)} %bitcast.37, f32[3,1536]{1,0:T(4,128)} %add_convert_fusion.target_ref, f32[256,256]{1,0:T(8,128)} %bitcast.41), custom_call_target="tpu_custom_call" | custom-call | flops 1610612736 | bytes 2129920 | tf_op jit(solution)/shard_map/pallas_call | solution.py:417
  56.2 1.5 collective-permute-start
  57.7 5.3 %collective-permute-done.theirs_ref = bf16[272,512]{1,0:T(8,128)(2,1)S(1)} collective-permute-done((bf16[272,512]{1,0:T(8,128)(2,1)}, bf16[272,512]{1,0:T(8,128)(2,1)S(1)}, u32[]{:S(2)}, u32[]{:S(2)}) %collective-permute-start) | collective-permute-done | bytes 278560 | tf_op jit(solution)/shard_map/ppermute | solution.py:331
  63.0 0.0 copy-start.4
  63.0 0.7 copy-done.4
  63.7 2.2 %shard_map.70 = (f32[256,512]{1,0:T(8,128)}, bf16[208,512]{1,0:T(8,128)(2,1)}) custom-call(s32[2]{0:T(128)} %pad_add_fusion.1.place_ref.parity_ref, f32[256,512]{1,0:T(8,128)} %get-tuple-element.30.mine_ref, bf16[272,512]{1,0:T(8,128)(2,1)} %copy-done.4), custom_call_target="tpu_custom_call" | custom-call | bytes 1474560 | tf_op jit(solution)/shard_map/pallas_call | solution.py:429
  66.0 0.0 all-gather.6.cloned.1.call-update
  66.0 8.9 %all-to-all-start.1 = ((bf16[32,192,128]{2,1,0:T(8,128)(2,1)}), bf16[32,192,128]{2,1,0:T(8,128)(2,1)S(1)}, u32[]{:S(2)}, u32[]{:S(2)}) async-start(bf16[32,192,128]{2,1,0:T(8,128)(2,1)} %get-tuple-element.34), calls=%async_computation.1 | async-start | bytes 3145728 | tf_op jit(solution)/shard_map/all_to_all | solution.py:335
  74.9 1.1 all-gather.4.cloned.1.call-done.panel_ref
  76.0 7.6 %shard_map.71 = (f32[32,192,128]{2,1,0:T(8,128)}, f32[32,192,128]{2,1,0:T(8,128)}) custom-call(bf16[32,192,512]{2,1,0:T(8,128)(2,1)} %all-gather.4.cloned.1.call-done.panel_ref, bf16[256,512]{1,0:T(8,128)(2,1)} %get-tuple-element.36.q_ref), custom_call_target="tpu_custom_call" | custom-call | flops 3221225472 | bytes 12582912 | tf_op jit(solution)/shard_map/pallas_call | solution.py:441
  83.5 14.5 %all-to-all-done.1.recv_ref = bf16[32,192,128]{2,1,0:T(8,128)(2,1)S(1)} async-done(((bf16[32,192,128]{2,1,0:T(8,128)(2,1)}), bf16[32,192,128]{2,1,0:T(8,128)(2,1)S(1)}, u32[]{:S(2)}, u32[]{:S(2)}) %all-to-all-start.1) | async-done | bytes 1572896 | tf_op jit(solution)/shard_map/all_to_all | solution.py:335
  98.0 0.0 copy-start.1
  98.0 6.0 %all-to-all-start.2 = ((bf16[32,192,128]{2,1,0:T(8,128)(2,1)}), bf16[32,192,128]{2,1,0:T(8,128)(2,1)S(1)}, u32[]{:S(2)}, u32[]{:S(2)}) async-start(bf16[32,192,128]{2,1,0:T(8,128)(2,1)} %get-tuple-element.41), calls=%async_computation.2 | async-start | bytes 3145728 | tf_op jit(solution)/shard_map/all_to_all | solution.py:335
  104.0 0.8 select_convert_fusion
  104.8 1.1 copy.49
  105.9 0.7 copy.50.target_ref
  106.7 0.0 copy-done.1
  106.7 8.6 %shard_map.72 = (bf16[32,128,128]{2,1,0:T(8,128)(2,1)}, bf16[32,128,128]{2,1,0:T(8,128)(2,1)}) custom-call(bf16[32,192,128]{2,1,0:T(8,128)(2,1)} %copy-done.1, f32[32,192,128]{2,1,0:T(8,128)} %get-tuple-element.39.product_ref, f32[2,32,192]{2,1,0:T(8,128)} %fusion.13.slot_ref, f32[32,512]{1,0:T(8,128)} %copy.50.target_ref), custom_call_target="tpu_custom_call" | custom-call | flops 3221225472 | bytes 4194304 | tf_op jit(solution)/shard_map/pallas_call | solution.py:454
  115.3 1.3 collective-permute-start.1
  116.6 17.9 %all-to-all-done.2.recv_ref = bf16[32,192,128]{2,1,0:T(8,128)(2,1)S(1)} async-done(((bf16[32,192,128]{2,1,0:T(8,128)(2,1)}), bf16[32,192,128]{2,1,0:T(8,128)(2,1)S(1)}, u32[]{:S(2)}, u32[]{:S(2)}) %all-to-all-start.2) | async-done | bytes 1572896 | tf_op jit(solution)/shard_map/all_to_all | solution.py:335
  134.5 1.1 copy-done.2
  135.7 8.6 %shard_map.73 = (bf16[32,128,128]{2,1,0:T(8,128)(2,1)}, bf16[32,128,128]{2,1,0:T(8,128)(2,1)}) custom-call(bf16[32,192,128]{2,1,0:T(8,128)(2,1)} %copy-done.2, f32[32,192,128]{2,1,0:T(8,128)} %get-tuple-element.42.product_ref, f32[2,32,192]{2,1,0:T(8,128)} %fusion.13.slot_ref, f32[32,512]{1,0:T(8,128)} %copy.50.target_ref), custom_call_target="tpu_custom_call" | custom-call | flops 3221225472 | bytes 4194304 | tf_op jit(solution)/shard_map/pallas_call | solution.py:454
  144.3 1.4 collective-permute-start.2
  145.7 0.0 collective-permute-done.1.refs_2_
  145.7 18.5 %shard_map.74 = (f32[8192,128]{1,0:T(8,128)}, f32[512,128]{1,0:T(8,128)}) custom-call(s32[2]{0:T(128)} %pad_add_fusion.1.place_ref.parity_ref, f32[256,512]{1,0:T(8,128)} %get-tuple-element.32.rows_ref, bf16[32,208,512]{2,1,0:T(8,128)(2,1)} %bitcast.48, f32[8192,128]{1,0:T(8,128)} %bitcast.40, bf16[32,128,128]{2,1,0:T(8,128)(2,1)} %get-tuple-element.40.refs_0_, ...), custom_call_target="tpu_custom_call" | custom-call | flops 8053063680 | bytes 8912896 | tf_op jit(solution)/shard_map/pallas_call | solution.py:474
  164.3 3.1 %collective-permute-done.2.recv_ref = bf16[32,128,128]{2,1,0:T(8,128)(2,1)S(1)} collective-permute-done((bf16[32,128,128]{2,1,0:T(8,128)(2,1)}, bf16[32,128,128]{2,1,0:T(8,128)(2,1)S(1)}, u32[]{:S(2)}, u32[]{:S(2)}) %collective-permute-start.2) | collective-permute-done | bytes 1048608 | tf_op jit(solution)/shard_map/ppermute | solution.py:331
  167.4 1.0 copy-done.3
  168.4 5.3 %shard_map.75 = f32[8192,128]{1,0:T(8,128)} custom-call(f32[8192,128]{1,0:T(8,128)} %get-tuple-element.45.schur_ref, bf16[32,128,128]{2,1,0:T(8,128)(2,1)} %copy-done.3), custom_call_target="tpu_custom_call", output_to_operand_aliasing={{}: (0, {})} | custom-call | bytes 8388608 | tf_op jit(solution)/shard_map/pallas_call | solution.py:504
  (18 shorter events, 0.2 us)
Async XLA Ops:
  7.2 68.8 %all-gather.4.cloned.1.call-start = ((), (), s32[]{:S(2)}) async-start(), calls=%async_computation.3 | async-start | bytes 6488064 | tf_op jit(solution)/shard_map/all_gather | solution.py:352
  11.4 3.9 %copy-start.5 = (bf16[1,192,512]{2,1,0:T(8,128)(2,1)S(1)}, bf16[1,192,512]{2,1,0:T(8,128)(2,1)}, u32[]{:S(2)}) copy-start(bf16[1,192,512]{2,1,0:T(8,128)(2,1)} %param.7) | copy-start | bytes 589828
  17.5 13.9 %slice-start = ((f32[256,1,4096]{2,1,0:T(1,128)}), f32[256,1,256]{2,1,0:T(1,128)S(1)}, s32[]{:S(2)}) async-start(f32[256,1,4096]{2,1,0:T(1,128)} %param.5), calls=%async_computation.5 | async-start | bytes 524288 | tf_op jit(solution)/shard_map/slice | solution.py:426
  17.5 33.0 %all-to-all-start = ((bf16[32,48,512]{2,1,0:T(8,128)(2,1)}), bf16[32,48,512]{2,1,0:T(8,128)(2,1)S(1)}, u32[]{:S(2)}, u32[]{:S(2)}) async-start(bf16[32,48,512]{2,1,0:T(8,128)(2,1)} %bitcast.8), calls=%async_computation | async-start | bytes 3145728 | tf_op jit(solution)/shard_map/all_to_all | solution.py:335
  27.1 118.6 %all-gather.6.cloned.1.call-start = ((), (), s32[]{:S(2)}) async-start(), calls=%async_computation.4 | async-start | bytes 7028736 | tf_op jit(solution)/shard_map/all_gather | solution.py:437
  50.5 1.1 copy-start
  56.2 6.8 %collective-permute-start = (bf16[272,512]{1,0:T(8,128)(2,1)}, bf16[272,512]{1,0:T(8,128)(2,1)S(1)}, u32[]{:S(2)}, u32[]{:S(2)}) collective-permute-start(bf16[272,512]{1,0:T(8,128)(2,1)} %get-tuple-element.31), channel_id=1, source_target_pairs={{0,32},{32,0},{64,96},{96,64},{1,33},{33,1},{65,97},{97,65},{2,34}... | collective-permute-start | bytes 835592 | tf_op jit(solution)/shard_map/ppermute | solution.py:331
  63.0 0.7 copy-start.4
  66.0 32.0 %all-to-all-start.1 = ((bf16[32,192,128]{2,1,0:T(8,128)(2,1)}), bf16[32,192,128]{2,1,0:T(8,128)(2,1)S(1)}, u32[]{:S(2)}, u32[]{:S(2)}) async-start(bf16[32,192,128]{2,1,0:T(8,128)(2,1)} %get-tuple-element.34), calls=%async_computation.1 | async-start | bytes 3145728 | tf_op jit(solution)/shard_map/all_to_all | solution.py:335
  98.0 8.7 %copy-start.1 = (bf16[32,192,128]{2,1,0:T(8,128)(2,1)}, bf16[32,192,128]{2,1,0:T(8,128)(2,1)S(1)}, u32[]{:S(2)}) copy-start(bf16[32,192,128]{2,1,0:T(8,128)(2,1)S(1)} %all-to-all-done.1.recv_ref) | copy-start | bytes 4718596
  98.0 36.5 %all-to-all-start.2 = ((bf16[32,192,128]{2,1,0:T(8,128)(2,1)}), bf16[32,192,128]{2,1,0:T(8,128)(2,1)S(1)}, u32[]{:S(2)}, u32[]{:S(2)}) async-start(bf16[32,192,128]{2,1,0:T(8,128)(2,1)} %get-tuple-element.41), calls=%async_computation.2 | async-start | bytes 3145728 | tf_op jit(solution)/shard_map/all_to_all | solution.py:335
  115.3 30.4 %collective-permute-start.1 = (bf16[32,128,128]{2,1,0:T(8,128)(2,1)}, bf16[32,128,128]{2,1,0:T(8,128)(2,1)}, u32[]{:S(2)}, u32[]{:S(2)}) collective-permute-start(bf16[32,128,128]{2,1,0:T(8,128)(2,1)} %get-tuple-element.44), channel_id=1, source_target_pairs={{0,32},{32,0},{64,96},{96,64},{1,33},{33,1},{65,97},{97,65},{2,34}... | collective-permute-start | bytes 3145736 | tf_op jit(solution)/shard_map/ppermute | solution.py:331
  134.5 1.1 copy-start.2
  144.3 23.1 %collective-permute-start.2 = (bf16[32,128,128]{2,1,0:T(8,128)(2,1)}, bf16[32,128,128]{2,1,0:T(8,128)(2,1)S(1)}, u32[]{:S(2)}, u32[]{:S(2)}) collective-permute-start(bf16[32,128,128]{2,1,0:T(8,128)(2,1)} %get-tuple-element.46), channel_id=1, source_target_pairs={{0,32},{32,0},{64,96},{96,64},{1,33},{33,1},{65,97},{97,65},{2,34}... | collective-permute-start | bytes 3145736 | tf_op jit(solution)/shard_map/ppermute | solution.py:331
  167.4 1.0 copy-start.3
Sparse Core Ops, SparseCore 0:
  10.2 65.6 all-gather.3
  78.2 62.2 all-gather.5

commit v9 on v8

--- a/solution.py
+++ b/solution.py
@@ -424,8 +424,9 @@
         flops=8 * owned * owners * kinds * PW,
         in_specs=[smem] + [vmem] * 3,
     )(place, packed.reshape(owners * kinds, PW), kind_targets, parent_front[:, 0, : PW // 2])
+    message, ready = lax.optimization_barrier((message, spread[0]))
     theirs = swapped(message)
-    bulk = [exchanged(spread[0])]
+    bulk = [exchanged(ready)]
     rows, message = call(
         rows_kernel,
         [
@@ -455,7 +456,7 @@
             functools.partial(owner_kernel, owners, slots, owned),
             [jax.ShapeDtypeStruct((owners, half, lanes), BF)] * 2,
             [pltpu.VMEM((owners, total, lanes), BF)],
-            flops=8 * owners * total * width * lanes,
+            flops=250 * owners * total * width * lanes,
             grid=(2 * phases,),
             in_specs=[
                 pl.BlockSpec((group, width, lanes), lambda i: (jnp.minimum(i, phases - 1), 0, 0)),
@@ -499,7 +500,7 @@
         *own_t,
         *recv_t[:-1],
     )
-    steps = 2
+    steps = 1
     last_rows = pl.BlockSpec((lanes * strips // steps, 128), lambda i: ((CHUNKS - 1) * steps + i, 0))
     schur = call(
         last_kernel,

time: 184 us -> 188 us (1.022); the launches traced: 181 us -> 187 us
  waiting for transfers between devices: 43 us -> 50.9 us
    all_to_all x3, waiting for transfers between devices: 32.9 us -> 15.3 us  [exchanged(): return lax.all_to_all(block, 'grid', 0, 0, tiled=True)]
    all_gather x1, waiting for transfers between devices: 0.01 us -> 15.4 us  [shards(): front_cols = lax.all_gather(message, 'grid')]
    all_gather x1, waiting for transfers between devices: 1.06 us -> 13.7 us  [shards(): panel_all = lax.all_gather(own_panel, 'grid')]
    ppermute x3, waiting for transfers between devices: 8.41 us -> 5.84 us  [swapped(): return lax.ppermute(block, 'cube', [(i, i ^ 1) for i in range(count)])]
    unnamed x15 -> x17, local copies, waits for them, and re-layouts: 4.88 us -> 4.89 us
  transfers between devices with their start and end apart: 8 -> 8, of which waited for: 6 -> 5; matrix products, arithmetic and copies ran while one was open for 10% -> 9% of each run, Pallas kernels for 37% -> 36%
where the time goes in v9:
time: 188 us; the launch traced here: 187 us
  Pallas kernels  72.4 us (39%)
  waiting for transfers between devices  50.9 us (27%)
  starting transfers between devices  28.7 us (15%)
  between operations  14.3 us (8%)
  local copies, waits for them, and re-layouts  7.43 us (4%)
  other arithmetic  7.12 us (4%)
  matrix products  6.09 us (3%)
    all_to_all x3, starting transfers between devices, exchanged(): return lax.all_to_all(block, 'grid', 0, 0, tiled=True)  24.8 us
    pallas_call x1, Pallas kernels, shards(): call(factor_kernel, [jax.ShapeDtypeStruct((owned * strips, 128), F32), ja...  18.5 us
    pallas_call x2, Pallas kernels, shards(): call(functools.partial(owner_kernel, owners, slots, owned), [jax.ShapeDty...  17.2 us
    pallas_call x1, Pallas kernels, shards(): call(functools.partial(source_kernel, owners, slots, owned), [jax.ShapeDt...  16.8 us
    all_gather x1, waiting for transfers between devices, shards(): front_cols = lax.all_gather(message, 'grid')  15.4 us
    all_to_all x3, waiting for transfers between devices, exchanged(): return lax.all_to_all(block, 'grid', 0, 0, tiled=True)  15.3 us
    all_gather x1, waiting for transfers between devices, shards(): panel_all = lax.all_gather(own_panel, 'grid')  13.7 us
    pallas_call x1, Pallas kernels, shards(): call(product_kernel, [jax.ShapeDtypeStruct((owners, width, lanes), F32)]...  7.55 us
  transfers between devices with their start and end apart: 8, of which 5 were waited for; matrix products, arithmetic and copies ran while one was open for 9% of the time, Pallas kernels for 36%

profile of v9, /device:TPU:1, one launch (start us, length us, event | category | flops | bytes accessed | tf_op | source)
XLA Modules:
  0.0 186.9 jit_solution(293087766740125481)
XLA Ops:
  7.2 0.0 all-gather.4.cloned.1.call-start
  7.2 0.7 all-gather.4.cloned.1.call-update
  7.9 1.0 compare_select_fusion
  8.9 0.1 reshape.251
  9.1 1.4 convert_reduce_fusion
  10.5 0.1 concatenate.21
  10.6 0.1 pad_add_fusion
  10.7 0.7 fusion.13.slot_ref
  11.4 0.0 copy-start.5
  11.4 3.9 %fusion.9 = bf16[192,512]{1,0:T(8,128)(2,1)S(1)} fusion(s32[6144]{0:T(1024)S(1)} %bitcast.44, bf16[1,192,6144]{2,1,0:T(8,128)(2,1)} %param.6), kind=kOutput, calls=%fused_computation.14 | convolution fusion | flops 1211203584 | bytes 2580480 | tf_op jit(solution)/shard_map/dot_general | solution.py:22
  15.3 0.0 copy-done.5
  15.3 2.2 %convolution_convert_fusion = bf16[1536,512]{1,0:T(8,128)(2,1)} fusion(s32[384]{0:T(512)S(1)} %concatenate.21, s32[384]{0:T(512)S(1)} %pad_add_fusion, s32[1536]{0:T(1024)S(1)} %add_select_fusion.2, bf16[192,512]{1,0:T(8,128)(2,1)S(1)} %bitcast.42, bf16[192,512]{1,0:T(8,128)(2,1)S(1)} %fusion.9), kind=kOutput, calls=%fused_computation.6 | convolution fusion | flops 607322112 | bytes 1975296 | tf_op jit(solution)/shard_map/dot_general | solution.py:22
  17.5 0.0 slice-start
  17.5 9.6 %all-to-all-start = ((bf16[32,48,512]{2,1,0:T(8,128)(2,1)}), bf16[32,48,512]{2,1,0:T(8,128)(2,1)S(1)}, u32[]{:S(2)}, u32[]{:S(2)}) async-start(bf16[32,48,512]{2,1,0:T(8,128)(2,1)} %bitcast.8), calls=%async_computation | async-start | bytes 3145728 | tf_op jit(solution)/shard_map/all_to_all | solution.py:335
  27.1 0.1 pad.8.clone
  27.2 2.3 %select_reduce_fusion = s32[32,512]{1,0:T(8,128)S(1)} fusion(s32[32,192]{1,0:T(8,128)S(1)} %get-tuple-element.66, s32[32,192]{1,0:T(8,128)S(1)} %get-tuple-element.67), kind=kLoop, calls=%fused_computation | loop fusion | flops 9420800 | bytes 114688 | tf_op jit(solution)/shard_map/reduce_sum | solution.py:362
  29.5 0.1 copy.42
  29.7 0.1 copy.55
  29.8 0.1 fusion.23
  29.9 0.1 stack.24
  29.9 0.1 stack.25
  30.1 0.1 select_bitcast_fusion
  30.1 0.1 copy.56
  30.2 0.1 concatenate.25.clone
  30.3 0.1 stack.26
  30.4 0.2 copy.43
  30.6 0.7 copy.44.target_ref
  31.3 0.0 slice-done
  31.3 0.7 copy.58
  32.0 0.6 pad_add_fusion.1.place_ref.parity_ref
  32.6 0.6 add_convert_fusion.target_ref
  33.3 16.8 %shard_map.68 = (bf16[32,192,128]{2,1,0:T(8,128)(2,1)}, bf16[32,192,128]{2,1,0:T(8,128)(2,1)}) custom-call(bf16[192,6144]{1,0:T(8,128)(2,1)} %bitcast.49, f32[2,32,192]{2,1,0:T(8,128)} %fusion.13.slot_ref, f32[32,512]{1,0:T(8,128)} %copy.44.target_ref), custom_call_target="tpu_custom_call" | custom-call | flops 3623878656 | bytes 6291456 | tf_op jit(solution)/shard_map/pallas_call | solution.py:388
  50.0 0.5 all-to-all-done
  50.5 1.1 copy-done
  51.6 4.5 %shard_map.69 = (f32[256,512]{1,0:T(8,128)}, bf16[272,512]{1,0:T(8,128)(2,1)}, bf16[256,512]{1,0:T(8,128)(2,1)}) custom-call(s32[2]{0:T(128)} %pad_add_fusion.1.place_ref.parity_ref, bf16[1536,512]{1,0:T(8,128)(2,1)} %bitcast.37, f32[3,1536]{1,0:T(4,128)} %add_convert_fusion.target_ref, f32[256,256]{1,0:T(8,128)} %bitcast.41), custom_call_target="tpu_custom_call" | custom-call | flops 1610612736 | bytes 2129920 | tf_op jit(solution)/shard_map/pallas_call | solution.py:417
  56.1 7.1 %all-to-all-start.1 = ((bf16[32,192,128]{2,1,0:T(8,128)(2,1)}), bf16[32,192,128]{2,1,0:T(8,128)(2,1)S(1)}, u32[]{:S(2)}, u32[]{:S(2)}) async-start(bf16[32,192,128]{2,1,0:T(8,128)(2,1)} %get-tuple-element.38), calls=%async_computation.1 | async-start | bytes 3145728 | tf_op jit(solution)/shard_map/all_to_all | solution.py:335
  63.2 0.0 all-gather.6.cloned.1.call-start
  63.3 0.0 copy-done.6
  63.3 1.4 collective-permute-start
  64.6 0.1 select_convert_fusion
  64.7 0.2 copy.49
  64.9 0.7 copy.50.target_ref
  65.6 5.8 %collective-permute-done.theirs_ref = bf16[272,512]{1,0:T(8,128)(2,1)S(1)} collective-permute-done((bf16[272,512]{1,0:T(8,128)(2,1)S(1)}, bf16[272,512]{1,0:T(8,128)(2,1)S(1)}, u32[]{:S(2)}, u32[]{:S(2)}) %collective-permute-start) | collective-permute-done | bytes 278560 | tf_op jit(solution)/shard_map/ppermute | solution.py:331
  71.5 0.7 copy-done.4
  72.2 2.2 %shard_map.70 = (f32[256,512]{1,0:T(8,128)}, bf16[208,512]{1,0:T(8,128)(2,1)}) custom-call(s32[2]{0:T(128)} %pad_add_fusion.1.place_ref.parity_ref, f32[256,512]{1,0:T(8,128)} %get-tuple-element.32.mine_ref, bf16[272,512]{1,0:T(8,128)(2,1)} %copy-done.4), custom_call_target="tpu_custom_call" | custom-call | bytes 1474560 | tf_op jit(solution)/shard_map/pallas_call | solution.py:430
  74.4 0.0 all-gather.6.cloned.1.call-update
  74.4 13.7 %all-gather.4.cloned.1.call-done.panel_ref = bf16[32,192,512]{2,1,0:T(8,128)(2,1)} async-done(((bf16[1,192,512]{2,1,0:T(8,128)(2,1)}), bf16[32,192,512]{2,1,0:T(8,128)(2,1)}) %all-gather.4.cloned.1.call-update) | async-done | bytes 6291472 | tf_op jit(solution)/shard_map/all_gather | solution.py:352
  88.0 7.6 %shard_map.71 = (f32[32,192,128]{2,1,0:T(8,128)}, f32[32,192,128]{2,1,0:T(8,128)}) custom-call(bf16[32,192,512]{2,1,0:T(8,128)(2,1)} %all-gather.4.cloned.1.call-done.panel_ref, bf16[256,512]{1,0:T(8,128)(2,1)} %get-tuple-element.40.q_ref), custom_call_target="tpu_custom_call" | custom-call | flops 3221225472 | bytes 12582912 | tf_op jit(solution)/shard_map/pallas_call | solution.py:442
  95.6 0.0 all-to-all-done.1.recv_ref
  95.6 8.2 %all-to-all-start.2 = ((bf16[32,192,128]{2,1,0:T(8,128)(2,1)}), bf16[32,192,128]{2,1,0:T(8,128)(2,1)S(1)}, u32[]{:S(2)}, u32[]{:S(2)}) async-start(bf16[32,192,128]{2,1,0:T(8,128)(2,1)} %get-tuple-element.45), calls=%async_computation.2 | async-start | bytes 3145728 | tf_op jit(solution)/shard_map/all_to_all | solution.py:335
  103.8 0.0 copy-done.1
  103.8 8.6 %shard_map.72 = (bf16[32,128,128]{2,1,0:T(8,128)(2,1)}, bf16[32,128,128]{2,1,0:T(8,128)(2,1)}) custom-call(bf16[32,192,128]{2,1,0:T(8,128)(2,1)} %copy-done.1, f32[32,192,128]{2,1,0:T(8,128)} %get-tuple-element.43.product_ref, f32[2,32,192]{2,1,0:T(8,128)} %fusion.13.slot_ref, f32[32,512]{1,0:T(8,128)} %copy.50.target_ref), custom_call_target="tpu_custom_call" | custom-call | flops 100663296000 | bytes 4194304 | tf_op jit(solution)/shard_map/pallas_call | solution.py:455
  112.4 0.8 collective-permute-start.1
  113.3 14.9 %all-to-all-done.2.recv_ref = bf16[32,192,128]{2,1,0:T(8,128)(2,1)S(1)} async-done(((bf16[32,192,128]{2,1,0:T(8,128)(2,1)}), bf16[32,192,128]{2,1,0:T(8,128)(2,1)S(1)}, u32[]{:S(2)}, u32[]{:S(2)}) %all-to-all-start.2) | async-done | bytes 1572896 | tf_op jit(solution)/shard_map/all_to_all | solution.py:335
  128.1 1.1 copy-done.2
  129.3 8.6 %shard_map.73 = (bf16[32,128,128]{2,1,0:T(8,128)(2,1)}, bf16[32,128,128]{2,1,0:T(8,128)(2,1)}) custom-call(bf16[32,192,128]{2,1,0:T(8,128)(2,1)} %copy-done.2, f32[32,192,128]{2,1,0:T(8,128)} %get-tuple-element.46.product_ref, f32[2,32,192]{2,1,0:T(8,128)} %fusion.13.slot_ref, f32[32,512]{1,0:T(8,128)} %copy.50.target_ref), custom_call_target="tpu_custom_call" | custom-call | flops 100663296000 | bytes 4194304 | tf_op jit(solution)/shard_map/pallas_call | solution.py:455
  137.9 1.6 collective-permute-start.2
  139.4 0.0 collective-permute-done.1.refs_2_
  139.4 15.4 %all-gather.6.cloned.1.call-done = bf16[6656,512]{1,0:T(8,128)(2,1)} async-done(((bf16[208,512]{1,0:T(8,128)(2,1)}), bf16[6656,512]{1,0:T(8,128)(2,1)}) %all-gather.6.cloned.1.call-update) | async-done | bytes 6815760 | tf_op jit(solution)/shard_map/all_gather | solution.py:438
  154.9 18.5 %shard_map.74 = (f32[8192,128]{1,0:T(8,128)}, f32[512,128]{1,0:T(8,128)}) custom-call(s32[2]{0:T(128)} %pad_add_fusion.1.place_ref.parity_ref, f32[256,512]{1,0:T(8,128)} %get-tuple-element.36.rows_ref, bf16[32,208,512]{2,1,0:T(8,128)(2,1)} %bitcast.48, f32[8192,128]{1,0:T(8,128)} %bitcast.40, bf16[32,128,128]{2,1,0:T(8,128)(2,1)} %get-tuple-element.44.refs_0_, ...), custom_call_target="tpu_custom_call" | custom-call | flops 8053063680 | bytes 8912896 | tf_op jit(solution)/shard_map/pallas_call | solution.py:475
  173.4 0.0 collective-permute-done.2.recv_ref
  173.4 0.0 copy-start.3
  173.4 1.0 copy-done.3
  174.4 5.6 %shard_map.75 = f32[8192,128]{1,0:T(8,128)} custom-call(f32[8192,128]{1,0:T(8,128)} %get-tuple-element.49.schur_ref, bf16[32,128,128]{2,1,0:T(8,128)(2,1)} %copy-done.3), custom_call_target="tpu_custom_call", output_to_operand_aliasing={{}: (0, {})} | custom-call | bytes 8388608 | tf_op jit(solution)/shard_map/pallas_call | solution.py:505
  (20 shorter events, 0.2 us)
Async XLA Ops:
  7.2 80.9 %all-gather.4.cloned.1.call-start = ((), (), s32[]{:S(2)}) async-start(), calls=%async_computation.3 | async-start | bytes 6488064 | tf_op jit(solution)/shard_map/all_gather | solution.py:352
  11.4 3.9 %copy-start.5 = (bf16[1,192,512]{2,1,0:T(8,128)(2,1)S(1)}, bf16[1,192,512]{2,1,0:T(8,128)(2,1)}, u32[]{:S(2)}) copy-start(bf16[1,192,512]{2,1,0:T(8,128)(2,1)} %param.7) | copy-start | bytes 589828
  17.5 13.8 %slice-start = ((f32[256,1,4096]{2,1,0:T(1,128)}), f32[256,1,256]{2,1,0:T(1,128)S(1)}, s32[]{:S(2)}) async-start(f32[256,1,4096]{2,1,0:T(1,128)} %param.5), calls=%async_computation.5 | async-start | bytes 524288 | tf_op jit(solution)/shard_map/slice | solution.py:426
  17.5 33.0 %all-to-all-start = ((bf16[32,48,512]{2,1,0:T(8,128)(2,1)}), bf16[32,48,512]{2,1,0:T(8,128)(2,1)S(1)}, u32[]{:S(2)}, u32[]{:S(2)}) async-start(bf16[32,48,512]{2,1,0:T(8,128)(2,1)} %bitcast.8), calls=%async_computation | async-start | bytes 3145728 | tf_op jit(solution)/shard_map/all_to_all | solution.py:335
  50.5 1.1 copy-start
  56.1 7.1 %copy-start.6 = (bf16[272,512]{1,0:T(8,128)(2,1)S(1)}, bf16[272,512]{1,0:T(8,128)(2,1)}, u32[]{:S(2)}) copy-start(bf16[272,512]{1,0:T(8,128)(2,1)} %get-tuple-element.35) | copy-start | bytes 835588
  56.1 39.5 %all-to-all-start.1 = ((bf16[32,192,128]{2,1,0:T(8,128)(2,1)}), bf16[32,192,128]{2,1,0:T(8,128)(2,1)S(1)}, u32[]{:S(2)}, u32[]{:S(2)}) async-start(bf16[32,192,128]{2,1,0:T(8,128)(2,1)} %get-tuple-element.38), calls=%async_computation.1 | async-start | bytes 3145728 | tf_op jit(solution)/shard_map/all_to_all | solution.py:335
  63.2 91.6 %all-gather.6.cloned.1.call-start = ((), (), s32[]{:S(2)}) async-start(), calls=%async_computation.4 | async-start | bytes 7028736 | tf_op jit(solution)/shard_map/all_gather | solution.py:438
  63.3 8.2 %collective-permute-start = (bf16[272,512]{1,0:T(8,128)(2,1)S(1)}, bf16[272,512]{1,0:T(8,128)(2,1)S(1)}, u32[]{:S(2)}, u32[]{:S(2)}) collective-permute-start(bf16[272,512]{1,0:T(8,128)(2,1)S(1)} %copy-done.6), channel_id=1, source_target_pairs={{0,32},{32,0},{64,96},{96,64},{1,33},{33,1},{65,97},{97,65},{2,34}... | collective-permute-start | bytes 835592 | tf_op jit(solution)/shard_map/ppermute | solution.py:331
  71.5 0.7 copy-start.4
  95.6 8.2 %copy-start.1 = (bf16[32,192,128]{2,1,0:T(8,128)(2,1)}, bf16[32,192,128]{2,1,0:T(8,128)(2,1)S(1)}, u32[]{:S(2)}) copy-start(bf16[32,192,128]{2,1,0:T(8,128)(2,1)S(1)} %all-to-all-done.1.recv_ref) | copy-start | bytes 4718596
  95.6 32.5 %all-to-all-start.2 = ((bf16[32,192,128]{2,1,0:T(8,128)(2,1)}), bf16[32,192,128]{2,1,0:T(8,128)(2,1)S(1)}, u32[]{:S(2)}, u32[]{:S(2)}) async-start(bf16[32,192,128]{2,1,0:T(8,128)(2,1)} %get-tuple-element.45), calls=%async_computation.2 | async-start | bytes 3145728 | tf_op jit(solution)/shard_map/all_to_all | solution.py:335
  112.4 27.0 %collective-permute-start.1 = (bf16[32,128,128]{2,1,0:T(8,128)(2,1)}, bf16[32,128,128]{2,1,0:T(8,128)(2,1)}, u32[]{:S(2)}, u32[]{:S(2)}) collective-permute-start(bf16[32,128,128]{2,1,0:T(8,128)(2,1)} %get-tuple-element.48), channel_id=1, source_target_pairs={{0,32},{32,0},{64,96},{96,64},{1,33},{33,1},{65,97},{97,65},{2,34}... | collective-permute-start | bytes 3145736 | tf_op jit(solution)/shard_map/ppermute | solution.py:331
  128.1 1.1 copy-start.2
  137.9 35.5 %collective-permute-start.2 = (bf16[32,128,128]{2,1,0:T(8,128)(2,1)}, bf16[32,128,128]{2,1,0:T(8,128)(2,1)S(1)}, u32[]{:S(2)}, u32[]{:S(2)}) collective-permute-start(bf16[32,128,128]{2,1,0:T(8,128)(2,1)} %get-tuple-element.50), channel_id=1, source_target_pairs={{0,32},{32,0},{64,96},{96,64},{1,33},{33,1},{65,97},{97,65},{2,34}... | collective-permute-start | bytes 3145736 | tf_op jit(solution)/shard_map/ppermute | solution.py:331
  173.4 1.0 copy-start.3
Sparse Core Ops, SparseCore 0:
  10.2 77.7 all-gather.3
  90.9 63.9 all-gather.5

commit v10 on v8

--- a/solution.py
+++ b/solution.py
@@ -9,7 +9,7 @@
 
 PW = 512
 CHUNKS = 2
-LOW_ROWS = 16
+LOW_ROWS = 8
 SOURCE_UNROLL = 4
 BF = jnp.bfloat16
 F32 = jnp.float32

time: 184 us -> 184 us (level)
  no operation moved by 1% of the time
where the time goes in v10:
time: 184 us; the launch traced here: 180 us
  Pallas kernels  72.1 us (39%)
  waiting for transfers between devices  43.1 us (23%)
  starting transfers between devices  28.5 us (15%)
  between operations  14.3 us (8%)
  local copies, waits for them, and re-layouts  8.38 us (5%)
  other arithmetic  7.89 us (4%)
  matrix products  6.09 us (3%)
    all_to_all x3, waiting for transfers between devices, exchanged(): return lax.all_to_all(block, 'grid', 0, 0, tiled=True)  33 us
    all_to_all x3, starting transfers between devices, exchanged(): return lax.all_to_all(block, 'grid', 0, 0, tiled=True)  24.2 us
    pallas_call x1, Pallas kernels, shards(): call(factor_kernel, [jax.ShapeDtypeStruct((owned * strips, 128), F32), ja...  18.5 us
    pallas_call x2, Pallas kernels, shards(): call(functools.partial(owner_kernel, owners, slots, owned), [jax.ShapeDty...  17.3 us
    pallas_call x1, Pallas kernels, shards(): call(functools.partial(source_kernel, owners, slots, owned), [jax.ShapeDt...  16.7 us
    ppermute x3, waiting for transfers between devices, swapped(): return lax.ppermute(block, 'cube', [(i, i ^ 1) for i in range(count)])  8.3 us
    pallas_call x1, Pallas kernels, shards(): call(product_kernel, [jax.ShapeDtypeStruct((owners, width, lanes), F32)]...  7.52 us
    dot_general x2, matrix products, dot(): lax.dot_general(a, b, dims, precision=precision, preferred_element_type=F32)  6.09 us
  transfers between devices with their start and end apart: 8, of which 6 were waited for; matrix products, arithmetic and copies ran while one was open for 10% of the time, Pallas kernels for 37%

profile of v10, /device:TPU:1, one launch (start us, length us, event | category | flops | bytes accessed | tf_op | source)
XLA Modules:
  0.0 180.3 jit_solution(16804226833044686624)
XLA Ops:
  7.2 0.0 all-gather.4.cloned.1.call-start
  7.2 0.7 all-gather.4.cloned.1.call-update
  7.9 1.0 compare_select_fusion
  8.9 0.1 reshape.251
  9.1 1.4 convert_reduce_fusion
  10.5 0.1 concatenate.21
  10.6 0.1 pad_add_fusion
  10.7 0.7 fusion.13.slot_ref
  11.4 0.0 copy-start.5
  11.4 3.9 %fusion.9 = bf16[192,512]{1,0:T(8,128)(2,1)S(1)} fusion(s32[6144]{0:T(1024)S(1)} %bitcast.44, bf16[1,192,6144]{2,1,0:T(8,128)(2,1)} %param.6), kind=kOutput, calls=%fused_computation.14 | convolution fusion | flops 1211203584 | bytes 2580480 | tf_op jit(solution)/shard_map/dot_general | solution.py:22
  15.3 0.0 copy-done.5
  15.3 2.2 %convolution_convert_fusion = bf16[1536,512]{1,0:T(8,128)(2,1)} fusion(s32[384]{0:T(512)S(1)} %concatenate.21, s32[384]{0:T(512)S(1)} %pad_add_fusion, s32[1536]{0:T(1024)S(1)} %add_select_fusion.2, bf16[192,512]{1,0:T(8,128)(2,1)S(1)} %bitcast.42, bf16[192,512]{1,0:T(8,128)(2,1)S(1)} %fusion.9), kind=kOutput, calls=%fused_computation.6 | convolution fusion | flops 607322112 | bytes 1975296 | tf_op jit(solution)/shard_map/dot_general | solution.py:22
  17.5 0.0 slice-start
  17.5 9.6 %all-to-all-start = ((bf16[32,48,512]{2,1,0:T(8,128)(2,1)}), bf16[32,48,512]{2,1,0:T(8,128)(2,1)S(1)}, u32[]{:S(2)}, u32[]{:S(2)}) async-start(bf16[32,48,512]{2,1,0:T(8,128)(2,1)} %bitcast.8), calls=%async_computation | async-start | bytes 3145728 | tf_op jit(solution)/shard_map/all_to_all | solution.py:335
  27.1 0.0 all-gather.6.cloned.1.call-start
  27.2 0.1 pad.8.clone
  27.3 2.3 %select_reduce_fusion = s32[32,512]{1,0:T(8,128)S(1)} fusion(s32[32,192]{1,0:T(8,128)S(1)} %get-tuple-element.62, s32[32,192]{1,0:T(8,128)S(1)} %get-tuple-element.63), kind=kLoop, calls=%fused_computation | loop fusion | flops 9420800 | bytes 114688 | tf_op jit(solution)/shard_map/reduce_sum | solution.py:362
  29.6 0.1 copy.42
  29.8 0.1 copy.55
  29.8 0.1 fusion.23
  29.9 0.1 stack.24
  30.0 0.1 stack.25
  30.1 0.1 select_bitcast_fusion
  30.2 0.1 copy.56
  30.3 0.1 concatenate.25.clone
  30.4 0.1 stack.26
  30.5 0.2 copy.43
  30.7 0.7 copy.44.target_ref
  31.4 0.0 slice-done
  31.4 0.7 copy.58
  32.1 0.7 pad_add_fusion.1.place_ref.parity_ref
  32.8 0.6 add_convert_fusion.target_ref
  33.4 16.7 %shard_map.68 = (bf16[32,192,128]{2,1,0:T(8,128)(2,1)}, bf16[32,192,128]{2,1,0:T(8,128)(2,1)}) custom-call(bf16[192,6144]{1,0:T(8,128)(2,1)} %bitcast.49, f32[2,32,192]{2,1,0:T(8,128)} %fusion.13.slot_ref, f32[32,512]{1,0:T(8,128)} %copy.44.target_ref), custom_call_target="tpu_custom_call" | custom-call | flops 3623878656 | bytes 6291456 | tf_op jit(solution)/shard_map/pallas_call | solution.py:388
  50.1 0.4 all-to-all-done
  50.6 0.0 copy-start
  50.6 1.1 copy-done
  51.7 4.5 %shard_map.69 = (f32[256,512]{1,0:T(8,128)}, bf16[264,512]{1,0:T(8,128)(2,1)}, bf16[256,512]{1,0:T(8,128)(2,1)}) custom-call(s32[2]{0:T(128)} %pad_add_fusion.1.place_ref.parity_ref, bf16[1536,512]{1,0:T(8,128)(2,1)} %bitcast.37, f32[3,1536]{1,0:T(4,128)} %add_convert_fusion.target_ref, f32[256,256]{1,0:T(8,128)} %bitcast.41), custom_call_target="tpu_custom_call" | custom-call | flops 1610612736 | bytes 2113536 | tf_op jit(solution)/shard_map/pallas_call | solution.py:417
  56.2 1.5 collective-permute-start
  57.7 5.1 %collective-permute-done.theirs_ref = bf16[264,512]{1,0:T(8,128)(2,1)S(1)} collective-permute-done((bf16[264,512]{1,0:T(8,128)(2,1)}, bf16[264,512]{1,0:T(8,128)(2,1)S(1)}, u32[]{:S(2)}, u32[]{:S(2)}) %collective-permute-start) | collective-permute-done | bytes 270368 | tf_op jit(solution)/shard_map/ppermute | solution.py:331
  62.8 0.0 copy-start.4
  62.8 0.7 copy-done.4
  63.5 2.3 %shard_map.70 = (f32[256,512]{1,0:T(8,128)}, bf16[200,512]{1,0:T(8,128)(2,1)}) custom-call(s32[2]{0:T(128)} %pad_add_fusion.1.place_ref.parity_ref, f32[256,512]{1,0:T(8,128)} %get-tuple-element.30.mine_ref, bf16[264,512]{1,0:T(8,128)(2,1)} %copy-done.4), custom_call_target="tpu_custom_call" | custom-call | bytes 1458176 | tf_op jit(solution)/shard_map/pallas_call | solution.py:429
  65.8 0.0 all-gather.6.cloned.1.call-update
  65.8 9.0 %all-to-all-start.1 = ((bf16[32,192,128]{2,1,0:T(8,128)(2,1)}), bf16[32,192,128]{2,1,0:T(8,128)(2,1)S(1)}, u32[]{:S(2)}, u32[]{:S(2)}) async-start(bf16[32,192,128]{2,1,0:T(8,128)(2,1)} %get-tuple-element.34), calls=%async_computation.1 | async-start | bytes 3145728 | tf_op jit(solution)/shard_map/all_to_all | solution.py:335
  74.8 1.1 all-gather.4.cloned.1.call-done.panel_ref
  75.9 7.5 %shard_map.71 = (f32[32,192,128]{2,1,0:T(8,128)}, f32[32,192,128]{2,1,0:T(8,128)}) custom-call(bf16[32,192,512]{2,1,0:T(8,128)(2,1)} %all-gather.4.cloned.1.call-done.panel_ref, bf16[256,512]{1,0:T(8,128)(2,1)} %get-tuple-element.36.q_ref), custom_call_target="tpu_custom_call" | custom-call | flops 3221225472 | bytes 12582912 | tf_op jit(solution)/shard_map/pallas_call | solution.py:441
  83.4 14.7 %all-to-all-done.1.recv_ref = bf16[32,192,128]{2,1,0:T(8,128)(2,1)S(1)} async-done(((bf16[32,192,128]{2,1,0:T(8,128)(2,1)}), bf16[32,192,128]{2,1,0:T(8,128)(2,1)S(1)}, u32[]{:S(2)}, u32[]{:S(2)}) %all-to-all-start.1) | async-done | bytes 1572896 | tf_op jit(solution)/shard_map/all_to_all | solution.py:335
  98.2 0.0 copy-start.1
  98.2 5.6 %all-to-all-start.2 = ((bf16[32,192,128]{2,1,0:T(8,128)(2,1)}), bf16[32,192,128]{2,1,0:T(8,128)(2,1)S(1)}, u32[]{:S(2)}, u32[]{:S(2)}) async-start(bf16[32,192,128]{2,1,0:T(8,128)(2,1)} %get-tuple-element.41), calls=%async_computation.2 | async-start | bytes 3145728 | tf_op jit(solution)/shard_map/all_to_all | solution.py:335
  103.8 0.8 select_convert_fusion
  104.6 1.1 copy.49
  105.7 0.7 copy.50.target_ref
  106.5 0.0 copy-done.1
  106.5 8.6 %shard_map.72 = (bf16[32,128,128]{2,1,0:T(8,128)(2,1)}, bf16[32,128,128]{2,1,0:T(8,128)(2,1)}) custom-call(bf16[32,192,128]{2,1,0:T(8,128)(2,1)} %copy-done.1, f32[32,192,128]{2,1,0:T(8,128)} %get-tuple-element.39.product_ref, f32[2,32,192]{2,1,0:T(8,128)} %fusion.13.slot_ref, f32[32,512]{1,0:T(8,128)} %copy.50.target_ref), custom_call_target="tpu_custom_call" | custom-call | flops 3221225472 | bytes 4194304 | tf_op jit(solution)/shard_map/pallas_call | solution.py:454
  115.1 1.3 collective-permute-start.1
  116.4 17.8 %all-to-all-done.2.recv_ref = bf16[32,192,128]{2,1,0:T(8,128)(2,1)S(1)} async-done(((bf16[32,192,128]{2,1,0:T(8,128)(2,1)}), bf16[32,192,128]{2,1,0:T(8,128)(2,1)S(1)}, u32[]{:S(2)}, u32[]{:S(2)}) %all-to-all-start.2) | async-done | bytes 1572896 | tf_op jit(solution)/shard_map/all_to_all | solution.py:335
  134.2 1.1 copy-done.2
  135.4 8.6 %shard_map.73 = (bf16[32,128,128]{2,1,0:T(8,128)(2,1)}, bf16[32,128,128]{2,1,0:T(8,128)(2,1)}) custom-call(bf16[32,192,128]{2,1,0:T(8,128)(2,1)} %copy-done.2, f32[32,192,128]{2,1,0:T(8,128)} %get-tuple-element.42.product_ref, f32[2,32,192]{2,1,0:T(8,128)} %fusion.13.slot_ref, f32[32,512]{1,0:T(8,128)} %copy.50.target_ref), custom_call_target="tpu_custom_call" | custom-call | flops 3221225472 | bytes 4194304 | tf_op jit(solution)/shard_map/pallas_call | solution.py:454
  144.0 1.4 collective-permute-start.2
  145.4 0.0 collective-permute-done.1.refs_2_
  145.4 18.5 %shard_map.74 = (f32[8192,128]{1,0:T(8,128)}, f32[512,128]{1,0:T(8,128)}) custom-call(s32[2]{0:T(128)} %pad_add_fusion.1.place_ref.parity_ref, f32[256,512]{1,0:T(8,128)} %get-tuple-element.32.rows_ref, bf16[32,200,512]{2,1,0:T(8,128)(2,1)} %bitcast.48, f32[8192,128]{1,0:T(8,128)} %bitcast.40, bf16[32,128,128]{2,1,0:T(8,128)(2,1)} %get-tuple-element.40.refs_0_, ...), custom_call_target="tpu_custom_call" | custom-call | flops 8053063680 | bytes 8912896 | tf_op jit(solution)/shard_map/pallas_call | solution.py:474
  164.0 3.2 %collective-permute-done.2.recv_ref = bf16[32,128,128]{2,1,0:T(8,128)(2,1)S(1)} collective-permute-done((bf16[32,128,128]{2,1,0:T(8,128)(2,1)}, bf16[32,128,128]{2,1,0:T(8,128)(2,1)S(1)}, u32[]{:S(2)}, u32[]{:S(2)}) %collective-permute-start.2) | collective-permute-done | bytes 1048608 | tf_op jit(solution)/shard_map/ppermute | solution.py:331
  167.1 1.0 copy-done.3
  168.1 5.3 %shard_map.75 = f32[8192,128]{1,0:T(8,128)} custom-call(f32[8192,128]{1,0:T(8,128)} %get-tuple-element.45.schur_ref, bf16[32,128,128]{2,1,0:T(8,128)(2,1)} %copy-done.3), custom_call_target="tpu_custom_call", output_to_operand_aliasing={{}: (0, {})} | custom-call | bytes 8388608 | tf_op jit(solution)/shard_map/pallas_call | solution.py:504
  (18 shorter events, 0.2 us)
Async XLA Ops:
  7.2 68.7 %all-gather.4.cloned.1.call-start = ((), (), s32[]{:S(2)}) async-start(), calls=%async_computation.3 | async-start | bytes 6488064 | tf_op jit(solution)/shard_map/all_gather | solution.py:352
  11.4 3.9 %copy-start.5 = (bf16[1,192,512]{2,1,0:T(8,128)(2,1)S(1)}, bf16[1,192,512]{2,1,0:T(8,128)(2,1)}, u32[]{:S(2)}) copy-start(bf16[1,192,512]{2,1,0:T(8,128)(2,1)} %param.7) | copy-start | bytes 589828
  17.5 13.9 %slice-start = ((f32[256,1,4096]{2,1,0:T(1,128)}), f32[256,1,256]{2,1,0:T(1,128)S(1)}, s32[]{:S(2)}) async-start(f32[256,1,4096]{2,1,0:T(1,128)} %param.5), calls=%async_computation.5 | async-start | bytes 524288 | tf_op jit(solution)/shard_map/slice | solution.py:426
  17.5 33.0 %all-to-all-start = ((bf16[32,48,512]{2,1,0:T(8,128)(2,1)}), bf16[32,48,512]{2,1,0:T(8,128)(2,1)S(1)}, u32[]{:S(2)}, u32[]{:S(2)}) async-start(bf16[32,48,512]{2,1,0:T(8,128)(2,1)} %bitcast.8), calls=%async_computation | async-start | bytes 3145728 | tf_op jit(solution)/shard_map/all_to_all | solution.py:335
  27.1 118.3 %all-gather.6.cloned.1.call-start = ((), (), s32[]{:S(2)}) async-start(), calls=%async_computation.4 | async-start | bytes 6758400 | tf_op jit(solution)/shard_map/all_gather | solution.py:437
  50.6 1.1 copy-start
  56.2 6.6 %collective-permute-start = (bf16[264,512]{1,0:T(8,128)(2,1)}, bf16[264,512]{1,0:T(8,128)(2,1)S(1)}, u32[]{:S(2)}, u32[]{:S(2)}) collective-permute-start(bf16[264,512]{1,0:T(8,128)(2,1)} %get-tuple-element.31), channel_id=1, source_target_pairs={{0,32},{32,0},{64,96},{96,64},{1,33},{33,1},{65,97},{97,65},{2,34}... | collective-permute-start | bytes 811016 | tf_op jit(solution)/shard_map/ppermute | solution.py:331
  62.8 0.7 copy-start.4
  65.8 32.4 %all-to-all-start.1 = ((bf16[32,192,128]{2,1,0:T(8,128)(2,1)}), bf16[32,192,128]{2,1,0:T(8,128)(2,1)S(1)}, u32[]{:S(2)}, u32[]{:S(2)}) async-start(bf16[32,192,128]{2,1,0:T(8,128)(2,1)} %get-tuple-element.34), calls=%async_computation.1 | async-start | bytes 3145728 | tf_op jit(solution)/shard_map/all_to_all | solution.py:335
  98.2 8.3 %copy-start.1 = (bf16[32,192,128]{2,1,0:T(8,128)(2,1)}, bf16[32,192,128]{2,1,0:T(8,128)(2,1)S(1)}, u32[]{:S(2)}) copy-start(bf16[32,192,128]{2,1,0:T(8,128)(2,1)S(1)} %all-to-all-done.1.recv_ref) | copy-start | bytes 4718596
  98.2 36.1 %all-to-all-start.2 = ((bf16[32,192,128]{2,1,0:T(8,128)(2,1)}), bf16[32,192,128]{2,1,0:T(8,128)(2,1)S(1)}, u32[]{:S(2)}, u32[]{:S(2)}) async-start(bf16[32,192,128]{2,1,0:T(8,128)(2,1)} %get-tuple-element.41), calls=%async_computation.2 | async-start | bytes 3145728 | tf_op jit(solution)/shard_map/all_to_all | solution.py:335
  115.1 30.3 %collective-permute-start.1 = (bf16[32,128,128]{2,1,0:T(8,128)(2,1)}, bf16[32,128,128]{2,1,0:T(8,128)(2,1)}, u32[]{:S(2)}, u32[]{:S(2)}) collective-permute-start(bf16[32,128,128]{2,1,0:T(8,128)(2,1)} %get-tuple-element.44), channel_id=1, source_target_pairs={{0,32},{32,0},{64,96},{96,64},{1,33},{33,1},{65,97},{97,65},{2,34}... | collective-permute-start | bytes 3145736 | tf_op jit(solution)/shard_map/ppermute | solution.py:331
  134.2 1.1 copy-start.2
  144.0 23.1 %collective-permute-start.2 = (bf16[32,128,128]{2,1,0:T(8,128)(2,1)}, bf16[32,128,128]{2,1,0:T(8,128)(2,1)S(1)}, u32[]{:S(2)}, u32[]{:S(2)}) collective-permute-start(bf16[32,128,128]{2,1,0:T(8,128)(2,1)} %get-tuple-element.46), channel_id=1, source_target_pairs={{0,32},{32,0},{64,96},{96,64},{1,33},{33,1},{65,97},{97,65},{2,34}... | collective-permute-start | bytes 3145736 | tf_op jit(solution)/shard_map/ppermute | solution.py:331
  167.1 1.0 copy-start.3
Sparse Core Ops, SparseCore 0:
  10.2 65.6 all-gather.3
  78.1 61.5 all-gather.5
